TPU v7x, 32 devices: a whole 2x2x4 slice. The times are simulated.
32 devices in a mesh: region: 4 (over y, core), sub: 8 (over z, x).
Axes of the slice: x: 2, y: 2, z: 4, core: 2. Of those that a mesh axis runs over, the one named last changes fastest.
Arguments:
- coords: float32 [3, 2048, 128], P(None, ('region', 'sub')), may hold values from -3 to 3
- smooth: float32 [2048, 128], P(('region', 'sub')), may hold values from 0.6 to 1.5
- masses: float32 [2048, 128], P(('region', 'sub')), may hold values from 0.01 to 0.1
- owners: int32 [2048], P(('region', 'sub')), may hold values from 0 to 3, as said below
- counts: int32 [2048], P(('region', 'sub')), may hold values from 32 to 128
- neighbours: int32 [2048, 4], P(('region', 'sub')), may hold values from 0 to 71, as said below
Outputs:
- density: float32 [2048, 128], P(('region', 'sub'))
- accel: float32 [3, 2048, 128], P(None, ('region', 'sub'))
Inputs may be any that keep to these rules, and one draw needn't show every extreme that they name: `owners`: within the 64 tiles of each device's block, every value 0 to 4 - 1 appears exactly 16 times. `neighbours`: the first entry of the list of slot t is 4 + t (the tile itself); the entries of one list are distinct and lie within 4 of 4 + t.
All inputs are finite; a program needn't handle non-finite values.
Results may differ from a plain program's by a relative error of at most 0.0001.
Values sent between devices are 32-bit elements; how exact they have to be, the bound alone decides.
No kernel may reach another device: no remote copies, remote signals or barrier semaphores. Data moves between devices by JAX's collectives and lax.ppermute only.
A program may use at most 64 MiB of HBM per device.

v0:
```python
import functools
import math

import jax
import jax.numpy as jnp
from jax import lax
from jax.experimental import pallas as pl
from jax.experimental.pallas import tpu as pltpu
from jax.sharding import PartitionSpec as P


HALO_TILES = 4
RIM = 2 * HALO_TILES
FIELDS = 5
UNROLL = 7
EMPTY_LOG = -1024.0
LOG2E = 1.4426950408889634
kernel_scale = math.pi ** (-1.5)

f32, bf16 = jnp.float32, jnp.bfloat16
VMEM = pl.BlockSpec(memory_space=pltpu.VMEM)
SMEM = pl.BlockSpec(memory_space=pltpu.SMEM)


def group_kernel(per_dest, owners_ref, coords_ref, smooth_ref, masses_ref, out_ref):
    regions = out_ref.shape[0]
    bits = per_dest.bit_length()
    per_word = 31 // bits
    seen = [jnp.int32(0)] * pl.cdiv(regions, per_word)
    for n in range(owners_ref.shape[0]):
        d = owners_ref[n]
        word = d // per_word if len(seen) > 1 else 0
        shift = (d - word * per_word) * bits
        k = seen[0]
        for w in range(1, len(seen)):
            k = jnp.where(word == w, seen[w], k)
        k = (k >> shift) & ((1 << bits) - 1)
        step = jnp.int32(1) << shift
        seen = [s + (jnp.where(word == w, step, 0) if len(seen) > 1 else step) for w, s in enumerate(seen)]
        for c in range(3):
            out_ref[d, pl.ds(c * per_dest + k, 1)] = coords_ref[c, n:n + 1]
        out_ref[d, pl.ds(3 * per_dest + k, 1)] = smooth_ref[n:n + 1]
        out_ref[d, pl.ds(4 * per_dest + k, 1)] = masses_ref[n:n + 1]


def group_tiles(coords, smooth, masses, owners, regions):
    tile_dev, rows = smooth.shape
    per_dest = tile_dev // regions
    return pl.pallas_call(
        functools.partial(group_kernel, per_dest),
        out_shape=jax.ShapeDtypeStruct((regions, FIELDS * per_dest, rows), f32),
        in_specs=[SMEM, VMEM, VMEM, VMEM],
        out_specs=VMEM,
        name="group_tiles",
    )(owners, coords, smooth, masses)


def parts_of(x, count):
    parts = []
    for _ in range(count):
        part = x.astype(bf16).astype(f32)
        parts.append(part)
        x = x - part
    return parts


def dot(a, b):
    return jnp.dot(a, b, preferred_element_type=f32)


def own_field(own_ref, live_ref, f):
    tile_dev = live_ref.shape[0]
    regions, per_dest = own_ref.shape[0], tile_dev // own_ref.shape[0]
    value = jnp.concatenate([own_ref[r, f * per_dest:(f + 1) * per_dest] for r in range(regions)], axis=0)
    return value * live_ref[...] if f == 4 else value


def field_terms(fields):
    pos, h, mass = fields[:3], fields[3], fields[4]
    inverse_sq = 1.0 / (h * h)
    return pos, mass > 0, mass, inverse_sq, kernel_scale * inverse_sq / h


def put_rows(ref, values):
    count = values[0].shape[0]
    for k, value in enumerate(values):
        ref[k * count:(k + 1) * count] = value


def put_features(pos, live, mass, inverse_sq, partner_ref, mine_ref):
    c = inverse_sq * LOG2E
    square = pos[0] * pos[0] + pos[1] * pos[1] + pos[2] * pos[2]
    log_mass = jnp.where(live, jnp.log2(jnp.where(live, mass, 1.0)), EMPTY_LOG)
    one, zero = jnp.ones_like(c), jnp.zeros_like(c)
    put_rows(partner_ref, pos + [square, log_mass, one, zero, zero])
    put_rows(mine_ref, [2 * c * x for x in pos] + [-c, one, -c * square, zero, zero])


def tile_of(ref, e):
    return ref[pl.ds(e, 8, stride=ref.shape[0] // 8)]


def turned(ref, e):
    p1, p2, p3 = parts_of(tile_of(ref, e), 3)
    block = jnp.concatenate([p1, p1, p2, p1, p3, p2], axis=0).astype(bf16)
    fill = jnp.zeros((block.shape[1] - block.shape[0], block.shape[1]), bf16)
    return jnp.concatenate([block, fill], axis=0).T


def pair_weights(ref, e):
    def one_tile(e):
        o1, o2, o3 = parts_of(tile_of(ref, e), 3)
        block = jnp.concatenate([o1, o2, o1, o3, o1, o2], axis=0).astype(bf16)
        return jnp.concatenate([block, jnp.zeros((block.shape[1] - block.shape[0], block.shape[1]), bf16)], axis=0)

    first, second = one_tile(e), one_tile(e + 1)
    blank = jnp.zeros_like(first)
    return jnp.concatenate(
        [jnp.concatenate([first, blank], axis=1), jnp.concatenate([blank, second], axis=1)], axis=0
    )


def density_pair(turned_ref, own, partners, part_ref, at, store):
    rows = own.shape[1] // 2
    total = None
    for n, (e0, e1) in enumerate(partners):
        t = jnp.exp2(dot(jnp.concatenate([turned_ref[e0], turned_ref[e1]], axis=1), own))
        if store is not None:
            store[n * rows:(n + 1) * rows] = t
        part = jnp.sum(t.reshape(rows // 8, 8, 2 * rows), axis=0)
        total = part if total is None else total + part
    part_ref[pl.ds(at, 8)] = total[:, :rows]
    part_ref[pl.ds(at + 8, 8)] = total[:, rows:]


def inner_kernel(
    lists_ref, own_ref, live_ref, pair_ref, part_ref, edge_ref, partner_ref, mine_ref, turned_ref, weights_ref,
):
    tile_dev = live_ref.shape[0]
    listed = lists_ref.shape[1]
    pos, live, mass, inverse_sq, _ = field_terms([own_field(own_ref, live_ref, f) for f in range(FIELDS)])
    put_features(pos, live, mass, inverse_sq, partner_ref, mine_ref)

    @pl.loop(0, tile_dev, unroll=8)
    def _(t):
        turned_ref[t] = turned(partner_ref, t)

    edge_ref[:RIM] = turned_ref[:RIM]
    edge_ref[RIM:] = turned_ref[tile_dev - RIM:]
    count = pair_ref.shape[0]

    @pl.loop(0, count, unroll=UNROLL)
    def _(p):
        weights_ref[p] = pair_weights(mine_ref, HALO_TILES + 2 * p)

    @pl.loop(0, count, unroll=UNROLL)
    def _(p):
        t = HALO_TILES + 2 * p
        partners = [(lists_ref[t, n] - HALO_TILES, lists_ref[t + 1, n] - HALO_TILES) for n in range(listed)]
        density_pair(turned_ref, weights_ref[p], partners, part_ref, 16 * p, pair_ref.at[p])


def outer_kernel(
    lists_ref, rim_lists_ref, own_ref, live_ref, below_ref, above_ref, pair_ref, part_ref, edge_ref,
    density_ref, accel_ref, partner_ref, mine_ref, turned_ref, rim_pair_ref, rim_part_ref, coef_ref, coefb_ref, out_ref,
):
    tile_dev, rows = live_ref.shape
    ext = tile_dev + 2 * RIM
    listed = lists_ref.shape[1]
    fields = [
        jnp.concatenate(
            [below_ref[f * RIM:(f + 1) * RIM], own_field(own_ref, live_ref, f), above_ref[f * RIM:(f + 1) * RIM]], axis=0
        )
        for f in range(FIELDS)
    ]
    pos, live, mass, inverse_sq, norm = field_terms(fields)

    def rims(x):
        return jnp.concatenate([x[:2 * RIM], x[tile_dev:]], axis=0)

    put_features([rims(x) for x in pos], rims(live), rims(mass), rims(inverse_sq), partner_ref, mine_ref)
    for e in range(RIM):
        turned_ref[e] = turned(partner_ref, e)
        turned_ref[RIM + e] = edge_ref[e]
        turned_ref[2 * RIM + e] = edge_ref[RIM + e]
        turned_ref[3 * RIM + e] = turned(partner_ref, 3 * RIM + e)

    edge_pairs = HALO_TILES
    half = HALO_TILES // 2
    for side in range(2):
        for i in range(edge_pairs):
            e = 2 * RIM * side + HALO_TILES + 2 * i
            own_side = (i >= half) if side == 0 else (i < half)
            if own_side:
                t = e - RIM if side == 0 else e - 3 * RIM + tile_dev
                shift = HALO_TILES if side == 0 else HALO_TILES - tile_dev + 2 * RIM
                partners = [(lists_ref[t, n] + shift, lists_ref[t + 1, n] + shift) for n in range(listed)]
                store = rim_pair_ref.at[half * side + i % half]
            else:
                first = (2 * i if side == 0 else HALO_TILES + 2 * (i - half)) * listed
                shift = HALO_TILES - tile_dev if side == 0 else HALO_TILES + 2 * RIM
                partners = [
                    (rim_lists_ref[first + n] + shift, rim_lists_ref[first + listed + n] + shift) for n in range(listed)
                ]
                store = None
            at = 16 * (edge_pairs * side + i)
            density_pair(turned_ref, pair_weights(mine_ref, e), partners, rim_part_ref, at, store)

    inner_tiles = tile_dev - RIM
    raw = jnp.concatenate(
        [
            sum(rim_part_ref[pl.ds(k, RIM, stride=8)] for k in range(8)),
            sum(part_ref[pl.ds(k, inner_tiles, stride=8)] for k in range(8)),
            sum(rim_part_ref[pl.ds(8 * RIM + k, RIM, stride=8)] for k in range(8)),
        ],
        axis=0,
    )
    inner = slice(HALO_TILES, ext - HALO_TILES)
    raw = raw * norm[inner]
    q = jnp.where(live[inner], jnp.exp2(jnp.log2(jnp.where(live[inner], raw, 1.0)) * (-1.0 / 3.0)), 0.0)
    pad = jnp.zeros((HALO_TILES, rows), f32)
    q = jnp.concatenate([pad, q, pad], axis=0)
    put_rows(coef_ref, [jnp.ones_like(q)] + pos + [q] + [q * x for x in pos])

    @pl.loop(0, ext, unroll=8)
    def _(e):
        coefb_ref[e] = jnp.concatenate(parts_of(tile_of(coef_ref, e), 2), axis=0).astype(bf16)

    def force_pair(t, pair):
        total = None
        for n in range(listed):
            e0, e1 = lists_ref[t, n] + HALO_TILES, lists_ref[t + 1, n] + HALO_TILES
            left = jnp.concatenate([coefb_ref[e0], coefb_ref[e1]], axis=0)
            w = pair[n * rows:(n + 1) * rows]
            high = w.astype(bf16)
            part = dot(left, high) + dot(left, (w - high.astype(f32)).astype(bf16))
            total = part if total is None else total + part
        at = 8 * t
        out_ref[pl.ds(at, 8)] = total[:8, :rows] + total[8:16, :rows]
        out_ref[pl.ds(at + 8, 8)] = total[16:24, rows:] + total[24:, rows:]

    for i in range(half):
        force_pair(2 * i, rim_pair_ref.at[i])
        force_pair(tile_dev - HALO_TILES + 2 * i, rim_pair_ref.at[half + i])

    @pl.loop(0, pair_ref.shape[0], unroll=UNROLL)
    def _(p):
        force_pair(HALO_TILES + 2 * p, pair_ref.at[p])

    mine = slice(RIM, RIM + tile_dev)
    own_live = live_ref[...]
    density_ref[...] = raw[HALO_TILES:HALO_TILES + tile_dev] * own_live
    q_own = q[mine]
    scale = own_live * (2.0 * inverse_sq[mine] * norm[mine])
    sums = [out_ref[pl.ds(k, tile_dev, stride=8)] for k in range(8)]
    for c in range(3):
        x = pos[c][mine]
        accel_ref[c] = scale * (q_own * (x * sums[0] - sums[1 + c]) + (x * sums[4] - sums[5 + c]))


def inner_density(lists, own, live):
    tile_dev, rows = live.shape
    listed = lists.shape[1]
    count = (tile_dev - RIM) // 2
    return pl.pallas_call(
        inner_kernel,
        out_shape=(
            jax.ShapeDtypeStruct((count, listed * rows, 2 * rows), f32),
            jax.ShapeDtypeStruct((16 * count, rows), f32),
            jax.ShapeDtypeStruct((2 * RIM, rows, rows), bf16),
        ),
        in_specs=[SMEM, VMEM, VMEM],
        out_specs=(VMEM, VMEM, VMEM),
        scratch_shapes=[
            pltpu.VMEM((8 * tile_dev, rows), f32),
            pltpu.VMEM((8 * tile_dev, rows), f32),
            pltpu.VMEM((tile_dev, rows, rows), bf16),
            pltpu.VMEM((count, 2 * rows, 2 * rows), bf16),
        ],
        compiler_params=pltpu.CompilerParams(vmem_limit_bytes=24 << 20),
        cost_estimate=pl.CostEstimate(flops=10 ** 9, bytes_accessed=10 ** 7, transcendentals=0),
        name="inner_density",
    )(lists, own, live)


def outer_step(lists, rim_lists, own, live, below, above, pair, part, edge):
    tile_dev, rows = live.shape
    ext = tile_dev + 2 * RIM
    listed = lists.shape[1]
    return pl.pallas_call(
        outer_kernel,
        out_shape=(jax.ShapeDtypeStruct((tile_dev, rows), f32), jax.ShapeDtypeStruct((3, tile_dev, rows), f32)),
        in_specs=[SMEM, SMEM] + [VMEM] * 7,
        out_specs=(VMEM, VMEM),
        scratch_shapes=[
            pltpu.VMEM((8 * 4 * RIM, rows), f32),
            pltpu.VMEM((8 * 4 * RIM, rows), f32),
            pltpu.VMEM((4 * RIM, rows, rows), bf16),
            pltpu.VMEM((HALO_TILES, listed * rows, 2 * rows), f32),
            pltpu.VMEM((8 * 2 * RIM, rows), f32),
            pltpu.VMEM((8 * ext, rows), f32),
            pltpu.VMEM((ext, 16, rows), bf16),
            pltpu.VMEM((8 * tile_dev, rows), f32),
        ],
        compiler_params=pltpu.CompilerParams(vmem_limit_bytes=24 << 20),
        name="outer_step",
    )(lists, rim_lists, own, live, below, above, pair, part, edge)


def per_device(coords, smooth, masses, owners, counts, neighbours):
    tile_dev, rows = smooth.shape
    regions = lax.axis_size("region")
    subs = lax.axis_size("sub")
    per_dest = tile_dev // regions
    listed = neighbours.shape[1]
    grouped = group_tiles(coords, smooth, masses, owners, regions)
    own = lax.all_to_all(grouped, "region", 0, 0, tiled=True)
    live = (jnp.arange(rows, dtype=jnp.int32)[None, :] < counts[:, None]).astype(f32)
    by_field = own.reshape(regions, FIELDS, per_dest, rows)

    def rim(first):
        if per_dest >= RIM:
            block = by_field[regions - 1 if not first else 0]
            block = block[:, :RIM] if first else block[:, per_dest - RIM:]
        else:
            blocks = RIM // per_dest
            block = by_field[:blocks] if first else by_field[regions - blocks:]
            block = jnp.swapaxes(block, 0, 1).reshape(FIELDS, RIM, rows)
        tiles = slice(0, RIM) if first else slice(tile_dev - RIM, tile_dev)
        block = jnp.concatenate([block[:4], (block[4] * live[tiles])[None]], axis=0).reshape(FIELDS * RIM, rows)
        near = slice(0, HALO_TILES) if first else slice(tile_dev - HALO_TILES, tile_dev)
        ids = neighbours[near].astype(f32).reshape(1, HALO_TILES * listed)
        return jnp.concatenate([block, jnp.pad(ids, ((0, 7), (0, rows - HALO_TILES * listed)))], axis=0)

    up = [(i, (i + 1) % subs) for i in range(subs)]
    down = [(j, i) for i, j in up]
    below = lax.ppermute(rim(False), "sub", up)
    above = lax.ppermute(rim(True), "sub", down)
    pair, part, edge = inner_density(neighbours, own, live)
    count = HALO_TILES * listed
    rim_lists = jnp.concatenate([below[FIELDS * RIM, :count], above[FIELDS * RIM, :count]]).astype(jnp.int32)
    return outer_step(neighbours, rim_lists, own, live, below, above, pair, part, edge)


def solution(mesh):
    in_specs = (
        P(None, ("region", "sub"), None),
        P(("region", "sub"), None),
        P(("region", "sub"), None),
        P(("region", "sub")),
        P(("region", "sub")),
        P(("region", "sub"), None),
    )
    out_specs = (P(("region", "sub"), None), P(None, ("region", "sub"), None))
    return jax.shard_map(
        per_device, mesh=mesh, in_specs=in_specs, out_specs=out_specs, check_vma=False
    )
```

profile of v0, /device:TPU:0, one launch (start us, length us, event | category | flops | bytes accessed | tf_op | source)
XLA Modules:
  0.0 29.5 jit_solution(1822236500593307429)
XLA Ops:
  0.6 1.8 %group_tiles.1 = f32[4,80,128]{2,1,0:T(8,128)} custom-call(s32[64]{0:T(128)} %owners_ref.1, f32[3,64,128]{2,1,0:T(8,128)} %coords_ref.1, f32[64,128]{1,0:T(8,128)} %smooth_ref.1, f32[64,128]{1,0:T(8,128)} %masses_ref.1), custom_call_target="tpu_custom_call" | custom-call | tf_op jit(solution)/shard_map/group_tiles/pallas_call | solution.py:49
  2.4 4.3 %all-to-all-start = ((f32[4,80,128]{2,1,0:T(8,128)}), f32[4,80,128]{2,1,0:T(8,128)S(1)}, u32[]{:S(2)}, u32[]{:S(2)}) async-start(f32[4,80,128]{2,1,0:T(8,128)} %group_tiles.1), calls=%async_computation | async-start | bytes 327680 | tf_op jit(solution)/shard_map/all_to_all | solution.py:317
  6.7 0.8 %slice_convert_fusion.1 = (f32[4,4]{0,1:T(4,128)S(1)}, f32[4,4]{0,1:T(4,128)S(1)}) fusion(s32[64,4]{0,1:T(4,128)} %param.11), kind=kLoop, calls=%fused_computation.14 | loop fusion | flops 32 | bytes 256 | tf_op jit(solution)/shard_map/convert_element_type | solution.py:332
  7.5 0.8 %copy.11.lists_ref = s32[64,4]{1,0:T(8,128)S(1)} copy(s32[64,4]{0,1:T(4,128)} %param.11) | data formatting | bytes 2048 | tf_op args[5]
  8.3 0.1 copy.8
  8.3 0.1 reshape.23
  8.4 0.1 copy.9
  8.5 0.1 reshape.25
  8.6 0.7 %fusion.live_ref = f32[64,128]{1,0:T(8,128)S(1)} fusion(s32[64]{0:T(128)} %param.10), kind=kLoop, calls=%fused_computation.1 | loop fusion | flops 16384 | bytes 33024 | tf_op jit(solution)/shard_map/convert_element_type | solution.py:318
  9.3 2.3 %all-to-all-done.own_ref = f32[4,80,128]{2,1,0:T(8,128)S(1)} async-done(((f32[4,80,128]{2,1,0:T(8,128)}), f32[4,80,128]{2,1,0:T(8,128)S(1)}, u32[]{:S(2)}, u32[]{:S(2)}) %all-to-all-start) | async-done | bytes 163872 | tf_op jit(solution)/shard_map/all_to_all | solution.py:317
  11.7 5.1 %collective-permute-start.1 = (f32[48,128]{1,0:T(8,128)S(1)}, f32[48,128]{1,0:T(8,128)S(1)}, u32[]{:S(2)}, u32[]{:S(2)}) collective-permute-start(f32[48,128]{1,0:T(8,128)S(1)} %select_maximum_fusion), channel_id=1, source_target_pairs={{1,0},{2,1},{3,2},{4,3},{5,4},{6,5},{7,6},{0,7},{9,8},{10,9},{11,1... | collective-permute-start | bytes 73736 | tf_op jit(solution)/shard_map/ppermute | solution.py:338
  16.8 0.1 collective-permute-start
  16.9 5.2 %inner_density.1 = (f32[28,512,256]{2,1,0:T(8,128)S(1)}, f32[448,128]{1,0:T(8,128)S(1)}, bf16[16,128,128]{2,1,0:T(8,128)(2,1)S(1)}) custom-call(s32[64,4]{1,0:T(8,128)S(1)} %copy.11.lists_ref, f32[4,80,128]{2,1,0:T(8,128)S(1)} %all-to-all-done.own_ref, f32[64,128]{1,0:T(8,128)S(1)} %fusion.live_ref), custom_call_target="tpu_custom_call" | custom-call | flops 1000000000 | bytes 10000000 | tf_op jit(solution)/shard_map/inner_density/pallas_call | solution.py:265
  22.1 0.0 collective-permute-done.1.above_ref
  22.1 1.3 %collective-permute-done.below_ref = f32[48,128]{1,0:T(8,128)S(1)} collective-permute-done((f32[48,128]{1,0:T(8,128)S(1)}, f32[48,128]{1,0:T(8,128)S(1)}, u32[]{:S(2)}, u32[]{:S(2)}) %collective-permute-start) | collective-permute-done | bytes 24608 | tf_op jit(solution)/shard_map/ppermute | solution.py:337
  23.4 0.1 maximum_convert_fusion.rim_lists_ref
  23.5 6.0 %outer_step.1 = (f32[64,128]{1,0:T(8,128)}, f32[3,64,128]{2,1,0:T(8,128)}) custom-call(s32[64,4]{1,0:T(8,128)S(1)} %copy.11.lists_ref, s32[32]{0:T(128)S(1)} %maximum_convert_fusion.rim_lists_ref, f32[4,80,128]{2,1,0:T(8,128)S(1)} %all-to-all-done.own_ref, f32[64,128]{1,0:T(8,128)S(1)} %fusion.live_ref, f32[48,128]{1,0:T(8,128)S(1)} %collective-permute-done.below_ref, ...), custom_call_target="tpu_custom_call" | custom-call | tf_op jit(solution)/shard_map/outer_step/pallas_call | solution.py:290
  (10 shorter events, 0.0 us)
Async XLA Ops:
  2.4 9.2 %all-to-all-start = ((f32[4,80,128]{2,1,0:T(8,128)}), f32[4,80,128]{2,1,0:T(8,128)S(1)}, u32[]{:S(2)}, u32[]{:S(2)}) async-start(f32[4,80,128]{2,1,0:T(8,128)} %group_tiles.1), calls=%async_computation | async-start | bytes 327680 | tf_op jit(solution)/shard_map/all_to_all | solution.py:317
  11.7 10.4 %collective-permute-start.1 = (f32[48,128]{1,0:T(8,128)S(1)}, f32[48,128]{1,0:T(8,128)S(1)}, u32[]{:S(2)}, u32[]{:S(2)}) collective-permute-start(f32[48,128]{1,0:T(8,128)S(1)} %select_maximum_fusion), channel_id=1, source_target_pairs={{1,0},{2,1},{3,2},{4,3},{5,4},{6,5},{7,6},{0,7},{9,8},{10,9},{11,1... | collective-permute-start | bytes 73736 | tf_op jit(solution)/shard_map/ppermute | solution.py:338
  16.8 6.6 %collective-permute-start = (f32[48,128]{1,0:T(8,128)S(1)}, f32[48,128]{1,0:T(8,128)S(1)}, u32[]{:S(2)}, u32[]{:S(2)}) collective-permute-start(f32[48,128]{1,0:T(8,128)S(1)} %select_maximum_fusion.1), channel_id=1, source_target_pairs={{0,1},{1,2},{2,3},{3,4},{4,5},{5,6},{6,7},{7,0},{8,9},{9,10},{10,1... | collective-permute-start | bytes 73736 | tf_op jit(solution)/shard_map/ppermute | solution.py:337
where the time goes:
time: 29.8 us; the launch traced here: 29.5 us
  Pallas kernels  13 us (44%)
  starting transfers between devices  9.43 us (32%)
  waiting for transfers between devices  3.57 us (12%)
  other arithmetic  1.67 us (6%)
  local copies, waits for them, and re-layouts  1.14 us (4%)
  between operations  0.7 us (2%)
    pallas_call x1, Pallas kernels, outer_step(): pl.pallas_call(outer_kernel, out_shape=(jax.ShapeDtypeStruct((tile_dev, r...  6.03 us
    pallas_call x1, Pallas kernels, inner_density(): pl.pallas_call(inner_kernel, out_shape=(jax.ShapeDtypeStruct((count, list...  5.18 us
    ppermute x1, starting transfers between devices, per_device(): above = lax.ppermute(rim(True), 'sub', down)  5.11 us
    all_to_all x1, starting transfers between devices, per_device(): own = lax.all_to_all(grouped, 'region', 0, 0, tiled=True)  4.26 us
    all_to_all x1, waiting for transfers between devices, per_device(): own = lax.all_to_all(grouped, 'region', 0, 0, tiled=True)  2.27 us
    pallas_call x1, Pallas kernels, group_tiles(): pl.pallas_call(functools.partial(group_kernel, per_dest), out_shape=jax.S...  1.76 us
    ppermute x1, waiting for transfers between devices, per_device(): below = lax.ppermute(rim(False), 'sub', up)  1.3 us
    convert_element_type x1, other arithmetic, rim(): ids = neighbours[near].astype(f32).reshape(1, HALO_TILES * listed)  0.83 us
  transfers between devices with their start and end apart: 3, of which 2 were waited for; matrix products, arithmetic and copies ran while one was open for 9% of the time, Pallas kernels for 18%

commit v1 on v0

--- a/solution.py
+++ b/solution.py
@@ -22,11 +22,24 @@
 SMEM = pl.BlockSpec(memory_space=pltpu.SMEM)
 
 
-def group_kernel(per_dest, owners_ref, coords_ref, smooth_ref, masses_ref, out_ref):
-    regions = out_ref.shape[0]
+def group_kernel(pairwise, owners_ref, coords_hbm, smooth_hbm, masses_hbm, *refs):
+    outs, (coords_ref, smooth_ref, masses_ref, sems) = refs[:-4], refs[-4:]
+    copies = [
+        pltpu.make_async_copy(source, target, sems.at[i])
+        for i, (source, target) in enumerate(
+            [(coords_hbm, coords_ref), (smooth_hbm, smooth_ref), (masses_hbm, masses_ref)]
+        )
+    ]
+    for copy in copies:
+        copy.start()
+    block_ref, outs = outs[-1], outs[:-1]
+    regions = block_ref.shape[0]
+    per_dest = block_ref.shape[1] // FIELDS
     bits = per_dest.bit_length()
     per_word = 31 // bits
     seen = [jnp.int32(0)] * pl.cdiv(regions, per_word)
+    me = lax.axis_index("region") if pairwise else 0
+    places = []
     for n in range(owners_ref.shape[0]):
         d = owners_ref[n]
         word = d // per_word if len(seen) > 1 else 0
@@ -37,20 +50,33 @@
         k = (k >> shift) & ((1 << bits) - 1)
         step = jnp.int32(1) << shift
         seen = [s + (jnp.where(word == w, step, 0) if len(seen) > 1 else step) for w, s in enumerate(seen)]
+        places.append((d ^ me if pairwise else d, k))
+    for copy in copies:
+        copy.wait()
+    for n, (d, k) in enumerate(places):
         for c in range(3):
-            out_ref[d, pl.ds(c * per_dest + k, 1)] = coords_ref[c, n:n + 1]
-        out_ref[d, pl.ds(3 * per_dest + k, 1)] = smooth_ref[n:n + 1]
-        out_ref[d, pl.ds(4 * per_dest + k, 1)] = masses_ref[n:n + 1]
-
-
-def group_tiles(coords, smooth, masses, owners, regions):
+            block_ref[d, pl.ds(c * per_dest + k, 1)] = coords_ref[c, n:n + 1]
+        block_ref[d, pl.ds(3 * per_dest + k, 1)] = smooth_ref[n:n + 1]
+        block_ref[d, pl.ds(4 * per_dest + k, 1)] = masses_ref[n:n + 1]
+    for k, out in enumerate(outs):
+        out[...] = block_ref[k]
+
+
+def group_tiles(coords, smooth, masses, owners, regions, pairwise):
     tile_dev, rows = smooth.shape
     per_dest = tile_dev // regions
+    block = (FIELDS * per_dest, rows)
+    hbm = pl.BlockSpec(memory_space=pltpu.HBM)
+    scratch = [pltpu.VMEM(a.shape, f32) for a in (coords, smooth, masses)] + [pltpu.SemaphoreType.DMA((3,))]
+    whole = (regions,) + block
+    shapes = [block] * regions if pairwise else [whole]
     return pl.pallas_call(
-        functools.partial(group_kernel, per_dest),
-        out_shape=jax.ShapeDtypeStruct((regions, FIELDS * per_dest, rows), f32),
-        in_specs=[SMEM, VMEM, VMEM, VMEM],
-        out_specs=VMEM,
+        functools.partial(group_kernel, pairwise),
+        out_shape=[jax.ShapeDtypeStruct(shape, f32) for shape in shapes],
+        in_specs=[SMEM, hbm, hbm, hbm],
+        out_specs=[VMEM] * len(shapes),
+        scratch_shapes=([pltpu.VMEM(whole, f32)] if pairwise else []) + scratch,
+        compiler_params=pltpu.CompilerParams(vmem_limit_bytes=63000000),
         name="group_tiles",
     )(owners, coords, smooth, masses)
 
@@ -68,10 +94,11 @@
     return jnp.dot(a, b, preferred_element_type=f32)
 
 
-def own_field(own_ref, live_ref, f):
+def own_field(block_ref, own_ref, live_ref, f):
     tile_dev = live_ref.shape[0]
     regions, per_dest = own_ref.shape[0], tile_dev // own_ref.shape[0]
-    value = jnp.concatenate([own_ref[r, f * per_dest:(f + 1) * per_dest] for r in range(regions)], axis=0)
+    rows = pl.ds(f * per_dest, per_dest)
+    value = jnp.concatenate([own_ref[block_ref[0] ^ r, rows] for r in range(regions)], axis=0)
     return value * live_ref[...] if f == 4 else value
 
 
@@ -134,11 +161,11 @@
 
 
 def inner_kernel(
-    lists_ref, own_ref, live_ref, pair_ref, part_ref, edge_ref, partner_ref, mine_ref, turned_ref, weights_ref,
+    block_ref, lists_ref, own_ref, live_ref, pair_ref, part_ref, edge_ref, partner_ref, mine_ref, turned_ref, weights_ref,
 ):
     tile_dev = live_ref.shape[0]
     listed = lists_ref.shape[1]
-    pos, live, mass, inverse_sq, _ = field_terms([own_field(own_ref, live_ref, f) for f in range(FIELDS)])
+    pos, live, mass, inverse_sq, _ = field_terms([own_field(block_ref, own_ref, live_ref, f) for f in range(FIELDS)])
     put_features(pos, live, mass, inverse_sq, partner_ref, mine_ref)
 
     @pl.loop(0, tile_dev, unroll=8)
@@ -161,7 +188,7 @@
 
 
 def outer_kernel(
-    lists_ref, rim_lists_ref, own_ref, live_ref, below_ref, above_ref, pair_ref, part_ref, edge_ref,
+    block_ref, lists_ref, rim_lists_ref, own_ref, live_ref, below_ref, above_ref, pair_ref, part_ref, edge_ref,
     density_ref, accel_ref, partner_ref, mine_ref, turned_ref, rim_pair_ref, rim_part_ref, coef_ref, coefb_ref, out_ref,
 ):
     tile_dev, rows = live_ref.shape
@@ -169,7 +196,7 @@
     listed = lists_ref.shape[1]
     fields = [
         jnp.concatenate(
-            [below_ref[f * RIM:(f + 1) * RIM], own_field(own_ref, live_ref, f), above_ref[f * RIM:(f + 1) * RIM]], axis=0
+            [below_ref[f * RIM:(f + 1) * RIM], own_field(block_ref, own_ref, live_ref, f), above_ref[f * RIM:(f + 1) * RIM]], axis=0
         )
         for f in range(FIELDS)
     ]
@@ -258,7 +285,7 @@
         accel_ref[c] = scale * (q_own * (x * sums[0] - sums[1 + c]) + (x * sums[4] - sums[5 + c]))
 
 
-def inner_density(lists, own, live):
+def inner_density(block, lists, own, live):
     tile_dev, rows = live.shape
     listed = lists.shape[1]
     count = (tile_dev - RIM) // 2
@@ -269,7 +296,7 @@
             jax.ShapeDtypeStruct((16 * count, rows), f32),
             jax.ShapeDtypeStruct((2 * RIM, rows, rows), bf16),
         ),
-        in_specs=[SMEM, VMEM, VMEM],
+        in_specs=[SMEM, SMEM, VMEM, VMEM],
         out_specs=(VMEM, VMEM, VMEM),
         scratch_shapes=[
             pltpu.VMEM((8 * tile_dev, rows), f32),
@@ -280,17 +307,17 @@
         compiler_params=pltpu.CompilerParams(vmem_limit_bytes=24 << 20),
         cost_estimate=pl.CostEstimate(flops=10 ** 9, bytes_accessed=10 ** 7, transcendentals=0),
         name="inner_density",
-    )(lists, own, live)
-
-
-def outer_step(lists, rim_lists, own, live, below, above, pair, part, edge):
+    )(block, lists, own, live)
+
+
+def outer_step(block, lists, rim_lists, own, live, below, above, pair, part, edge):
     tile_dev, rows = live.shape
     ext = tile_dev + 2 * RIM
     listed = lists.shape[1]
     return pl.pallas_call(
         outer_kernel,
         out_shape=(jax.ShapeDtypeStruct((tile_dev, rows), f32), jax.ShapeDtypeStruct((3, tile_dev, rows), f32)),
-        in_specs=[SMEM, SMEM] + [VMEM] * 7,
+        in_specs=[SMEM] * 3 + [VMEM] * 7,
         out_specs=(VMEM, VMEM),
         scratch_shapes=[
             pltpu.VMEM((8 * 4 * RIM, rows), f32),
@@ -304,7 +331,7 @@
         ],
         compiler_params=pltpu.CompilerParams(vmem_limit_bytes=24 << 20),
         name="outer_step",
-    )(lists, rim_lists, own, live, below, above, pair, part, edge)
+    )(block, lists, rim_lists, own, live, below, above, pair, part, edge)
 
 
 def per_device(coords, smooth, masses, owners, counts, neighbours):
@@ -313,14 +340,24 @@
     subs = lax.axis_size("sub")
     per_dest = tile_dev // regions
     listed = neighbours.shape[1]
-    grouped = group_tiles(coords, smooth, masses, owners, regions)
-    own = lax.all_to_all(grouped, "region", 0, 0, tiled=True)
+    pairwise = regions <= 4 and regions & (regions - 1) == 0
+    grouped = group_tiles(coords, smooth, masses, owners, regions, pairwise)
+    if pairwise:
+        me = lax.axis_index("region")
+        blocks = [grouped[0]]
+        for k in range(1, regions):
+            blocks.append(lax.ppermute(grouped[k], "region", [(i, i ^ k) for i in range(regions)]))
+        own = jnp.stack(blocks)
+    else:
+        me = jnp.int32(0)
+        own = lax.all_to_all(grouped[0], "region", 0, 0, tiled=True)
+    first_block = me.astype(jnp.int32).reshape(1)
     live = (jnp.arange(rows, dtype=jnp.int32)[None, :] < counts[:, None]).astype(f32)
     by_field = own.reshape(regions, FIELDS, per_dest, rows)
 
     def rim(first):
-        if per_dest >= RIM:
-            block = by_field[regions - 1 if not first else 0]
+        if pairwise:
+            block = lax.dynamic_index_in_dim(by_field, me ^ (0 if first else regions - 1), 0, keepdims=False)
             block = block[:, :RIM] if first else block[:, per_dest - RIM:]
         else:
             blocks = RIM // per_dest
@@ -336,10 +373,10 @@
     down = [(j, i) for i, j in up]
     below = lax.ppermute(rim(False), "sub", up)
     above = lax.ppermute(rim(True), "sub", down)
-    pair, part, edge = inner_density(neighbours, own, live)
+    pair, part, edge = inner_density(first_block, neighbours, own, live)
     count = HALO_TILES * listed
     rim_lists = jnp.concatenate([below[FIELDS * RIM, :count], above[FIELDS * RIM, :count]]).astype(jnp.int32)
-    return outer_step(neighbours, rim_lists, own, live, below, above, pair, part, edge)
+    return outer_step(first_block, neighbours, rim_lists, own, live, below, above, pair, part, edge)
 
 
 def solution(mesh):

time: 29.8 us -> 28.5 us (0.956)
  waiting for transfers between devices: 3.57 us -> 1.5 us
  starting transfers between devices: 9.43 us -> 7.82 us
  other arithmetic: 1.67 us -> 3.25 us
  Pallas kernels: 13 us -> 13.7 us
    all_to_all x1 -> x0, starting transfers between devices: 4.26 us -> none  [per_device(): own = lax.all_to_all(grouped, 'region', 0, 0, tiled=True)]
    ppermute x0 -> x3, starting transfers between devices: none -> 3.18 us  [per_device(): lax.ppermute(grouped[k], 'region', [(i, i ^ k) for i in range(regions)])]
    all_to_all x1 -> x0, waiting for transfers between devices: 2.27 us -> none  [per_device(): own = lax.all_to_all(grouped, 'region', 0, 0, tiled=True)]
    another operation x0 -> x2, other arithmetic: none -> 1.58 us  [per_device(): own = jnp.stack(blocks)]
    ppermute x0 -> x3, waiting for transfers between devices: none -> 1.01 us  [per_device(): lax.ppermute(grouped[k], 'region', [(i, i ^ k) for i in range(regions)])]
    ppermute x1, waiting for transfers between devices: 1.3 us -> 0.48 us  [per_device(): below = lax.ppermute(rim(False), 'sub', up)]
    pallas_call x1, Pallas kernels: 1.76 us -> 2.39 us  [group_tiles(): pl.pallas_call(functools.partial(group_kernel, pairwise), out_shape=[jax....]
    ppermute x1, starting transfers between devices: 5.11 us -> 4.58 us  [per_device(): above = lax.ppermute(rim(True), 'sub', down)]
  transfers between devices with their start and end apart: 3 -> 5, of which waited for: 2 -> 2; matrix products, arithmetic and copies ran while one was open for 9% -> 12% of each run, Pallas kernels for 18% -> 18%
where the time goes in v1:
time: 28.5 us; the launch traced here: 28.2 us
  Pallas kernels  13.7 us (48%)
  starting transfers between devices  7.82 us (27%)
  other arithmetic  3.25 us (11%)
  waiting for transfers between devices  1.5 us (5%)
  local copies, waits for them, and re-layouts  1.15 us (4%)
  between operations  0.73 us (3%)
    pallas_call x1, Pallas kernels, outer_step(): pl.pallas_call(outer_kernel, out_shape=(jax.ShapeDtypeStruct((tile_dev, r...  6.12 us
    pallas_call x1, Pallas kernels, inner_density(): pl.pallas_call(inner_kernel, out_shape=(jax.ShapeDtypeStruct((count, list...  5.2 us
    ppermute x1, starting transfers between devices, per_device(): above = lax.ppermute(rim(True), 'sub', down)  4.58 us
    ppermute x3, starting transfers between devices, per_device(): lax.ppermute(grouped[k], 'region', [(i, i ^ k) for i in range(regions)])  3.18 us
    pallas_call x1, Pallas kernels, group_tiles(): pl.pallas_call(functools.partial(group_kernel, pairwise), out_shape=[jax....  2.39 us
    another operation x2, other arithmetic, per_device(): own = jnp.stack(blocks)  1.58 us
    ppermute x3, waiting for transfers between devices, per_device(): lax.ppermute(grouped[k], 'region', [(i, i ^ k) for i in range(regions)])  1.01 us
    convert_element_type x1, other arithmetic, rim(): ids = neighbours[near].astype(f32).reshape(1, HALO_TILES * listed)  0.83 us
  transfers between devices with their start and end apart: 5, of which 2 were waited for; matrix products, arithmetic and copies ran while one was open for 12% of the time, Pallas kernels for 18%

profile of v1, /device:TPU:0, one launch (start us, length us, event | category | flops | bytes accessed | tf_op | source)
XLA Modules:
  0.0 28.2 jit_solution(4778989183579186944)
XLA Ops:
  0.6 2.4 %group_tiles.1 = (f32[80,128]{1,0:T(8,128)}, f32[80,128]{1,0:T(8,128)}, f32[80,128]{1,0:T(8,128)}, f32[80,128]{1,0:T(8,128)}) custom-call(s32[64]{0:T(128)} %owners_ref.1, f32[3,64,128]{2,1,0:T(8,128)} %coords_hbm.1, f32[64,128]{1,0:T(8,128)} %smooth_hbm.1, f32[64,128]{1,0:T(8,128)} %masses_hbm.1), custom_call_target="tpu_custom_call" | custom-call | tf_op jit(solution)/shard_map/group_tiles/pallas_call | solution.py:73
  3.0 0.6 %collective-permute-start = (f32[80,128]{1,0:T(8,128)}, f32[80,128]{1,0:T(8,128)S(1)}, u32[]{:S(2)}, u32[]{:S(2)}) collective-permute-start(f32[80,128]{1,0:T(8,128)} %get-tuple-element.10), channel_id=1, source_target_pairs={{0,8},{8,0},{16,24},{24,16},{1,9},{9,1},{17,25},{25,17},{2,10},{10... | collective-permute-start | bytes 122888 | tf_op jit(solution)/shard_map/ppermute | solution.py:349
  3.6 2.6 %collective-permute-start.1 = (f32[80,128]{1,0:T(8,128)}, f32[80,128]{1,0:T(8,128)S(1)}, u32[]{:S(2)}, u32[]{:S(2)}) collective-permute-start(f32[80,128]{1,0:T(8,128)} %get-tuple-element.11), channel_id=1, source_target_pairs={{0,16},{8,24},{16,0},{24,8},{1,17},{9,25},{17,1},{25,9},{2,18},{10... | collective-permute-start | bytes 122888 | tf_op jit(solution)/shard_map/ppermute | solution.py:349
  6.2 0.0 collective-permute-start.2
  6.2 0.7 %fusion.live_ref = f32[64,128]{1,0:T(8,128)S(1)} fusion(s32[64]{0:T(128)} %param.10), kind=kLoop, calls=%fused_computation.5 | loop fusion | flops 16384 | bytes 33024 | tf_op jit(solution)/shard_map/convert_element_type | solution.py:355
  6.9 0.8 %slice_convert_fusion.1 = (f32[4,4]{0,1:T(4,128)S(1)}, f32[4,4]{0,1:T(4,128)S(1)}) fusion(s32[64,4]{0,1:T(4,128)} %param.11), kind=kLoop, calls=%fused_computation.18 | loop fusion | flops 32 | bytes 256 | tf_op jit(solution)/shard_map/convert_element_type | solution.py:369
  7.8 0.8 %copy.11.lists_ref = s32[64,4]{1,0:T(8,128)S(1)} copy(s32[64,4]{0,1:T(4,128)} %param.11) | data formatting | bytes 2048 | tf_op args[5]
  8.5 0.1 copy.8
  8.6 0.1 reshape.31
  8.7 0.1 copy.9
  8.8 0.1 reshape.33
  8.9 0.0 collective-permute-done
  8.9 0.0 collective-permute-done.1
  8.9 1.0 %collective-permute-done.2 = f32[80,128]{1,0:T(8,128)S(1)} collective-permute-done((f32[80,128]{1,0:T(8,128)}, f32[80,128]{1,0:T(8,128)S(1)}, u32[]{:S(2)}, u32[]{:S(2)}) %collective-permute-start.2) | collective-permute-done | bytes 40992 | tf_op jit(solution)/shard_map/ppermute | solution.py:349
  9.9 0.8 %pad_maximum_fusion = f32[4,5,16,128]{3,2,1,0:T(8,128)S(1)} fusion(f32[1,5,16,128]{3,2,1,0:T(8,128)S(1)} %bitcast.39, f32[1,5,16,128]{3,2,1,0:T(8,128)S(1)} %bitcast.37, f32[1,5,16,128]{3,2,1,0:T(8,128)S(1)} %bitcast.35, f32[1,5,16,128]{3,2,1,0:T(8,128)} %bitcast.33), kind=kLoop, calls=%fused_computation | loop fusion | flops 122880 | bytes 327680 | tf_op jit(solution)/shard_map/stack | solution.py:350
  10.8 4.6 %collective-permute-start.4 = (f32[48,128]{1,0:T(8,128)S(1)}, f32[48,128]{1,0:T(8,128)S(1)}, u32[]{:S(2)}, u32[]{:S(2)}) collective-permute-start(f32[48,128]{1,0:T(8,128)S(1)} %select_maximum_fusion), channel_id=1, source_target_pairs={{1,0},{2,1},{3,2},{4,3},{5,4},{6,5},{7,6},{0,7},{9,8},{10,9},{11,1... | collective-permute-start | bytes 73736 | tf_op jit(solution)/shard_map/ppermute | solution.py:375
  15.4 0.1 collective-permute-start.3
  15.4 0.8 %pad_maximum_fusion.1.own_ref = f32[4,80,128]{2,1,0:T(8,128)S(1)} fusion(f32[1,80,128]{2,1,0:T(8,128)S(1)} %bitcast.40, f32[1,80,128]{2,1,0:T(8,128)S(1)} %bitcast.38, f32[1,80,128]{2,1,0:T(8,128)S(1)} %bitcast.36, f32[1,80,128]{2,1,0:T(8,128)} %bitcast.34), kind=kLoop, calls=%fused_computation.1 | loop fusion | flops 122880 | bytes 327680 | tf_op jit(solution)/shard_map/stack | solution.py:350
  16.2 5.2 %inner_density.1 = (f32[28,512,256]{2,1,0:T(8,128)S(1)}, f32[448,128]{1,0:T(8,128)S(1)}, bf16[16,128,128]{2,1,0:T(8,128)(2,1)S(1)}) custom-call(s32[1]{0:T(128)} %bitcast.block_ref, s32[64,4]{1,0:T(8,128)S(1)} %copy.11.lists_ref, f32[4,80,128]{2,1,0:T(8,128)S(1)} %pad_maximum_fusion.1.own_ref, f32[64,128]{1,0:T(8,128)S(1)} %fusion.live_ref), custom_call_target="tpu_custom_call" | custom-call | flops 1000000000 | bytes 10000000 | tf_op jit(solution)/shard_map/inner_density/pallas_call | solution.py:292
  21.4 0.0 collective-permute-done.4.above_ref
  21.5 0.5 %collective-permute-done.3.below_ref = f32[48,128]{1,0:T(8,128)S(1)} collective-permute-done((f32[48,128]{1,0:T(8,128)S(1)}, f32[48,128]{1,0:T(8,128)S(1)}, u32[]{:S(2)}, u32[]{:S(2)}) %collective-permute-start.3) | collective-permute-done | bytes 24608 | tf_op jit(solution)/shard_map/ppermute | solution.py:374
  22.0 0.1 maximum_convert_fusion.rim_lists_ref
  22.0 6.1 %outer_step.1 = (f32[64,128]{1,0:T(8,128)}, f32[3,64,128]{2,1,0:T(8,128)}) custom-call(s32[1]{0:T(128)} %bitcast.block_ref, s32[64,4]{1,0:T(8,128)S(1)} %copy.11.lists_ref, s32[32]{0:T(128)S(1)} %maximum_convert_fusion.rim_lists_ref, f32[4,80,128]{2,1,0:T(8,128)S(1)} %pad_maximum_fusion.1.own_ref, f32[64,128]{1,0:T(8,128)S(1)} %fusion.live_ref, ...), custom_call_target="tpu_custom_call" | custom-call | tf_op jit(solution)/shard_map/outer_step/pallas_call | solution.py:317
  (10 shorter events, 0.1 us)
Async XLA Ops:
  3.0 5.9 %collective-permute-start = (f32[80,128]{1,0:T(8,128)}, f32[80,128]{1,0:T(8,128)S(1)}, u32[]{:S(2)}, u32[]{:S(2)}) collective-permute-start(f32[80,128]{1,0:T(8,128)} %get-tuple-element.10), channel_id=1, source_target_pairs={{0,8},{8,0},{16,24},{24,16},{1,9},{9,1},{17,25},{25,17},{2,10},{10... | collective-permute-start | bytes 122888 | tf_op jit(solution)/shard_map/ppermute | solution.py:349
  3.6 5.3 %collective-permute-start.1 = (f32[80,128]{1,0:T(8,128)}, f32[80,128]{1,0:T(8,128)S(1)}, u32[]{:S(2)}, u32[]{:S(2)}) collective-permute-start(f32[80,128]{1,0:T(8,128)} %get-tuple-element.11), channel_id=1, source_target_pairs={{0,16},{8,24},{16,0},{24,8},{1,17},{9,25},{17,1},{25,9},{2,18},{10... | collective-permute-start | bytes 122888 | tf_op jit(solution)/shard_map/ppermute | solution.py:349
  6.2 3.7 %collective-permute-start.2 = (f32[80,128]{1,0:T(8,128)}, f32[80,128]{1,0:T(8,128)S(1)}, u32[]{:S(2)}, u32[]{:S(2)}) collective-permute-start(f32[80,128]{1,0:T(8,128)} %get-tuple-element.12), channel_id=1, source_target_pairs={{0,24},{8,16},{16,8},{24,0},{1,25},{9,17},{17,9},{25,1},{2,26},{10... | collective-permute-start | bytes 122888 | tf_op jit(solution)/shard_map/ppermute | solution.py:349
  10.8 10.7 %collective-permute-start.4 = (f32[48,128]{1,0:T(8,128)S(1)}, f32[48,128]{1,0:T(8,128)S(1)}, u32[]{:S(2)}, u32[]{:S(2)}) collective-permute-start(f32[48,128]{1,0:T(8,128)S(1)} %select_maximum_fusion), channel_id=1, source_target_pairs={{1,0},{2,1},{3,2},{4,3},{5,4},{6,5},{7,6},{0,7},{9,8},{10,9},{11,1... | collective-permute-start | bytes 73736 | tf_op jit(solution)/shard_map/ppermute | solution.py:375
  15.4 6.6 %collective-permute-start.3 = (f32[48,128]{1,0:T(8,128)S(1)}, f32[48,128]{1,0:T(8,128)S(1)}, u32[]{:S(2)}, u32[]{:S(2)}) collective-permute-start(f32[48,128]{1,0:T(8,128)S(1)} %select_maximum_fusion.1), channel_id=1, source_target_pairs={{0,1},{1,2},{2,3},{3,4},{4,5},{5,6},{6,7},{7,0},{8,9},{9,10},{10,1... | collective-permute-start | bytes 73736 | tf_op jit(solution)/shard_map/ppermute | solution.py:374

commit v2 on v1

--- a/solution.py
+++ b/solution.py
@@ -22,17 +22,14 @@
 SMEM = pl.BlockSpec(memory_space=pltpu.SMEM)
 
 
-def group_kernel(pairwise, owners_ref, coords_hbm, smooth_hbm, masses_hbm, *refs):
-    outs, (coords_ref, smooth_ref, masses_ref, sems) = refs[:-4], refs[-4:]
-    copies = [
-        pltpu.make_async_copy(source, target, sems.at[i])
-        for i, (source, target) in enumerate(
-            [(coords_hbm, coords_ref), (smooth_hbm, smooth_ref), (masses_hbm, masses_ref)]
-        )
-    ]
+def group_kernel(pairwise, count, *refs):
+    sources, outs = refs[:4], refs[4:4 + count]
+    owners_ref, coords_ref, smooth_ref, masses_ref, block_ref, sems, out_sems = refs[4 + count:]
+    targets = (owners_ref, coords_ref, smooth_ref, masses_ref)
+    copies = [pltpu.make_async_copy(s, t, sems.at[i]) for i, (s, t) in enumerate(zip(sources, targets))]
     for copy in copies:
         copy.start()
-    block_ref, outs = outs[-1], outs[:-1]
+    copies[0].wait()
     regions = block_ref.shape[0]
     per_dest = block_ref.shape[1] // FIELDS
     bits = per_dest.bit_length()
@@ -51,15 +48,20 @@
         step = jnp.int32(1) << shift
         seen = [s + (jnp.where(word == w, step, 0) if len(seen) > 1 else step) for w, s in enumerate(seen)]
         places.append((d ^ me if pairwise else d, k))
-    for copy in copies:
+    for copy in copies[1:]:
         copy.wait()
     for n, (d, k) in enumerate(places):
         for c in range(3):
             block_ref[d, pl.ds(c * per_dest + k, 1)] = coords_ref[c, n:n + 1]
         block_ref[d, pl.ds(3 * per_dest + k, 1)] = smooth_ref[n:n + 1]
         block_ref[d, pl.ds(4 * per_dest + k, 1)] = masses_ref[n:n + 1]
-    for k, out in enumerate(outs):
-        out[...] = block_ref[k]
+    copies = [
+        pltpu.make_async_copy(block_ref.at[k] if pairwise else block_ref, out, out_sems.at[k]) for k, out in enumerate(outs)
+    ]
+    for copy in copies:
+        copy.start()
+    for copy in copies:
+        copy.wait()
 
 
 def group_tiles(coords, smooth, masses, owners, regions, pairwise):
@@ -67,18 +69,53 @@
     per_dest = tile_dev // regions
     block = (FIELDS * per_dest, rows)
     hbm = pl.BlockSpec(memory_space=pltpu.HBM)
-    scratch = [pltpu.VMEM(a.shape, f32) for a in (coords, smooth, masses)] + [pltpu.SemaphoreType.DMA((3,))]
     whole = (regions,) + block
     shapes = [block] * regions if pairwise else [whole]
     return pl.pallas_call(
-        functools.partial(group_kernel, pairwise),
+        functools.partial(group_kernel, pairwise, len(shapes)),
         out_shape=[jax.ShapeDtypeStruct(shape, f32) for shape in shapes],
-        in_specs=[SMEM, hbm, hbm, hbm],
-        out_specs=[VMEM] * len(shapes),
-        scratch_shapes=([pltpu.VMEM(whole, f32)] if pairwise else []) + scratch,
-        compiler_params=pltpu.CompilerParams(vmem_limit_bytes=63000000),
+        in_specs=[hbm] * 4,
+        out_specs=[hbm] * len(shapes),
+        scratch_shapes=[pltpu.SMEM(owners.shape, jnp.int32)]
+        + [pltpu.VMEM(a.shape, f32) for a in (coords, smooth, masses)]
+        + [pltpu.VMEM(whole, f32), pltpu.SemaphoreType.DMA((4,)), pltpu.SemaphoreType.DMA((len(shapes),))],
         name="group_tiles",
     )(owners, coords, smooth, masses)
+
+
+def stage_kernel(lists_ref, local_ref, live_ref, ids_ref, here_ref):
+    tile_dev, rows = live_ref.shape
+    listed = lists_ref.shape[0] - 1
+    lane = lax.broadcasted_iota(jnp.int32, (8, rows), 1)
+    row = lax.broadcasted_iota(jnp.int32, (8, rows), 0)
+    for t in range(0, tile_dev, 8):
+        limit = jnp.full((8, rows), lists_ref[listed, t])
+        for i in range(1, 8):
+            limit = jnp.where(row == i, lists_ref[listed, t + i], limit)
+        live_ref[t:t + 8] = (lane < limit).astype(f32)
+    for side, start in enumerate((0, tile_dev - HALO_TILES)):
+        ids = jnp.zeros((8, rows), f32)
+        for i in range(HALO_TILES):
+            for n in range(listed):
+                ids = jnp.where(lane == i * listed + n, lists_ref[n, start + i].astype(f32), ids)
+        ids_ref[side] = ids
+    here_ref[...] = local_ref[...]
+
+
+def stage(lists, local):
+    tile_dev, rows = lists.shape[1], local.shape[-1]
+    return pl.pallas_call(
+        stage_kernel,
+        out_shape=(
+            jax.ShapeDtypeStruct((tile_dev, rows), f32),
+            jax.ShapeDtypeStruct((2, 8, rows), f32),
+            jax.ShapeDtypeStruct(local.shape, f32),
+        ),
+        in_specs=[SMEM, VMEM],
+        out_specs=(VMEM,) * 3,
+        compiler_params=pltpu.CompilerParams(vmem_limit_bytes=4 << 20),
+        name="stage",
+    )(lists, local)
 
 
 def parts_of(x, count):
@@ -164,7 +201,7 @@
     block_ref, lists_ref, own_ref, live_ref, pair_ref, part_ref, edge_ref, partner_ref, mine_ref, turned_ref, weights_ref,
 ):
     tile_dev = live_ref.shape[0]
-    listed = lists_ref.shape[1]
+    listed = lists_ref.shape[0] - 1
     pos, live, mass, inverse_sq, _ = field_terms([own_field(block_ref, own_ref, live_ref, f) for f in range(FIELDS)])
     put_features(pos, live, mass, inverse_sq, partner_ref, mine_ref)
 
@@ -183,7 +220,7 @@
     @pl.loop(0, count, unroll=UNROLL)
     def _(p):
         t = HALO_TILES + 2 * p
-        partners = [(lists_ref[t, n] - HALO_TILES, lists_ref[t + 1, n] - HALO_TILES) for n in range(listed)]
+        partners = [(lists_ref[n, t] - HALO_TILES, lists_ref[n, t + 1] - HALO_TILES) for n in range(listed)]
         density_pair(turned_ref, weights_ref[p], partners, part_ref, 16 * p, pair_ref.at[p])
 
 
@@ -193,7 +230,7 @@
 ):
     tile_dev, rows = live_ref.shape
     ext = tile_dev + 2 * RIM
-    listed = lists_ref.shape[1]
+    listed = lists_ref.shape[0] - 1
     fields = [
         jnp.concatenate(
             [below_ref[f * RIM:(f + 1) * RIM], own_field(block_ref, own_ref, live_ref, f), above_ref[f * RIM:(f + 1) * RIM]], axis=0
@@ -221,7 +258,7 @@
             if own_side:
                 t = e - RIM if side == 0 else e - 3 * RIM + tile_dev
                 shift = HALO_TILES if side == 0 else HALO_TILES - tile_dev + 2 * RIM
-                partners = [(lists_ref[t, n] + shift, lists_ref[t + 1, n] + shift) for n in range(listed)]
+                partners = [(lists_ref[n, t] + shift, lists_ref[n, t + 1] + shift) for n in range(listed)]
                 store = rim_pair_ref.at[half * side + i % half]
             else:
                 first = (2 * i if side == 0 else HALO_TILES + 2 * (i - half)) * listed
@@ -256,7 +293,7 @@
     def force_pair(t, pair):
         total = None
         for n in range(listed):
-            e0, e1 = lists_ref[t, n] + HALO_TILES, lists_ref[t + 1, n] + HALO_TILES
+            e0, e1 = lists_ref[n, t] + HALO_TILES, lists_ref[n, t + 1] + HALO_TILES
             left = jnp.concatenate([coefb_ref[e0], coefb_ref[e1]], axis=0)
             w = pair[n * rows:(n + 1) * rows]
             high = w.astype(bf16)
@@ -287,7 +324,7 @@
 
 def inner_density(block, lists, own, live):
     tile_dev, rows = live.shape
-    listed = lists.shape[1]
+    listed = lists.shape[0] - 1
     count = (tile_dev - RIM) // 2
     return pl.pallas_call(
         inner_kernel,
@@ -313,7 +350,7 @@
 def outer_step(block, lists, rim_lists, own, live, below, above, pair, part, edge):
     tile_dev, rows = live.shape
     ext = tile_dev + 2 * RIM
-    listed = lists.shape[1]
+    listed = lists.shape[0] - 1
     return pl.pallas_call(
         outer_kernel,
         out_shape=(jax.ShapeDtypeStruct((tile_dev, rows), f32), jax.ShapeDtypeStruct((3, tile_dev, rows), f32)),
@@ -340,19 +377,21 @@
     subs = lax.axis_size("sub")
     per_dest = tile_dev // regions
     listed = neighbours.shape[1]
+    lists = jnp.concatenate([neighbours.T, counts[None]], axis=0)
     pairwise = regions <= 4 and regions & (regions - 1) == 0
     grouped = group_tiles(coords, smooth, masses, owners, regions, pairwise)
     if pairwise:
         me = lax.axis_index("region")
-        blocks = [grouped[0]]
+        live, ids, local = stage(lists, grouped[0])
+        blocks = [local]
         for k in range(1, regions):
             blocks.append(lax.ppermute(grouped[k], "region", [(i, i ^ k) for i in range(regions)]))
         own = jnp.stack(blocks)
     else:
         me = jnp.int32(0)
+        live, ids, _ = stage(lists, grouped[0][0])
         own = lax.all_to_all(grouped[0], "region", 0, 0, tiled=True)
     first_block = me.astype(jnp.int32).reshape(1)
-    live = (jnp.arange(rows, dtype=jnp.int32)[None, :] < counts[:, None]).astype(f32)
     by_field = own.reshape(regions, FIELDS, per_dest, rows)
 
     def rim(first):
@@ -365,18 +404,16 @@
             block = jnp.swapaxes(block, 0, 1).reshape(FIELDS, RIM, rows)
         tiles = slice(0, RIM) if first else slice(tile_dev - RIM, tile_dev)
         block = jnp.concatenate([block[:4], (block[4] * live[tiles])[None]], axis=0).reshape(FIELDS * RIM, rows)
-        near = slice(0, HALO_TILES) if first else slice(tile_dev - HALO_TILES, tile_dev)
-        ids = neighbours[near].astype(f32).reshape(1, HALO_TILES * listed)
-        return jnp.concatenate([block, jnp.pad(ids, ((0, 7), (0, rows - HALO_TILES * listed)))], axis=0)
+        return jnp.concatenate([block, ids[0 if first else 1]], axis=0)
 
     up = [(i, (i + 1) % subs) for i in range(subs)]
     down = [(j, i) for i, j in up]
     below = lax.ppermute(rim(False), "sub", up)
     above = lax.ppermute(rim(True), "sub", down)
-    pair, part, edge = inner_density(first_block, neighbours, own, live)
+    pair, part, edge = inner_density(first_block, lists, own, live)
     count = HALO_TILES * listed
     rim_lists = jnp.concatenate([below[FIELDS * RIM, :count], above[FIELDS * RIM, :count]]).astype(jnp.int32)
-    return outer_step(first_block, neighbours, rim_lists, own, live, below, above, pair, part, edge)
+    return outer_step(first_block, lists, rim_lists, own, live, below, above, pair, part, edge)
 
 
 def solution(mesh):

time: 28.5 us -> 26.5 us (0.930)
  other arithmetic: 3.25 us -> 0.84 us
  waiting for transfers between devices: 1.5 us -> 3.29 us
  Pallas kernels: 13.7 us -> 12.8 us
  local copies, waits for them, and re-layouts: 1.15 us -> 0.81 us
    convert_element_type x2 -> x0, other arithmetic: 1.56 us -> none  [the longest x1 0.83 us: rim(): ids = neighbours[near].astype(f32).reshape(1, HALO_TILES * listed)]
    another operation x2, other arithmetic: 1.58 us -> 0.03 us  [per_device(): own = jnp.stack(blocks)]
    ppermute x1, waiting for transfers between devices: 0.48 us -> 1.74 us  [per_device(): below = lax.ppermute(rim(False), 'sub', up)]
    concatenate x2 -> x3, other arithmetic: 0.02 us -> 0.72 us  [the longest x1 0.71 us: per_device(): lists = jnp.concatenate([neighbours.T, counts[None]], axis=0)]
    ppermute x3, waiting for transfers between devices: 1.01 us -> 1.54 us  [per_device(): lax.ppermute(grouped[k], 'region', [(i, i ^ k) for i in range(regions)])]
    pallas_call x1, Pallas kernels: 5.2 us -> 4.73 us  [inner_density(): pl.pallas_call(inner_kernel, out_shape=(jax.ShapeDtypeStruct((count, list...]
    pallas_call x1, Pallas kernels: 6.12 us -> 5.65 us  [outer_step(): pl.pallas_call(outer_kernel, out_shape=(jax.ShapeDtypeStruct((tile_dev, r...]
    unnamed x1 -> x2, local copies, waits for them, and re-layouts: 0.77 us -> 0.78 us
  transfers between devices with their start and end apart: 5 -> 5, of which waited for: 2 -> 3; matrix products, arithmetic and copies ran while one was open for 12% -> 3% of each run, Pallas kernels for 18% -> 20%
where the time goes in v2:
time: 26.5 us; the launch traced here: 26.2 us
  Pallas kernels  12.8 us (48%)
  starting transfers between devices  7.76 us (29%)
  waiting for transfers between devices  3.29 us (12%)
  other arithmetic  0.84 us (3%)
  local copies, waits for them, and re-layouts  0.81 us (3%)
  between operations  0.76 us (3%)
    pallas_call x1, Pallas kernels, outer_step(): pl.pallas_call(outer_kernel, out_shape=(jax.ShapeDtypeStruct((tile_dev, r...  5.65 us
    pallas_call x1, Pallas kernels, inner_density(): pl.pallas_call(inner_kernel, out_shape=(jax.ShapeDtypeStruct((count, list...  4.73 us
    ppermute x1, starting transfers between devices, per_device(): above = lax.ppermute(rim(True), 'sub', down)  4.58 us
    ppermute x3, starting transfers between devices, per_device(): lax.ppermute(grouped[k], 'region', [(i, i ^ k) for i in range(regions)])  3.18 us
    pallas_call x1, Pallas kernels, group_tiles(): pl.pallas_call(functools.partial(group_kernel, pairwise, len(shapes)), ou...  1.75 us
    ppermute x1, waiting for transfers between devices, per_device(): below = lax.ppermute(rim(False), 'sub', up)  1.74 us
    ppermute x3, waiting for transfers between devices, per_device(): lax.ppermute(grouped[k], 'region', [(i, i ^ k) for i in range(regions)])  1.54 us
    unnamed x2, local copies, waits for them, and re-layouts  0.78 us
  transfers between devices with their start and end apart: 5, of which 3 were waited for; matrix products, arithmetic and copies ran while one was open for 3% of the time, Pallas kernels for 20%

profile of v2, /device:TPU:0, one launch (start us, length us, event | category | flops | bytes accessed | tf_op | source)
XLA Modules:
  0.0 26.2 jit_solution(382797871021146488)
XLA Ops:
  0.6 1.7 %group_tiles.1 = (f32[80,128]{1,0:T(8,128)}, f32[80,128]{1,0:T(8,128)}, f32[80,128]{1,0:T(8,128)}, f32[80,128]{1,0:T(8,128)}) custom-call(s32[64]{0:T(128)} %refs_0_.1, f32[3,64,128]{2,1,0:T(8,128)} %refs_1_.1, f32[64,128]{1,0:T(8,128)} %refs_2_.1, f32[64,128]{1,0:T(8,128)} %refs_3_.1), custom_call_target="tpu_custom_call" | custom-call | tf_op jit(solution)/shard_map/group_tiles/pallas_call | solution.py:74
  2.4 0.6 %collective-permute-start = (f32[80,128]{1,0:T(8,128)}, f32[80,128]{1,0:T(8,128)S(1)}, u32[]{:S(2)}, u32[]{:S(2)}) collective-permute-start(f32[80,128]{1,0:T(8,128)} %get-tuple-element.14), channel_id=1, source_target_pairs={{0,8},{8,0},{16,24},{24,16},{1,9},{9,1},{17,25},{25,17},{2,10},{10... | collective-permute-start | bytes 122888 | tf_op jit(solution)/shard_map/ppermute | solution.py:388
  2.9 2.6 %collective-permute-start.1 = (f32[80,128]{1,0:T(8,128)}, f32[80,128]{1,0:T(8,128)S(1)}, u32[]{:S(2)}, u32[]{:S(2)}) collective-permute-start(f32[80,128]{1,0:T(8,128)} %get-tuple-element.15), channel_id=1, source_target_pairs={{0,16},{8,24},{16,0},{24,8},{1,17},{9,25},{17,1},{25,9},{2,18},{10... | collective-permute-start | bytes 122888 | tf_op jit(solution)/shard_map/ppermute | solution.py:388
  5.5 0.0 collective-permute-start.2
  5.6 0.7 %pad_add_fusion.lists_ref = s32[5,64]{1,0:T(8,128)S(1)} fusion(s32[1,64]{1,0:T(1,128)} %bitcast.52, s32[4,64]{1,0:T(4,128)} %bitcast.51), kind=kLoop, calls=%fused_computation.14 | loop fusion | flops 320 | bytes 2560 | tf_op jit(solution)/shard_map/concatenate | solution.py:380
  6.3 0.0 copy-start
  6.3 0.8 %copy-done = f32[80,128]{1,0:T(8,128)S(1)} copy-done((f32[80,128]{1,0:T(8,128)S(1)}, f32[80,128]{1,0:T(8,128)}, u32[]{:S(2)}) %copy-start) | copy-done | bytes 40984
  7.1 0.6 %stage.1 = (f32[64,128]{1,0:T(8,128)S(1)}, f32[2,8,128]{2,1,0:T(8,128)S(1)}, f32[80,128]{1,0:T(8,128)S(1)}) custom-call(s32[5,64]{1,0:T(8,128)S(1)} %pad_add_fusion.lists_ref, f32[80,128]{1,0:T(8,128)S(1)} %copy-done), custom_call_target="tpu_custom_call" | custom-call | tf_op jit(solution)/shard_map/stage/pallas_call | solution.py:107
  7.7 0.0 collective-permute-done
  7.7 0.2 collective-permute-done.1
  7.9 1.4 %collective-permute-done.2 = f32[80,128]{1,0:T(8,128)S(1)} collective-permute-done((f32[80,128]{1,0:T(8,128)}, f32[80,128]{1,0:T(8,128)S(1)}, u32[]{:S(2)}, u32[]{:S(2)}) %collective-permute-start.2) | collective-permute-done | bytes 40992 | tf_op jit(solution)/shard_map/ppermute | solution.py:388
  9.4 4.6 %collective-permute-start.4 = (f32[48,128]{1,0:T(8,128)S(1)}, f32[48,128]{1,0:T(8,128)S(1)}, u32[]{:S(2)}, u32[]{:S(2)}) collective-permute-start(f32[48,128]{1,0:T(8,128)S(1)} %pad_maximum_fusion.3), channel_id=1, source_target_pairs={{1,0},{2,1},{3,2},{4,3},{5,4},{6,5},{7,6},{0,7},{9,8},{10,9},{11,1... | collective-permute-start | bytes 73736 | tf_op jit(solution)/shard_map/ppermute | solution.py:412
  14.0 0.0 collective-permute-start.3
  14.0 4.7 %inner_density.1 = (f32[28,512,256]{2,1,0:T(8,128)S(1)}, f32[448,128]{1,0:T(8,128)S(1)}, bf16[16,128,128]{2,1,0:T(8,128)(2,1)S(1)}) custom-call(s32[1]{0:T(128)} %bitcast.block_ref, s32[5,64]{1,0:T(8,128)S(1)} %pad_add_fusion.lists_ref, f32[4,80,128]{2,1,0:T(8,128)S(1)} %pad_maximum_fusion.1.own_ref, f32[64,128]{1,0:T(8,128)S(1)} %get-tuple-element.17.live_ref), custom_call_target="tpu_custom_call" | custom-call | flops 1000000000 | bytes 10000000 | tf_op jit(solution)/shard_map/inner_density/pallas_call | solution.py:329
  18.7 0.0 collective-permute-done.4.above_ref
  18.7 1.7 %collective-permute-done.3.below_ref = f32[48,128]{1,0:T(8,128)S(1)} collective-permute-done((f32[48,128]{1,0:T(8,128)S(1)}, f32[48,128]{1,0:T(8,128)S(1)}, u32[]{:S(2)}, u32[]{:S(2)}) %collective-permute-start.3) | collective-permute-done | bytes 24608 | tf_op jit(solution)/shard_map/ppermute | solution.py:411
  20.5 0.1 maximum_convert_fusion.rim_lists_ref
  20.6 5.7 %outer_step.1 = (f32[64,128]{1,0:T(8,128)}, f32[3,64,128]{2,1,0:T(8,128)}) custom-call(s32[1]{0:T(128)} %bitcast.block_ref, s32[5,64]{1,0:T(8,128)S(1)} %pad_add_fusion.lists_ref, s32[32]{0:T(128)S(1)} %maximum_convert_fusion.rim_lists_ref, f32[4,80,128]{2,1,0:T(8,128)S(1)} %pad_maximum_fusion.1.own_ref, f32[64,128]{1,0:T(8,128)S(1)} %get-tuple-element.17.live_ref, ...), custom_call_target="tpu_custom_call" | custom-call | tf_op jit(solution)/shard_map/outer_step/pallas_call | solution.py:354
  (13 shorter events, 0.1 us)
Async XLA Ops:
  2.4 5.3 %collective-permute-start = (f32[80,128]{1,0:T(8,128)}, f32[80,128]{1,0:T(8,128)S(1)}, u32[]{:S(2)}, u32[]{:S(2)}) collective-permute-start(f32[80,128]{1,0:T(8,128)} %get-tuple-element.14), channel_id=1, source_target_pairs={{0,8},{8,0},{16,24},{24,16},{1,9},{9,1},{17,25},{25,17},{2,10},{10... | collective-permute-start | bytes 122888 | tf_op jit(solution)/shard_map/ppermute | solution.py:388
  2.9 5.0 %collective-permute-start.1 = (f32[80,128]{1,0:T(8,128)}, f32[80,128]{1,0:T(8,128)S(1)}, u32[]{:S(2)}, u32[]{:S(2)}) collective-permute-start(f32[80,128]{1,0:T(8,128)} %get-tuple-element.15), channel_id=1, source_target_pairs={{0,16},{8,24},{16,0},{24,8},{1,17},{9,25},{17,1},{25,9},{2,18},{10... | collective-permute-start | bytes 122888 | tf_op jit(solution)/shard_map/ppermute | solution.py:388
  5.5 3.7 %collective-permute-start.2 = (f32[80,128]{1,0:T(8,128)}, f32[80,128]{1,0:T(8,128)S(1)}, u32[]{:S(2)}, u32[]{:S(2)}) collective-permute-start(f32[80,128]{1,0:T(8,128)} %get-tuple-element.16), channel_id=1, source_target_pairs={{0,24},{8,16},{16,8},{24,0},{1,25},{9,17},{17,9},{25,1},{2,26},{10... | collective-permute-start | bytes 122888 | tf_op jit(solution)/shard_map/ppermute | solution.py:388
  6.3 0.8 %copy-start = (f32[80,128]{1,0:T(8,128)S(1)}, f32[80,128]{1,0:T(8,128)}, u32[]{:S(2)}) copy-start(f32[80,128]{1,0:T(8,128)} %get-tuple-element.12.local_ref) | copy-start | bytes 122884
  9.4 9.4 %collective-permute-start.4 = (f32[48,128]{1,0:T(8,128)S(1)}, f32[48,128]{1,0:T(8,128)S(1)}, u32[]{:S(2)}, u32[]{:S(2)}) collective-permute-start(f32[48,128]{1,0:T(8,128)S(1)} %pad_maximum_fusion.3), channel_id=1, source_target_pairs={{1,0},{2,1},{3,2},{4,3},{5,4},{6,5},{7,6},{0,7},{9,8},{10,9},{11,1... | collective-permute-start | bytes 73736 | tf_op jit(solution)/shard_map/ppermute | solution.py:412
  14.0 6.5 %collective-permute-start.3 = (f32[48,128]{1,0:T(8,128)S(1)}, f32[48,128]{1,0:T(8,128)S(1)}, u32[]{:S(2)}, u32[]{:S(2)}) collective-permute-start(f32[48,128]{1,0:T(8,128)S(1)} %pad_maximum_fusion.2), channel_id=1, source_target_pairs={{0,1},{1,2},{2,3},{3,4},{4,5},{5,6},{6,7},{7,0},{8,9},{9,10},{10,1... | collective-permute-start | bytes 73736 | tf_op jit(solution)/shard_map/ppermute | solution.py:411

commit v3 on v2

--- a/solution.py
+++ b/solution.py
@@ -13,6 +13,7 @@
 RIM = 2 * HALO_TILES
 FIELDS = 5
 UNROLL = 7
+CHUNKS = 4
 EMPTY_LOG = -1024.0
 LOG2E = 1.4426950408889634
 kernel_scale = math.pi ** (-1.5)
@@ -197,31 +198,50 @@
     part_ref[pl.ds(at + 8, 8)] = total[:, rows:]
 
 
-def inner_kernel(
-    block_ref, lists_ref, own_ref, live_ref, pair_ref, part_ref, edge_ref, partner_ref, mine_ref, turned_ref, weights_ref,
-):
+def inner_kernel(last, flag_ref, block_ref, lists_ref, own_ref, live_ref, *refs):
+    pair_ref, part_ref, edge_ref, turned_ref, weights_ref, partner_ref, mine_ref = refs[5:] if last else refs
     tile_dev = live_ref.shape[0]
     listed = lists_ref.shape[0] - 1
-    pos, live, mass, inverse_sq, _ = field_terms([own_field(block_ref, own_ref, live_ref, f) for f in range(FIELDS)])
-    put_features(pos, live, mass, inverse_sq, partner_ref, mine_ref)
-
-    @pl.loop(0, tile_dev, unroll=8)
-    def _(t):
+    chunk = pair_ref.shape[0] // CHUNKS
+    ahead = 2 * chunk + 2 * HALO_TILES
+
+    def turn(t):
         turned_ref[t] = turned(partner_ref, t)
 
-    edge_ref[:RIM] = turned_ref[:RIM]
-    edge_ref[RIM:] = turned_ref[tile_dev - RIM:]
-    count = pair_ref.shape[0]
-
-    @pl.loop(0, count, unroll=UNROLL)
-    def _(p):
+    def weigh(p):
         weights_ref[p] = pair_weights(mine_ref, HALO_TILES + 2 * p)
 
-    @pl.loop(0, count, unroll=UNROLL)
-    def _(p):
+    def pair(p):
         t = HALO_TILES + 2 * p
         partners = [(lists_ref[n, t] - HALO_TILES, lists_ref[n, t + 1] - HALO_TILES) for n in range(listed)]
         density_pair(turned_ref, weights_ref[p], partners, part_ref, 16 * p, pair_ref.at[p])
+
+    @pl.when(flag_ref[0] == 1)
+    def _():
+        pos, live, mass, inverse_sq, _ = field_terms(
+            [own_field(block_ref, own_ref, live_ref, f) for f in range(FIELDS)]
+        )
+        put_features(pos, live, mass, inverse_sq, partner_ref, mine_ref)
+        for t in range(ahead):
+            turn(t)
+        for p in range(chunk):
+            weigh(p)
+
+        @pl.loop(0, CHUNKS - 1)
+        def _(c):
+            for i in range(chunk):
+                pair(c * chunk + i)
+            for i in range(2 * chunk):
+                turn(c * 2 * chunk + ahead + i)
+            for i in range(chunk):
+                weigh((c + 1) * chunk + i)
+
+        edge_ref[:RIM] = turned_ref[:RIM]
+        edge_ref[RIM:] = turned_ref[tile_dev - RIM:]
+
+    if last:
+        for i in range(chunk):
+            pair((CHUNKS - 1) * chunk + i)
 
 
 def outer_kernel(
@@ -322,29 +342,29 @@
         accel_ref[c] = scale * (q_own * (x * sums[0] - sums[1 + c]) + (x * sums[4] - sums[5 + c]))
 
 
-def inner_density(block, lists, own, live):
+def inner_density(flag, block, lists, own, live, carried):
     tile_dev, rows = live.shape
     listed = lists.shape[0] - 1
     count = (tile_dev - RIM) // 2
+    last = carried is not None
+    shapes = (
+        jax.ShapeDtypeStruct((count, listed * rows, 2 * rows), f32),
+        jax.ShapeDtypeStruct((16 * count, rows), f32),
+        jax.ShapeDtypeStruct((2 * RIM, rows, rows), bf16),
+        jax.ShapeDtypeStruct((tile_dev, rows, rows), bf16),
+        jax.ShapeDtypeStruct((count, 2 * rows, 2 * rows), bf16),
+    )
     return pl.pallas_call(
-        inner_kernel,
-        out_shape=(
-            jax.ShapeDtypeStruct((count, listed * rows, 2 * rows), f32),
-            jax.ShapeDtypeStruct((16 * count, rows), f32),
-            jax.ShapeDtypeStruct((2 * RIM, rows, rows), bf16),
-        ),
-        in_specs=[SMEM, SMEM, VMEM, VMEM],
-        out_specs=(VMEM, VMEM, VMEM),
-        scratch_shapes=[
-            pltpu.VMEM((8 * tile_dev, rows), f32),
-            pltpu.VMEM((8 * tile_dev, rows), f32),
-            pltpu.VMEM((tile_dev, rows, rows), bf16),
-            pltpu.VMEM((count, 2 * rows, 2 * rows), bf16),
-        ],
+        functools.partial(inner_kernel, last),
+        out_shape=shapes,
+        in_specs=[SMEM] * 3 + [VMEM] * (7 if last else 2),
+        out_specs=(VMEM,) * 5,
+        input_output_aliases={5 + i: i for i in range(5)} if last else {},
+        scratch_shapes=[pltpu.VMEM((8 * tile_dev, rows), f32), pltpu.VMEM((8 * tile_dev, rows), f32)],
         compiler_params=pltpu.CompilerParams(vmem_limit_bytes=24 << 20),
         cost_estimate=pl.CostEstimate(flops=10 ** 9, bytes_accessed=10 ** 7, transcendentals=0),
-        name="inner_density",
-    )(block, lists, own, live)
+        name="inner_density_last" if last else "inner_density",
+    )(flag, block, lists, own, live, *(carried or ()))
 
 
 def outer_step(block, lists, rim_lists, own, live, below, above, pair, part, edge):
@@ -389,7 +409,7 @@
         own = jnp.stack(blocks)
     else:
         me = jnp.int32(0)
-        live, ids, _ = stage(lists, grouped[0][0])
+        live, ids, unused = stage(lists, grouped[0][0])
         own = lax.all_to_all(grouped[0], "region", 0, 0, tiled=True)
     first_block = me.astype(jnp.int32).reshape(1)
     by_field = own.reshape(regions, FIELDS, per_dest, rows)
@@ -408,9 +428,15 @@
 
     up = [(i, (i + 1) % subs) for i in range(subs)]
     down = [(j, i) for i, j in up]
+    first_sub = lax.axis_index("sub") == 0
+    early = first_sub.astype(jnp.int32).reshape(1)
     below = lax.ppermute(rim(False), "sub", up)
-    above = lax.ppermute(rim(True), "sub", down)
-    pair, part, edge = inner_density(first_block, lists, own, live)
+    ends = rim(True)
+    above = lax.ppermute(ends, "sub", [pair for pair in down if pair[0] != 0])
+    carried = inner_density(early, first_block, lists, own, live, None)
+    around = lax.ppermute(ends, "sub", [pair for pair in down if pair[0] == 0])
+    pair, part, edge, *unused = inner_density(1 - early, first_block, lists, own, live, carried)
+    above = jnp.where(lax.axis_index("sub") == subs - 1, around, above)
     count = HALO_TILES * listed
     rim_lists = jnp.concatenate([below[FIELDS * RIM, :count], above[FIELDS * RIM, :count]]).astype(jnp.int32)
     return outer_step(first_block, lists, rim_lists, own, live, below, above, pair, part, edge)

time: 26.5 us -> 30.9 us (1.17)
  starting transfers between devices: 7.76 us -> 12.1 us
  Pallas kernels: 12.8 us -> 12.4 us
    ppermute x1 -> x2, starting transfers between devices: 4.58 us -> 8.87 us  [the longest x1 7.58 us: per_device(): around = lax.ppermute(ends, 'sub', [pair for pair in down if pair[0] == 0])]
    pallas_call x1 -> x2, Pallas kernels: 4.73 us -> 4.39 us  [inner_density(): pl.pallas_call(functools.partial(inner_kernel, last), out_shape=shapes, i...]
  transfers between devices with their start and end apart: 5 -> 6, of which waited for: 3 -> 3; matrix products, arithmetic and copies ran while one was open for 3% -> 2% of each run, Pallas kernels for 20% -> 16%
where the time goes in v3:
time: 30.9 us; the launch traced here: 30.6 us
  Pallas kernels  12.4 us (40%)
  starting transfers between devices  12.1 us (39%)
  waiting for transfers between devices  3.58 us (12%)
  other arithmetic  0.84 us (3%)
  between operations  0.82 us (3%)
  local copies, waits for them, and re-layouts  0.81 us (3%)
    ppermute x1, starting transfers between devices, per_device(): around = lax.ppermute(ends, 'sub', [pair for pair in down if pair[0] == 0])  7.58 us
    pallas_call x1, Pallas kernels, outer_step(): pl.pallas_call(outer_kernel, out_shape=(jax.ShapeDtypeStruct((tile_dev, r...  5.67 us
    pallas_call x2, Pallas kernels, inner_density(): pl.pallas_call(functools.partial(inner_kernel, last), out_shape=shapes, i...  4.39 us
    ppermute x3, starting transfers between devices, per_device(): lax.ppermute(grouped[k], 'region', [(i, i ^ k) for i in range(regions)])  3.18 us
    ppermute x1, waiting for transfers between devices, per_device(): below = lax.ppermute(rim(False), 'sub', up)  2.04 us
    pallas_call x1, Pallas kernels, group_tiles(): pl.pallas_call(functools.partial(group_kernel, pairwise, len(shapes)), ou...  1.75 us
    ppermute x3, waiting for transfers between devices, per_device(): lax.ppermute(grouped[k], 'region', [(i, i ^ k) for i in range(regions)])  1.54 us
    ppermute x1, starting transfers between devices, per_device(): above = lax.ppermute(ends, 'sub', [pair for pair in down if pair[0] != 0])  1.29 us
  transfers between devices with their start and end apart: 6, of which 3 were waited for; matrix products, arithmetic and copies ran while one was open for 2% of the time, Pallas kernels for 16%

profile of v3, /device:TPU:0, one launch (start us, length us, event | category | flops | bytes accessed | tf_op | source)
XLA Modules:
  0.0 30.6 jit_solution(2755582790164723555)
XLA Ops:
  0.6 1.8 %group_tiles.1 = (f32[80,128]{1,0:T(8,128)}, f32[80,128]{1,0:T(8,128)}, f32[80,128]{1,0:T(8,128)}, f32[80,128]{1,0:T(8,128)}) custom-call(s32[64]{0:T(128)} %refs_0_.1, f32[3,64,128]{2,1,0:T(8,128)} %refs_1_.1, f32[64,128]{1,0:T(8,128)} %refs_2_.1, f32[64,128]{1,0:T(8,128)} %refs_3_.1), custom_call_target="tpu_custom_call" | custom-call | tf_op jit(solution)/shard_map/group_tiles/pallas_call | solution.py:75
  2.4 0.6 %collective-permute-start = (f32[80,128]{1,0:T(8,128)}, f32[80,128]{1,0:T(8,128)S(1)}, u32[]{:S(2)}, u32[]{:S(2)}) collective-permute-start(f32[80,128]{1,0:T(8,128)} %get-tuple-element.19), channel_id=1, source_target_pairs={{0,8},{8,0},{16,24},{24,16},{1,9},{9,1},{17,25},{25,17},{2,10},{10... | collective-permute-start | bytes 122888 | tf_op jit(solution)/shard_map/ppermute | solution.py:408
  2.9 2.6 %collective-permute-start.1 = (f32[80,128]{1,0:T(8,128)}, f32[80,128]{1,0:T(8,128)S(1)}, u32[]{:S(2)}, u32[]{:S(2)}) collective-permute-start(f32[80,128]{1,0:T(8,128)} %get-tuple-element.20), channel_id=1, source_target_pairs={{0,16},{8,24},{16,0},{24,8},{1,17},{9,25},{17,1},{25,9},{2,18},{10... | collective-permute-start | bytes 122888 | tf_op jit(solution)/shard_map/ppermute | solution.py:408
  5.5 0.0 collective-permute-start.2
  5.6 0.7 %pad_add_fusion.lists_ref = s32[5,64]{1,0:T(8,128)S(1)} fusion(s32[1,64]{1,0:T(1,128)} %bitcast.53, s32[4,64]{1,0:T(4,128)} %bitcast.52), kind=kLoop, calls=%fused_computation.15 | loop fusion | flops 320 | bytes 2560 | tf_op jit(solution)/shard_map/concatenate | solution.py:400
  6.3 0.0 copy-start
  6.3 0.8 %copy-done = f32[80,128]{1,0:T(8,128)S(1)} copy-done((f32[80,128]{1,0:T(8,128)S(1)}, f32[80,128]{1,0:T(8,128)}, u32[]{:S(2)}) %copy-start) | copy-done | bytes 40984
  7.1 0.6 %stage.1 = (f32[64,128]{1,0:T(8,128)S(1)}, f32[2,8,128]{2,1,0:T(8,128)S(1)}, f32[80,128]{1,0:T(8,128)S(1)}) custom-call(s32[5,64]{1,0:T(8,128)S(1)} %pad_add_fusion.lists_ref, f32[80,128]{1,0:T(8,128)S(1)} %copy-done), custom_call_target="tpu_custom_call" | custom-call | tf_op jit(solution)/shard_map/stage/pallas_call | solution.py:108
  7.7 0.0 collective-permute-done
  7.7 0.2 collective-permute-done.1
  7.9 1.4 %collective-permute-done.2 = f32[80,128]{1,0:T(8,128)S(1)} collective-permute-done((f32[80,128]{1,0:T(8,128)}, f32[80,128]{1,0:T(8,128)S(1)}, u32[]{:S(2)}, u32[]{:S(2)}) %collective-permute-start.2) | collective-permute-done | bytes 40992 | tf_op jit(solution)/shard_map/ppermute | solution.py:408
  9.4 1.3 %collective-permute-start.5 = (f32[48,128]{1,0:T(8,128)S(1)}, f32[48,128]{1,0:T(8,128)S(1)}, u32[]{:S(2)}, u32[]{:S(2)}) collective-permute-start(f32[48,128]{1,0:T(8,128)S(1)} %pad_maximum_fusion.3), channel_id=1, source_target_pairs={{1,0},{2,1},{3,2},{4,3},{5,4},{6,5},{7,6},{9,8},{10,9},{11,10},{12... | collective-permute-start | bytes 73736 | tf_op jit(solution)/shard_map/ppermute | solution.py:435
  10.7 7.6 %collective-permute-start.4 = (f32[48,128]{1,0:T(8,128)S(1)}, f32[48,128]{1,0:T(8,128)S(1)}, u32[]{:S(2)}, u32[]{:S(2)}) collective-permute-start(f32[48,128]{1,0:T(8,128)S(1)} %pad_maximum_fusion.3), channel_id=1, source_target_pairs={{0,7},{8,15},{16,23},{24,31}} | collective-permute-start | bytes 73736 | tf_op jit(solution)/shard_map/ppermute | solution.py:437
  18.3 0.1 collective-permute-start.3
  18.4 3.1 %inner_density.1 = (f32[28,512,256]{2,1,0:T(8,128)S(1)}, f32[448,128]{1,0:T(8,128)S(1)}, bf16[16,128,128]{2,1,0:T(8,128)(2,1)S(1)}, bf16[64,128,128]{2,1,0:T(8,128)(2,1)S(1)}, bf16[28,256,256]{2,1,0:T(8,128)(2,1)S(1)}) custom-call(s32[1]{0:T(128)} %bitcast.23.flag_ref, s32[1]{0:T(128)} %bitcast.block_ref, s32[5,64]{1,0:T(8,128)S(1)} %pad_add_fusion.lists_ref, ...), custom_call_target="tpu_custom_call" | custom-call | flops 1000000000 | bytes 10000000 | tf_op jit(solution)/shard_map/inner_density/pallas_call | solution.py:357
  21.5 1.3 %inner_density_last.1 = (f32[28,512,256]{2,1,0:T(8,128)S(1)}, f32[448,128]{1,0:T(8,128)S(1)}, bf16[16,128,128]{2,1,0:T(8,128)(2,1)S(1)}, bf16[64,128,128]{2,1,0:T(8,128)(2,1)S(1)}, bf16[28,256,256]{2,1,0:T(8,128)(2,1)S(1)}) custom-call(s32[1]{0:T(128)S(6)} %sub.3.flag_ref, ...), custom_call_target="tpu_custom_call", output_to_operand_aliasing={{0}: (5, {}), {1}: (6, {}), {2}: (7, {}), {3}: (8, {}), {4}... | custom-call | flops 1000000000 | bytes 10000000 | tf_op jit(solution)/shard_map/inner_density_last/pallas_call | solution.py:357
  22.8 0.0 collective-permute-done.5
  22.8 0.0 collective-permute-done.4
  22.8 2.0 %collective-permute-done.3.below_ref = f32[48,128]{1,0:T(8,128)S(1)} collective-permute-done((f32[48,128]{1,0:T(8,128)S(1)}, f32[48,128]{1,0:T(8,128)S(1)}, u32[]{:S(2)}, u32[]{:S(2)}) %collective-permute-start.3) | collective-permute-done | bytes 24608 | tf_op jit(solution)/shard_map/ppermute | solution.py:433
  24.9 0.1 maximum_convert_fusion.rim_lists_ref
  24.9 5.7 %outer_step.1 = (f32[64,128]{1,0:T(8,128)}, f32[3,64,128]{2,1,0:T(8,128)}) custom-call(s32[1]{0:T(128)} %bitcast.block_ref, s32[5,64]{1,0:T(8,128)S(1)} %pad_add_fusion.lists_ref, s32[32]{0:T(128)S(1)} %maximum_convert_fusion.rim_lists_ref, f32[4,80,128]{2,1,0:T(8,128)S(1)} %pad_maximum_fusion.1.own_ref, f32[64,128]{1,0:T(8,128)S(1)} %get-tuple-element.22.live_ref, ...), custom_call_target="tpu_custom_call" | custom-call | tf_op jit(solution)/shard_map/outer_step/pallas_call | solution.py:374
  (14 shorter events, 0.1 us)
Async XLA Ops:
  2.4 5.3 %collective-permute-start = (f32[80,128]{1,0:T(8,128)}, f32[80,128]{1,0:T(8,128)S(1)}, u32[]{:S(2)}, u32[]{:S(2)}) collective-permute-start(f32[80,128]{1,0:T(8,128)} %get-tuple-element.19), channel_id=1, source_target_pairs={{0,8},{8,0},{16,24},{24,16},{1,9},{9,1},{17,25},{25,17},{2,10},{10... | collective-permute-start | bytes 122888 | tf_op jit(solution)/shard_map/ppermute | solution.py:408
  2.9 5.0 %collective-permute-start.1 = (f32[80,128]{1,0:T(8,128)}, f32[80,128]{1,0:T(8,128)S(1)}, u32[]{:S(2)}, u32[]{:S(2)}) collective-permute-start(f32[80,128]{1,0:T(8,128)} %get-tuple-element.20), channel_id=1, source_target_pairs={{0,16},{8,24},{16,0},{24,8},{1,17},{9,25},{17,1},{25,9},{2,18},{10... | collective-permute-start | bytes 122888 | tf_op jit(solution)/shard_map/ppermute | solution.py:408
  5.5 3.7 %collective-permute-start.2 = (f32[80,128]{1,0:T(8,128)}, f32[80,128]{1,0:T(8,128)S(1)}, u32[]{:S(2)}, u32[]{:S(2)}) collective-permute-start(f32[80,128]{1,0:T(8,128)} %get-tuple-element.21), channel_id=1, source_target_pairs={{0,24},{8,16},{16,8},{24,0},{1,25},{9,17},{17,9},{25,1},{2,26},{10... | collective-permute-start | bytes 122888 | tf_op jit(solution)/shard_map/ppermute | solution.py:408
  6.3 0.8 %copy-start = (f32[80,128]{1,0:T(8,128)S(1)}, f32[80,128]{1,0:T(8,128)}, u32[]{:S(2)}) copy-start(f32[80,128]{1,0:T(8,128)} %get-tuple-element.17.local_ref) | copy-start | bytes 122884
  9.4 13.4 %collective-permute-start.5 = (f32[48,128]{1,0:T(8,128)S(1)}, f32[48,128]{1,0:T(8,128)S(1)}, u32[]{:S(2)}, u32[]{:S(2)}) collective-permute-start(f32[48,128]{1,0:T(8,128)S(1)} %pad_maximum_fusion.3), channel_id=1, source_target_pairs={{1,0},{2,1},{3,2},{4,3},{5,4},{6,5},{7,6},{9,8},{10,9},{11,10},{12... | collective-permute-start | bytes 73736 | tf_op jit(solution)/shard_map/ppermute | solution.py:435
  10.7 12.1 %collective-permute-start.4 = (f32[48,128]{1,0:T(8,128)S(1)}, f32[48,128]{1,0:T(8,128)S(1)}, u32[]{:S(2)}, u32[]{:S(2)}) collective-permute-start(f32[48,128]{1,0:T(8,128)S(1)} %pad_maximum_fusion.3), channel_id=1, source_target_pairs={{0,7},{8,15},{16,23},{24,31}} | collective-permute-start | bytes 73736 | tf_op jit(solution)/shard_map/ppermute | solution.py:437
  18.3 6.6 %collective-permute-start.3 = (f32[48,128]{1,0:T(8,128)S(1)}, f32[48,128]{1,0:T(8,128)S(1)}, u32[]{:S(2)}, u32[]{:S(2)}) collective-permute-start(f32[48,128]{1,0:T(8,128)S(1)} %pad_maximum_fusion.2), channel_id=1, source_target_pairs={{0,1},{1,2},{2,3},{3,4},{4,5},{5,6},{6,7},{7,0},{8,9},{9,10},{10,1... | collective-permute-start | bytes 73736 | tf_op jit(solution)/shard_map/ppermute | solution.py:433

commit v4 on v3

--- a/solution.py
+++ b/solution.py
@@ -14,6 +14,7 @@
 FIELDS = 5
 UNROLL = 7
 CHUNKS = 4
+EARLY = 2
 EMPTY_LOG = -1024.0
 LOG2E = 1.4426950408889634
 kernel_scale = math.pi ** (-1.5)
@@ -84,27 +85,27 @@
     )(owners, coords, smooth, masses)
 
 
-def stage_kernel(lists_ref, local_ref, live_ref, ids_ref, here_ref):
+def stage_kernel(table_ref, local_ref, live_ref, ids_ref, here_ref):
     tile_dev, rows = live_ref.shape
-    listed = lists_ref.shape[0] - 1
+    listed = table_ref.shape[0] - 2
     lane = lax.broadcasted_iota(jnp.int32, (8, rows), 1)
     row = lax.broadcasted_iota(jnp.int32, (8, rows), 0)
     for t in range(0, tile_dev, 8):
-        limit = jnp.full((8, rows), lists_ref[listed, t])
+        limit = jnp.full((8, rows), table_ref[listed, t])
         for i in range(1, 8):
-            limit = jnp.where(row == i, lists_ref[listed, t + i], limit)
+            limit = jnp.where(row == i, table_ref[listed, t + i], limit)
         live_ref[t:t + 8] = (lane < limit).astype(f32)
     for side, start in enumerate((0, tile_dev - HALO_TILES)):
         ids = jnp.zeros((8, rows), f32)
         for i in range(HALO_TILES):
             for n in range(listed):
-                ids = jnp.where(lane == i * listed + n, lists_ref[n, start + i].astype(f32), ids)
+                ids = jnp.where(lane == i * listed + n, table_ref[n, start + i].astype(f32), ids)
         ids_ref[side] = ids
     here_ref[...] = local_ref[...]
 
 
-def stage(lists, local):
-    tile_dev, rows = lists.shape[1], local.shape[-1]
+def stage(table, local):
+    tile_dev, rows = table.shape[1], local.shape[-1]
     return pl.pallas_call(
         stage_kernel,
         out_shape=(
@@ -116,7 +117,7 @@
         out_specs=(VMEM,) * 3,
         compiler_params=pltpu.CompilerParams(vmem_limit_bytes=4 << 20),
         name="stage",
-    )(lists, local)
+    )(table, local)
 
 
 def parts_of(x, count):
@@ -132,11 +133,11 @@
     return jnp.dot(a, b, preferred_element_type=f32)
 
 
-def own_field(block_ref, own_ref, live_ref, f):
+def own_field(table_ref, own_ref, live_ref, f):
     tile_dev = live_ref.shape[0]
     regions, per_dest = own_ref.shape[0], tile_dev // own_ref.shape[0]
     rows = pl.ds(f * per_dest, per_dest)
-    value = jnp.concatenate([own_ref[block_ref[0] ^ r, rows] for r in range(regions)], axis=0)
+    value = jnp.concatenate([own_ref[table_ref[table_ref.shape[0] - 1, 0] ^ r, rows] for r in range(regions)], axis=0)
     return value * live_ref[...] if f == 4 else value
 
 
@@ -198,10 +199,11 @@
     part_ref[pl.ds(at + 8, 8)] = total[:, rows:]
 
 
-def inner_kernel(last, flag_ref, block_ref, lists_ref, own_ref, live_ref, *refs):
-    pair_ref, part_ref, edge_ref, turned_ref, weights_ref, partner_ref, mine_ref = refs[5:] if last else refs
+def inner_kernel(late, table_ref, own_ref, live_ref, *refs):
+    pair_ref, part_ref, turned_ref, weights_ref = refs[-6 - late:-2 - late]
+    partner_ref, mine_ref = refs[-2:]
     tile_dev = live_ref.shape[0]
-    listed = lists_ref.shape[0] - 1
+    listed = table_ref.shape[0] - 2
     chunk = pair_ref.shape[0] // CHUNKS
     ahead = 2 * chunk + 2 * HALO_TILES
 
@@ -211,49 +213,55 @@
     def weigh(p):
         weights_ref[p] = pair_weights(mine_ref, HALO_TILES + 2 * p)
 
-    def pair(p):
-        t = HALO_TILES + 2 * p
-        partners = [(lists_ref[n, t] - HALO_TILES, lists_ref[n, t + 1] - HALO_TILES) for n in range(listed)]
-        density_pair(turned_ref, weights_ref[p], partners, part_ref, 16 * p, pair_ref.at[p])
-
-    @pl.when(flag_ref[0] == 1)
-    def _():
+    def features():
         pos, live, mass, inverse_sq, _ = field_terms(
-            [own_field(block_ref, own_ref, live_ref, f) for f in range(FIELDS)]
+            [own_field(table_ref, own_ref, live_ref, f) for f in range(FIELDS)]
         )
         put_features(pos, live, mass, inverse_sq, partner_ref, mine_ref)
+
+    def do_chunk(c, more=True):
+        for i in range(chunk):
+            t = HALO_TILES + 2 * (c * chunk + i)
+            partners = [(table_ref[n, t] - HALO_TILES, table_ref[n, t + 1] - HALO_TILES) for n in range(listed)]
+            p = c * chunk + i
+            density_pair(turned_ref, weights_ref[p], partners, part_ref, 16 * p, pair_ref.at[p])
+        if more:
+            for i in range(2 * chunk):
+                turn(c * 2 * chunk + ahead + i)
+            for i in range(chunk):
+                weigh((c + 1) * chunk + i)
+
+    if late:
+        features()
+
+    @pl.when(table_ref[listed + 1, 1] == (0 if late else 1))
+    def _():
+        if not late:
+            features()
         for t in range(ahead):
             turn(t)
         for p in range(chunk):
             weigh(p)
-
-        @pl.loop(0, CHUNKS - 1)
-        def _(c):
-            for i in range(chunk):
-                pair(c * chunk + i)
-            for i in range(2 * chunk):
-                turn(c * 2 * chunk + ahead + i)
-            for i in range(chunk):
-                weigh((c + 1) * chunk + i)
-
+        pl.loop(0, EARLY)(do_chunk)
+
+    if late:
+        edge_ref = refs[-3]
+        pl.loop(EARLY, CHUNKS - 1)(do_chunk)
+        do_chunk(CHUNKS - 1, False)
         edge_ref[:RIM] = turned_ref[:RIM]
         edge_ref[RIM:] = turned_ref[tile_dev - RIM:]
 
-    if last:
-        for i in range(chunk):
-            pair((CHUNKS - 1) * chunk + i)
-
 
 def outer_kernel(
-    block_ref, lists_ref, rim_lists_ref, own_ref, live_ref, below_ref, above_ref, pair_ref, part_ref, edge_ref,
+    table_ref, rim_lists_ref, own_ref, live_ref, below_ref, above_ref, pair_ref, part_ref, edge_ref,
     density_ref, accel_ref, partner_ref, mine_ref, turned_ref, rim_pair_ref, rim_part_ref, coef_ref, coefb_ref, out_ref,
 ):
     tile_dev, rows = live_ref.shape
     ext = tile_dev + 2 * RIM
-    listed = lists_ref.shape[0] - 1
+    listed = table_ref.shape[0] - 2
     fields = [
         jnp.concatenate(
-            [below_ref[f * RIM:(f + 1) * RIM], own_field(block_ref, own_ref, live_ref, f), above_ref[f * RIM:(f + 1) * RIM]], axis=0
+            [below_ref[f * RIM:(f + 1) * RIM], own_field(table_ref, own_ref, live_ref, f), above_ref[f * RIM:(f + 1) * RIM]], axis=0
         )
         for f in range(FIELDS)
     ]
@@ -278,7 +286,7 @@
             if own_side:
                 t = e - RIM if side == 0 else e - 3 * RIM + tile_dev
                 shift = HALO_TILES if side == 0 else HALO_TILES - tile_dev + 2 * RIM
-                partners = [(lists_ref[n, t] + shift, lists_ref[n, t + 1] + shift) for n in range(listed)]
+                partners = [(table_ref[n, t] + shift, table_ref[n, t + 1] + shift) for n in range(listed)]
                 store = rim_pair_ref.at[half * side + i % half]
             else:
                 first = (2 * i if side == 0 else HALO_TILES + 2 * (i - half)) * listed
@@ -313,7 +321,7 @@
     def force_pair(t, pair):
         total = None
         for n in range(listed):
-            e0, e1 = lists_ref[n, t] + HALO_TILES, lists_ref[n, t + 1] + HALO_TILES
+            e0, e1 = table_ref[n, t] + HALO_TILES, table_ref[n, t + 1] + HALO_TILES
             left = jnp.concatenate([coefb_ref[e0], coefb_ref[e1]], axis=0)
             w = pair[n * rows:(n + 1) * rows]
             high = w.astype(bf16)
@@ -342,39 +350,39 @@
         accel_ref[c] = scale * (q_own * (x * sums[0] - sums[1 + c]) + (x * sums[4] - sums[5 + c]))
 
 
-def inner_density(flag, block, lists, own, live, carried):
+def inner_density(table, own, live, carried=()):
     tile_dev, rows = live.shape
-    listed = lists.shape[0] - 1
+    listed = table.shape[0] - 2
     count = (tile_dev - RIM) // 2
-    last = carried is not None
-    shapes = (
+    late = len(carried) > 0
+    shapes = [
         jax.ShapeDtypeStruct((count, listed * rows, 2 * rows), f32),
         jax.ShapeDtypeStruct((16 * count, rows), f32),
-        jax.ShapeDtypeStruct((2 * RIM, rows, rows), bf16),
         jax.ShapeDtypeStruct((tile_dev, rows, rows), bf16),
         jax.ShapeDtypeStruct((count, 2 * rows, 2 * rows), bf16),
-    )
+    ]
+    edges = [jax.ShapeDtypeStruct((2 * RIM, rows, rows), bf16)] if late else []
     return pl.pallas_call(
-        functools.partial(inner_kernel, last),
-        out_shape=shapes,
-        in_specs=[SMEM] * 3 + [VMEM] * (7 if last else 2),
-        out_specs=(VMEM,) * 5,
-        input_output_aliases={5 + i: i for i in range(5)} if last else {},
+        functools.partial(inner_kernel, late),
+        out_shape=shapes + edges,
+        in_specs=[SMEM] + [VMEM] * (2 + len(carried)),
+        out_specs=[VMEM] * len(shapes + edges),
+        input_output_aliases={3 + i: i for i in range(len(carried))},
         scratch_shapes=[pltpu.VMEM((8 * tile_dev, rows), f32), pltpu.VMEM((8 * tile_dev, rows), f32)],
         compiler_params=pltpu.CompilerParams(vmem_limit_bytes=24 << 20),
         cost_estimate=pl.CostEstimate(flops=10 ** 9, bytes_accessed=10 ** 7, transcendentals=0),
-        name="inner_density_last" if last else "inner_density",
-    )(flag, block, lists, own, live, *(carried or ()))
-
-
-def outer_step(block, lists, rim_lists, own, live, below, above, pair, part, edge):
+        name="inner_late" if late else "inner_early",
+    )(table, own, live, *carried)
+
+
+def outer_step(table, rim_lists, own, live, below, above, pair, part, edge):
     tile_dev, rows = live.shape
     ext = tile_dev + 2 * RIM
-    listed = lists.shape[0] - 1
+    listed = table.shape[0] - 2
     return pl.pallas_call(
         outer_kernel,
         out_shape=(jax.ShapeDtypeStruct((tile_dev, rows), f32), jax.ShapeDtypeStruct((3, tile_dev, rows), f32)),
-        in_specs=[SMEM] * 3 + [VMEM] * 7,
+        in_specs=[SMEM] * 2 + [VMEM] * 7,
         out_specs=(VMEM, VMEM),
         scratch_shapes=[
             pltpu.VMEM((8 * 4 * RIM, rows), f32),
@@ -388,7 +396,7 @@
         ],
         compiler_params=pltpu.CompilerParams(vmem_limit_bytes=24 << 20),
         name="outer_step",
-    )(block, lists, rim_lists, own, live, below, above, pair, part, edge)
+    )(table, rim_lists, own, live, below, above, pair, part, edge)
 
 
 def per_device(coords, smooth, masses, owners, counts, neighbours):
@@ -397,21 +405,22 @@
     subs = lax.axis_size("sub")
     per_dest = tile_dev // regions
     listed = neighbours.shape[1]
-    lists = jnp.concatenate([neighbours.T, counts[None]], axis=0)
+    early = (lax.axis_index("sub") == 0).astype(jnp.int32)
     pairwise = regions <= 4 and regions & (regions - 1) == 0
     grouped = group_tiles(coords, smooth, masses, owners, regions, pairwise)
+    me = lax.axis_index("region") if pairwise else jnp.int32(0)
+    slot = jnp.arange(tile_dev, dtype=jnp.int32)
+    scalars = jnp.where(slot == 0, me, jnp.where(slot == 1, early, 0))
+    table = jnp.concatenate([neighbours.T, counts[None], scalars[None]], axis=0)
     if pairwise:
-        me = lax.axis_index("region")
-        live, ids, local = stage(lists, grouped[0])
+        live, ids, local = stage(table, grouped[0])
         blocks = [local]
         for k in range(1, regions):
             blocks.append(lax.ppermute(grouped[k], "region", [(i, i ^ k) for i in range(regions)]))
         own = jnp.stack(blocks)
     else:
-        me = jnp.int32(0)
-        live, ids, unused = stage(lists, grouped[0][0])
+        live, ids, _ = stage(table, grouped[0][0])
         own = lax.all_to_all(grouped[0], "region", 0, 0, tiled=True)
-    first_block = me.astype(jnp.int32).reshape(1)
     by_field = own.reshape(regions, FIELDS, per_dest, rows)
 
     def rim(first):
@@ -428,18 +437,13 @@
 
     up = [(i, (i + 1) % subs) for i in range(subs)]
     down = [(j, i) for i, j in up]
-    first_sub = lax.axis_index("sub") == 0
-    early = first_sub.astype(jnp.int32).reshape(1)
     below = lax.ppermute(rim(False), "sub", up)
-    ends = rim(True)
-    above = lax.ppermute(ends, "sub", [pair for pair in down if pair[0] != 0])
-    carried = inner_density(early, first_block, lists, own, live, None)
-    around = lax.ppermute(ends, "sub", [pair for pair in down if pair[0] == 0])
-    pair, part, edge, *unused = inner_density(1 - early, first_block, lists, own, live, carried)
-    above = jnp.where(lax.axis_index("sub") == subs - 1, around, above)
+    carried = inner_density(table, own, live)
+    above = lax.ppermute(rim(True), "sub", down)
+    pair, part, _, _, edge = inner_density(table, own, live, carried)
     count = HALO_TILES * listed
     rim_lists = jnp.concatenate([below[FIELDS * RIM, :count], above[FIELDS * RIM, :count]]).astype(jnp.int32)
-    return outer_step(first_block, lists, rim_lists, own, live, below, above, pair, part, edge)
+    return outer_step(table, rim_lists, own, live, below, above, pair, part, edge)
 
 
 def solution(mesh):

time: 30.9 us -> 26.5 us (0.86)
  starting transfers between devices: 12.1 us -> 7.76 us
    ppermute x2 -> x1, starting transfers between devices: 8.87 us -> 4.58 us  [per_device(): above = lax.ppermute(rim(True), 'sub', down)]
  transfers between devices with their start and end apart: 6 -> 5, of which waited for: 3 -> 3; matrix products, arithmetic and copies ran while one was open for 2% -> 3% of each run, Pallas kernels for 16% -> 19%
where the time goes in v4:
time: 26.5 us; the launch traced here: 26.3 us
  Pallas kernels  12.4 us (47%)
  starting transfers between devices  7.76 us (29%)
  waiting for transfers between devices  3.66 us (14%)
  other arithmetic  0.84 us (3%)
  local copies, waits for them, and re-layouts  0.81 us (3%)
  between operations  0.77 us (3%)
    pallas_call x1, Pallas kernels, outer_step(): pl.pallas_call(outer_kernel, out_shape=(jax.ShapeDtypeStruct((tile_dev, r...  5.67 us
    ppermute x1, starting transfers between devices, per_device(): above = lax.ppermute(rim(True), 'sub', down)  4.58 us
    pallas_call x2, Pallas kernels, inner_density(): pl.pallas_call(functools.partial(inner_kernel, late), out_shape=shapes +...  4.34 us
    ppermute x3, starting transfers between devices, per_device(): lax.ppermute(grouped[k], 'region', [(i, i ^ k) for i in range(regions)])  3.18 us
    ppermute x1, waiting for transfers between devices, per_device(): below = lax.ppermute(rim(False), 'sub', up)  2.12 us
    pallas_call x1, Pallas kernels, group_tiles(): pl.pallas_call(functools.partial(group_kernel, pairwise, len(shapes)), ou...  1.77 us
    ppermute x3, waiting for transfers between devices, per_device(): lax.ppermute(grouped[k], 'region', [(i, i ^ k) for i in range(regions)])  1.54 us
    unnamed x2, local copies, waits for them, and re-layouts  0.78 us
  transfers between devices with their start and end apart: 5, of which 3 were waited for; matrix products, arithmetic and copies ran while one was open for 3% of the time, Pallas kernels for 19%

profile of v4, /device:TPU:0, one launch (start us, length us, event | category | flops | bytes accessed | tf_op | source)
XLA Modules:
  0.0 26.3 jit_solution(9098328823269708817)
XLA Ops:
  0.6 1.8 %group_tiles.1 = (f32[80,128]{1,0:T(8,128)}, f32[80,128]{1,0:T(8,128)}, f32[80,128]{1,0:T(8,128)}, f32[80,128]{1,0:T(8,128)}) custom-call(s32[64]{0:T(128)} %refs_0_.1, f32[3,64,128]{2,1,0:T(8,128)} %refs_1_.1, f32[64,128]{1,0:T(8,128)} %refs_2_.1, f32[64,128]{1,0:T(8,128)} %refs_3_.1), custom_call_target="tpu_custom_call" | custom-call | tf_op jit(solution)/shard_map/group_tiles/pallas_call | solution.py:76
  2.4 0.6 %collective-permute-start = (f32[80,128]{1,0:T(8,128)}, f32[80,128]{1,0:T(8,128)S(1)}, u32[]{:S(2)}, u32[]{:S(2)}) collective-permute-start(f32[80,128]{1,0:T(8,128)} %get-tuple-element.18), channel_id=1, source_target_pairs={{0,8},{8,0},{16,24},{24,16},{1,9},{9,1},{17,25},{25,17},{2,10},{10... | collective-permute-start | bytes 122888 | tf_op jit(solution)/shard_map/ppermute | solution.py:419
  3.0 2.6 %collective-permute-start.1 = (f32[80,128]{1,0:T(8,128)}, f32[80,128]{1,0:T(8,128)S(1)}, u32[]{:S(2)}, u32[]{:S(2)}) collective-permute-start(f32[80,128]{1,0:T(8,128)} %get-tuple-element.19), channel_id=1, source_target_pairs={{0,16},{8,24},{16,0},{24,8},{1,17},{9,25},{17,1},{25,9},{2,18},{10... | collective-permute-start | bytes 122888 | tf_op jit(solution)/shard_map/ppermute | solution.py:419
  5.5 0.0 collective-permute-start.2
  5.6 0.7 %pad_add_fusion.table_ref = s32[6,64]{1,0:T(8,128)S(1)} fusion(s32[1,64]{1,0:T(1,128)S(1)} %compare_select_fusion.1, s32[1,64]{1,0:T(1,128)} %bitcast.51, s32[4,64]{1,0:T(4,128)} %bitcast.50), kind=kLoop, calls=%fused_computation.14 | loop fusion | flops 768 | bytes 3072 | tf_op jit(solution)/shard_map/concatenate | solution.py:414
  6.3 0.0 copy-start
  6.3 0.8 %copy-done = f32[80,128]{1,0:T(8,128)S(1)} copy-done((f32[80,128]{1,0:T(8,128)S(1)}, f32[80,128]{1,0:T(8,128)}, u32[]{:S(2)}) %copy-start) | copy-done | bytes 40984
  7.1 0.6 %stage.1 = (f32[64,128]{1,0:T(8,128)S(1)}, f32[2,8,128]{2,1,0:T(8,128)S(1)}, f32[80,128]{1,0:T(8,128)S(1)}) custom-call(s32[6,64]{1,0:T(8,128)S(1)} %pad_add_fusion.table_ref, f32[80,128]{1,0:T(8,128)S(1)} %copy-done), custom_call_target="tpu_custom_call" | custom-call | tf_op jit(solution)/shard_map/stage/pallas_call | solution.py:109
  7.7 0.0 collective-permute-done
  7.7 0.2 collective-permute-done.1
  7.9 1.4 %collective-permute-done.2 = f32[80,128]{1,0:T(8,128)S(1)} collective-permute-done((f32[80,128]{1,0:T(8,128)}, f32[80,128]{1,0:T(8,128)S(1)}, u32[]{:S(2)}, u32[]{:S(2)}) %collective-permute-start.2) | collective-permute-done | bytes 40992 | tf_op jit(solution)/shard_map/ppermute | solution.py:419
  9.4 4.6 %collective-permute-start.4 = (f32[48,128]{1,0:T(8,128)S(1)}, f32[48,128]{1,0:T(8,128)S(1)}, u32[]{:S(2)}, u32[]{:S(2)}) collective-permute-start(f32[48,128]{1,0:T(8,128)S(1)} %pad_maximum_fusion.3), channel_id=1, source_target_pairs={{1,0},{2,1},{3,2},{4,3},{5,4},{6,5},{7,6},{0,7},{9,8},{10,9},{11,1... | collective-permute-start | bytes 73736 | tf_op jit(solution)/shard_map/ppermute | solution.py:442
  14.0 0.0 collective-permute-start.3
  14.0 2.4 %inner_early.1 = (f32[28,512,256]{2,1,0:T(8,128)S(1)}, f32[448,128]{1,0:T(8,128)S(1)}, bf16[64,128,128]{2,1,0:T(8,128)(2,1)S(1)}, bf16[28,256,256]{2,1,0:T(8,128)(2,1)S(1)}) custom-call(s32[6,64]{1,0:T(8,128)S(1)} %pad_add_fusion.table_ref, f32[4,80,128]{2,1,0:T(8,128)S(1)} %pad_maximum_fusion.1.own_ref, f32[64,128]{1,0:T(8,128)S(1)} %get-tuple-element.21.live_ref), custom_call_target="tpu_custom_call" | custom-call | flops 1000000000 | bytes 10000000 | tf_op jit(solution)/shard_map/inner_early/pallas_call | solution.py:365
  16.4 2.0 %inner_late.1 = (f32[28,512,256]{2,1,0:T(8,128)S(1)}, f32[448,128]{1,0:T(8,128)S(1)}, bf16[64,128,128]{2,1,0:T(8,128)(2,1)S(1)}, bf16[28,256,256]{2,1,0:T(8,128)(2,1)S(1)}, bf16[16,128,128]{2,1,0:T(8,128)(2,1)S(1)}) custom-call(s32[6,64]{1,0:T(8,128)S(1)} %pad_add_fusion.table_ref, ...), custom_call_target="tpu_custom_call", output_to_operand_aliasing={{0}: (3, {}), {1}: (4, {}), {2}: (5, {}), {3}: (6, {})} | custom-call | flops 1000000000 | bytes 10000000 | tf_op jit(solution)/shard_map/inner_late/pallas_call | solution.py:365
  18.4 0.0 collective-permute-done.4.above_ref
  18.4 2.1 %collective-permute-done.3.below_ref = f32[48,128]{1,0:T(8,128)S(1)} collective-permute-done((f32[48,128]{1,0:T(8,128)S(1)}, f32[48,128]{1,0:T(8,128)S(1)}, u32[]{:S(2)}, u32[]{:S(2)}) %collective-permute-start.3) | collective-permute-done | bytes 24608 | tf_op jit(solution)/shard_map/ppermute | solution.py:440
  20.5 0.1 maximum_convert_fusion.rim_lists_ref
  20.6 5.7 %outer_step.1 = (f32[64,128]{1,0:T(8,128)}, f32[3,64,128]{2,1,0:T(8,128)}) custom-call(s32[6,64]{1,0:T(8,128)S(1)} %pad_add_fusion.table_ref, s32[32]{0:T(128)S(1)} %maximum_convert_fusion.rim_lists_ref, f32[4,80,128]{2,1,0:T(8,128)S(1)} %pad_maximum_fusion.1.own_ref, f32[64,128]{1,0:T(8,128)S(1)} %get-tuple-element.21.live_ref, ...), custom_call_target="tpu_custom_call" | custom-call | tf_op jit(solution)/shard_map/outer_step/pallas_call | solution.py:382
  (14 shorter events, 0.1 us)
Async XLA Ops:
  2.4 5.3 %collective-permute-start = (f32[80,128]{1,0:T(8,128)}, f32[80,128]{1,0:T(8,128)S(1)}, u32[]{:S(2)}, u32[]{:S(2)}) collective-permute-start(f32[80,128]{1,0:T(8,128)} %get-tuple-element.18), channel_id=1, source_target_pairs={{0,8},{8,0},{16,24},{24,16},{1,9},{9,1},{17,25},{25,17},{2,10},{10... | collective-permute-start | bytes 122888 | tf_op jit(solution)/shard_map/ppermute | solution.py:419
  3.0 5.0 %collective-permute-start.1 = (f32[80,128]{1,0:T(8,128)}, f32[80,128]{1,0:T(8,128)S(1)}, u32[]{:S(2)}, u32[]{:S(2)}) collective-permute-start(f32[80,128]{1,0:T(8,128)} %get-tuple-element.19), channel_id=1, source_target_pairs={{0,16},{8,24},{16,0},{24,8},{1,17},{9,25},{17,1},{25,9},{2,18},{10... | collective-permute-start | bytes 122888 | tf_op jit(solution)/shard_map/ppermute | solution.py:419
  5.5 3.7 %collective-permute-start.2 = (f32[80,128]{1,0:T(8,128)}, f32[80,128]{1,0:T(8,128)S(1)}, u32[]{:S(2)}, u32[]{:S(2)}) collective-permute-start(f32[80,128]{1,0:T(8,128)} %get-tuple-element.20), channel_id=1, source_target_pairs={{0,24},{8,16},{16,8},{24,0},{1,25},{9,17},{17,9},{25,1},{2,26},{10... | collective-permute-start | bytes 122888 | tf_op jit(solution)/shard_map/ppermute | solution.py:419
  6.3 0.8 %copy-start = (f32[80,128]{1,0:T(8,128)S(1)}, f32[80,128]{1,0:T(8,128)}, u32[]{:S(2)}) copy-start(f32[80,128]{1,0:T(8,128)} %get-tuple-element.16.local_ref) | copy-start | bytes 122884
  9.4 9.0 %collective-permute-start.4 = (f32[48,128]{1,0:T(8,128)S(1)}, f32[48,128]{1,0:T(8,128)S(1)}, u32[]{:S(2)}, u32[]{:S(2)}) collective-permute-start(f32[48,128]{1,0:T(8,128)S(1)} %pad_maximum_fusion.3), channel_id=1, source_target_pairs={{1,0},{2,1},{3,2},{4,3},{5,4},{6,5},{7,6},{0,7},{9,8},{10,9},{11,1... | collective-permute-start | bytes 73736 | tf_op jit(solution)/shard_map/ppermute | solution.py:442
  14.0 6.5 %collective-permute-start.3 = (f32[48,128]{1,0:T(8,128)S(1)}, f32[48,128]{1,0:T(8,128)S(1)}, u32[]{:S(2)}, u32[]{:S(2)}) collective-permute-start(f32[48,128]{1,0:T(8,128)S(1)} %pad_maximum_fusion.2), channel_id=1, source_target_pairs={{0,1},{1,2},{2,3},{3,4},{4,5},{5,6},{6,7},{7,0},{8,9},{9,10},{10,1... | collective-permute-start | bytes 73736 | tf_op jit(solution)/shard_map/ppermute | solution.py:440

commit v5 on v4

--- a/solution.py
+++ b/solution.py
@@ -14,7 +14,6 @@
 FIELDS = 5
 UNROLL = 7
 CHUNKS = 4
-EARLY = 2
 EMPTY_LOG = -1024.0
 LOG2E = 1.4426950408889634
 kernel_scale = math.pi ** (-1.5)
@@ -231,25 +230,29 @@
             for i in range(chunk):
                 weigh((c + 1) * chunk + i)
 
-    if late:
+    early = table_ref[listed + 1, 1]
+
+    def begin():
         features()
-
-    @pl.when(table_ref[listed + 1, 1] == (0 if late else 1))
-    def _():
-        if not late:
-            features()
         for t in range(ahead):
             turn(t)
         for p in range(chunk):
             weigh(p)
-        pl.loop(0, EARLY)(do_chunk)
 
     if late:
+        pl.when(early > 0)(features)
+        pl.when(early == 0)(begin)
         edge_ref = refs[-3]
-        pl.loop(EARLY, CHUNKS - 1)(do_chunk)
+        pl.loop(early, CHUNKS - 1)(do_chunk)
         do_chunk(CHUNKS - 1, False)
         edge_ref[:RIM] = turned_ref[:RIM]
         edge_ref[RIM:] = turned_ref[tile_dev - RIM:]
+    else:
+
+        @pl.when(early > 0)
+        def _():
+            begin()
+            pl.loop(0, early)(do_chunk)
 
 
 def outer_kernel(
@@ -405,7 +408,7 @@
     subs = lax.axis_size("sub")
     per_dest = tile_dev // regions
     listed = neighbours.shape[1]
-    early = (lax.axis_index("sub") == 0).astype(jnp.int32)
+    early = jnp.maximum(CHUNKS - 1 - lax.axis_index("sub"), 0).astype(jnp.int32)
     pairwise = regions <= 4 and regions & (regions - 1) == 0
     grouped = group_tiles(coords, smooth, masses, owners, regions, pairwise)
     me = lax.axis_index("region") if pairwise else jnp.int32(0)

time: 26.5 us -> 26.5 us (level)
  no operation moved by 1% of the time
where the time goes in v5:
time: 26.5 us; the launch traced here: 26.3 us
  Pallas kernels  12.5 us (47%)
  starting transfers between devices  7.76 us (29%)
  waiting for transfers between devices  3.58 us (14%)
  other arithmetic  0.84 us (3%)
  local copies, waits for them, and re-layouts  0.81 us (3%)
  between operations  0.77 us (3%)
    pallas_call x1, Pallas kernels, outer_step(): pl.pallas_call(outer_kernel, out_shape=(jax.ShapeDtypeStruct((tile_dev, r...  5.67 us
    ppermute x1, starting transfers between devices, per_device(): above = lax.ppermute(rim(True), 'sub', down)  4.58 us
    pallas_call x2, Pallas kernels, inner_density(): pl.pallas_call(functools.partial(inner_kernel, late), out_shape=shapes +...  4.42 us
    ppermute x3, starting transfers between devices, per_device(): lax.ppermute(grouped[k], 'region', [(i, i ^ k) for i in range(regions)])  3.18 us
    ppermute x1, waiting for transfers between devices, per_device(): below = lax.ppermute(rim(False), 'sub', up)  2.04 us
    pallas_call x1, Pallas kernels, group_tiles(): pl.pallas_call(functools.partial(group_kernel, pairwise, len(shapes)), ou...  1.77 us
    ppermute x3, waiting for transfers between devices, per_device(): lax.ppermute(grouped[k], 'region', [(i, i ^ k) for i in range(regions)])  1.54 us
    unnamed x2, local copies, waits for them, and re-layouts  0.78 us
  transfers between devices with their start and end apart: 5, of which 3 were waited for; matrix products, arithmetic and copies ran while one was open for 3% of the time, Pallas kernels for 19%

profile of v5, /device:TPU:0, one launch (start us, length us, event | category | flops | bytes accessed | tf_op | source)
XLA Modules:
  0.0 26.3 jit_solution(13788045101791394378)
XLA Ops:
  0.6 1.8 %group_tiles.1 = (f32[80,128]{1,0:T(8,128)}, f32[80,128]{1,0:T(8,128)}, f32[80,128]{1,0:T(8,128)}, f32[80,128]{1,0:T(8,128)}) custom-call(s32[64]{0:T(128)} %refs_0_.1, f32[3,64,128]{2,1,0:T(8,128)} %refs_1_.1, f32[64,128]{1,0:T(8,128)} %refs_2_.1, f32[64,128]{1,0:T(8,128)} %refs_3_.1), custom_call_target="tpu_custom_call" | custom-call | tf_op jit(solution)/shard_map/group_tiles/pallas_call | solution.py:75
  2.4 0.6 %collective-permute-start = (f32[80,128]{1,0:T(8,128)}, f32[80,128]{1,0:T(8,128)S(1)}, u32[]{:S(2)}, u32[]{:S(2)}) collective-permute-start(f32[80,128]{1,0:T(8,128)} %get-tuple-element.18), channel_id=1, source_target_pairs={{0,8},{8,0},{16,24},{24,16},{1,9},{9,1},{17,25},{25,17},{2,10},{10... | collective-permute-start | bytes 122888 | tf_op jit(solution)/shard_map/ppermute | solution.py:422
  3.0 2.6 %collective-permute-start.1 = (f32[80,128]{1,0:T(8,128)}, f32[80,128]{1,0:T(8,128)S(1)}, u32[]{:S(2)}, u32[]{:S(2)}) collective-permute-start(f32[80,128]{1,0:T(8,128)} %get-tuple-element.19), channel_id=1, source_target_pairs={{0,16},{8,24},{16,0},{24,8},{1,17},{9,25},{17,1},{25,9},{2,18},{10... | collective-permute-start | bytes 122888 | tf_op jit(solution)/shard_map/ppermute | solution.py:422
  5.5 0.0 collective-permute-start.2
  5.6 0.7 %pad_add_fusion.table_ref = s32[6,64]{1,0:T(8,128)S(1)} fusion(s32[1,64]{1,0:T(1,128)S(1)} %compare_select_fusion.1, s32[1,64]{1,0:T(1,128)} %bitcast.51, s32[4,64]{1,0:T(4,128)} %bitcast.50), kind=kLoop, calls=%fused_computation.14 | loop fusion | flops 768 | bytes 3072 | tf_op jit(solution)/shard_map/concatenate | solution.py:417
  6.3 0.0 copy-start
  6.3 0.8 %copy-done = f32[80,128]{1,0:T(8,128)S(1)} copy-done((f32[80,128]{1,0:T(8,128)S(1)}, f32[80,128]{1,0:T(8,128)}, u32[]{:S(2)}) %copy-start) | copy-done | bytes 40984
  7.1 0.6 %stage.1 = (f32[64,128]{1,0:T(8,128)S(1)}, f32[2,8,128]{2,1,0:T(8,128)S(1)}, f32[80,128]{1,0:T(8,128)S(1)}) custom-call(s32[6,64]{1,0:T(8,128)S(1)} %pad_add_fusion.table_ref, f32[80,128]{1,0:T(8,128)S(1)} %copy-done), custom_call_target="tpu_custom_call" | custom-call | tf_op jit(solution)/shard_map/stage/pallas_call | solution.py:108
  7.7 0.0 collective-permute-done
  7.7 0.2 collective-permute-done.1
  7.9 1.4 %collective-permute-done.2 = f32[80,128]{1,0:T(8,128)S(1)} collective-permute-done((f32[80,128]{1,0:T(8,128)}, f32[80,128]{1,0:T(8,128)S(1)}, u32[]{:S(2)}, u32[]{:S(2)}) %collective-permute-start.2) | collective-permute-done | bytes 40992 | tf_op jit(solution)/shard_map/ppermute | solution.py:422
  9.4 4.6 %collective-permute-start.4 = (f32[48,128]{1,0:T(8,128)S(1)}, f32[48,128]{1,0:T(8,128)S(1)}, u32[]{:S(2)}, u32[]{:S(2)}) collective-permute-start(f32[48,128]{1,0:T(8,128)S(1)} %pad_maximum_fusion.3), channel_id=1, source_target_pairs={{1,0},{2,1},{3,2},{4,3},{5,4},{6,5},{7,6},{0,7},{9,8},{10,9},{11,1... | collective-permute-start | bytes 73736 | tf_op jit(solution)/shard_map/ppermute | solution.py:445
  14.0 0.0 collective-permute-start.3
  14.0 3.1 %inner_early.1 = (f32[28,512,256]{2,1,0:T(8,128)S(1)}, f32[448,128]{1,0:T(8,128)S(1)}, bf16[64,128,128]{2,1,0:T(8,128)(2,1)S(1)}, bf16[28,256,256]{2,1,0:T(8,128)(2,1)S(1)}) custom-call(s32[6,64]{1,0:T(8,128)S(1)} %pad_add_fusion.table_ref, f32[4,80,128]{2,1,0:T(8,128)S(1)} %pad_maximum_fusion.1.own_ref, f32[64,128]{1,0:T(8,128)S(1)} %get-tuple-element.21.live_ref), custom_call_target="tpu_custom_call" | custom-call | flops 1000000000 | bytes 10000000 | tf_op jit(solution)/shard_map/inner_early/pallas_call | solution.py:368
  17.1 1.3 %inner_late.1 = (f32[28,512,256]{2,1,0:T(8,128)S(1)}, f32[448,128]{1,0:T(8,128)S(1)}, bf16[64,128,128]{2,1,0:T(8,128)(2,1)S(1)}, bf16[28,256,256]{2,1,0:T(8,128)(2,1)S(1)}, bf16[16,128,128]{2,1,0:T(8,128)(2,1)S(1)}) custom-call(s32[6,64]{1,0:T(8,128)S(1)} %pad_add_fusion.table_ref, ...), custom_call_target="tpu_custom_call", output_to_operand_aliasing={{0}: (3, {}), {1}: (4, {}), {2}: (5, {}), {3}: (6, {})} | custom-call | flops 1000000000 | bytes 10000000 | tf_op jit(solution)/shard_map/inner_late/pallas_call | solution.py:368
  18.4 0.0 collective-permute-done.4.above_ref
  18.5 2.0 %collective-permute-done.3.below_ref = f32[48,128]{1,0:T(8,128)S(1)} collective-permute-done((f32[48,128]{1,0:T(8,128)S(1)}, f32[48,128]{1,0:T(8,128)S(1)}, u32[]{:S(2)}, u32[]{:S(2)}) %collective-permute-start.3) | collective-permute-done | bytes 24608 | tf_op jit(solution)/shard_map/ppermute | solution.py:443
  20.5 0.1 maximum_convert_fusion.rim_lists_ref
  20.6 5.7 %outer_step.1 = (f32[64,128]{1,0:T(8,128)}, f32[3,64,128]{2,1,0:T(8,128)}) custom-call(s32[6,64]{1,0:T(8,128)S(1)} %pad_add_fusion.table_ref, s32[32]{0:T(128)S(1)} %maximum_convert_fusion.rim_lists_ref, f32[4,80,128]{2,1,0:T(8,128)S(1)} %pad_maximum_fusion.1.own_ref, f32[64,128]{1,0:T(8,128)S(1)} %get-tuple-element.21.live_ref, ...), custom_call_target="tpu_custom_call" | custom-call | tf_op jit(solution)/shard_map/outer_step/pallas_call | solution.py:385
  (14 shorter events, 0.1 us)
Async XLA Ops:
  2.4 5.3 %collective-permute-start = (f32[80,128]{1,0:T(8,128)}, f32[80,128]{1,0:T(8,128)S(1)}, u32[]{:S(2)}, u32[]{:S(2)}) collective-permute-start(f32[80,128]{1,0:T(8,128)} %get-tuple-element.18), channel_id=1, source_target_pairs={{0,8},{8,0},{16,24},{24,16},{1,9},{9,1},{17,25},{25,17},{2,10},{10... | collective-permute-start | bytes 122888 | tf_op jit(solution)/shard_map/ppermute | solution.py:422
  3.0 5.0 %collective-permute-start.1 = (f32[80,128]{1,0:T(8,128)}, f32[80,128]{1,0:T(8,128)S(1)}, u32[]{:S(2)}, u32[]{:S(2)}) collective-permute-start(f32[80,128]{1,0:T(8,128)} %get-tuple-element.19), channel_id=1, source_target_pairs={{0,16},{8,24},{16,0},{24,8},{1,17},{9,25},{17,1},{25,9},{2,18},{10... | collective-permute-start | bytes 122888 | tf_op jit(solution)/shard_map/ppermute | solution.py:422
  5.5 3.7 %collective-permute-start.2 = (f32[80,128]{1,0:T(8,128)}, f32[80,128]{1,0:T(8,128)S(1)}, u32[]{:S(2)}, u32[]{:S(2)}) collective-permute-start(f32[80,128]{1,0:T(8,128)} %get-tuple-element.20), channel_id=1, source_target_pairs={{0,24},{8,16},{16,8},{24,0},{1,25},{9,17},{17,9},{25,1},{2,26},{10... | collective-permute-start | bytes 122888 | tf_op jit(solution)/shard_map/ppermute | solution.py:422
  6.3 0.8 %copy-start = (f32[80,128]{1,0:T(8,128)S(1)}, f32[80,128]{1,0:T(8,128)}, u32[]{:S(2)}) copy-start(f32[80,128]{1,0:T(8,128)} %get-tuple-element.16.local_ref) | copy-start | bytes 122884
  9.4 9.1 %collective-permute-start.4 = (f32[48,128]{1,0:T(8,128)S(1)}, f32[48,128]{1,0:T(8,128)S(1)}, u32[]{:S(2)}, u32[]{:S(2)}) collective-permute-start(f32[48,128]{1,0:T(8,128)S(1)} %pad_maximum_fusion.3), channel_id=1, source_target_pairs={{1,0},{2,1},{3,2},{4,3},{5,4},{6,5},{7,6},{0,7},{9,8},{10,9},{11,1... | collective-permute-start | bytes 73736 | tf_op jit(solution)/shard_map/ppermute | solution.py:445
  14.0 6.5 %collective-permute-start.3 = (f32[48,128]{1,0:T(8,128)S(1)}, f32[48,128]{1,0:T(8,128)S(1)}, u32[]{:S(2)}, u32[]{:S(2)}) collective-permute-start(f32[48,128]{1,0:T(8,128)S(1)} %pad_maximum_fusion.2), channel_id=1, source_target_pairs={{0,1},{1,2},{2,3},{3,4},{4,5},{5,6},{6,7},{7,0},{8,9},{9,10},{10,1... | collective-permute-start | bytes 73736 | tf_op jit(solution)/shard_map/ppermute | solution.py:443

commit v6 on v5

--- a/solution.py
+++ b/solution.py
@@ -12,7 +12,6 @@
 HALO_TILES = 4
 RIM = 2 * HALO_TILES
 FIELDS = 5
-UNROLL = 7
 CHUNKS = 4
 EMPTY_LOG = -1024.0
 LOG2E = 1.4426950408889634
@@ -198,9 +197,37 @@
     part_ref[pl.ds(at + 8, 8)] = total[:, rows:]
 
 
+def pressure(raw, live):
+    return jnp.where(live, jnp.exp2(jnp.log2(jnp.where(live, raw, 1.0)) * (-1.0 / 3.0)), 0.0)
+
+
+def put_coefficients(ref, pos, q):
+    put_rows(ref, [jnp.ones_like(q)] + pos + [q] + [q * x for x in pos])
+
+
+def narrow(narrow_ref, ref, e):
+    narrow_ref[e] = jnp.concatenate(parts_of(tile_of(ref, e), 2), axis=0).astype(bf16)
+
+
+def force_pair(narrow_ref, partners, pair, out_ref, at):
+    rows = pair.shape[1] // 2
+    total = None
+    for n, (e0, e1) in enumerate(partners):
+        left = jnp.concatenate([narrow_ref[e0], narrow_ref[e1]], axis=0)
+        w = pair[n * rows:(n + 1) * rows]
+        high = w.astype(bf16)
+        part = dot(left, high) + dot(left, (w - high.astype(f32)).astype(bf16))
+        total = part if total is None else total + part
+    out_ref[pl.ds(at, 8)] = total[:8, :rows] + total[8:16, :rows]
+    out_ref[pl.ds(at + 8, 8)] = total[16:24, rows:] + total[24:, rows:]
+
+
 def inner_kernel(late, table_ref, own_ref, live_ref, *refs):
-    pair_ref, part_ref, turned_ref, weights_ref = refs[-6 - late:-2 - late]
-    partner_ref, mine_ref = refs[-2:]
+    if late:
+        refs, (edge_ref, out_ref, partner_ref, mine_ref, coef_ref, narrow_ref) = refs[:-6], refs[-6:]
+    else:
+        refs, (partner_ref, mine_ref) = refs[:-2], refs[-2:]
+    pair_ref, part_ref, turned_ref, weights_ref = refs[-4:]
     tile_dev = live_ref.shape[0]
     listed = table_ref.shape[0] - 2
     chunk = pair_ref.shape[0] // CHUNKS
@@ -242,11 +269,27 @@
     if late:
         pl.when(early > 0)(features)
         pl.when(early == 0)(begin)
-        edge_ref = refs[-3]
         pl.loop(early, CHUNKS - 1)(do_chunk)
         do_chunk(CHUNKS - 1, False)
         edge_ref[:RIM] = turned_ref[:RIM]
         edge_ref[RIM:] = turned_ref[tile_dev - RIM:]
+        pos, live, _, _, norm = field_terms([own_field(table_ref, own_ref, live_ref, f) for f in range(FIELDS)])
+        inside = slice(HALO_TILES, tile_dev - HALO_TILES)
+        raw = sum(part_ref[pl.ds(k, tile_dev - RIM, stride=8)] for k in range(8)) * norm[inside]
+        blank = jnp.zeros((HALO_TILES, live_ref.shape[1]), f32)
+        put_coefficients(coef_ref, pos, jnp.concatenate([blank, pressure(raw, live[inside]), blank], axis=0))
+
+        @pl.loop(HALO_TILES, tile_dev - HALO_TILES, unroll=8)
+        def _(t):
+            narrow(narrow_ref, coef_ref, t)
+
+        half = HALO_TILES // 2
+
+        @pl.loop(half, pair_ref.shape[0] - half, unroll=8)
+        def _(p):
+            t = HALO_TILES + 2 * p
+            partners = [(table_ref[n, t] - HALO_TILES, table_ref[n, t + 1] - HALO_TILES) for n in range(listed)]
+            force_pair(narrow_ref, partners, pair_ref.at[p], out_ref, 8 * t)
     else:
 
         @pl.when(early > 0)
@@ -256,19 +299,26 @@
 
 
 def outer_kernel(
-    table_ref, rim_lists_ref, own_ref, live_ref, below_ref, above_ref, pair_ref, part_ref, edge_ref,
-    density_ref, accel_ref, partner_ref, mine_ref, turned_ref, rim_pair_ref, rim_part_ref, coef_ref, coefb_ref, out_ref,
+    table_ref, rim_lists_ref, own_ref, live_ref, below_ref, above_ref, pair_ref, part_ref, edge_ref, inner_out_ref,
+    density_ref, accel_ref, partner_ref, mine_ref, turned_ref, weights_ref, rim_pair_ref, rim_part_ref, coef_ref,
+    coefb_ref, out_ref,
 ):
     tile_dev, rows = live_ref.shape
     ext = tile_dev + 2 * RIM
     listed = table_ref.shape[0] - 2
     fields = [
         jnp.concatenate(
-            [below_ref[f * RIM:(f + 1) * RIM], own_field(table_ref, own_ref, live_ref, f), above_ref[f * RIM:(f + 1) * RIM]], axis=0
+            [
+                below_ref[f * RIM:(f + 1) * RIM],
+                own_field(table_ref, own_ref, live_ref, f),
+                above_ref[f * RIM:(f + 1) * RIM],
+            ],
+            axis=0,
         )
         for f in range(FIELDS)
     ]
     pos, live, mass, inverse_sq, norm = field_terms(fields)
+    rim_pairs = RIM
 
     def rims(x):
         return jnp.concatenate([x[:2 * RIM], x[tile_dev:]], axis=0)
@@ -279,75 +329,56 @@
         turned_ref[RIM + e] = edge_ref[e]
         turned_ref[2 * RIM + e] = edge_ref[RIM + e]
         turned_ref[3 * RIM + e] = turned(partner_ref, 3 * RIM + e)
-
-    edge_pairs = HALO_TILES
-    half = HALO_TILES // 2
-    for side in range(2):
-        for i in range(edge_pairs):
-            e = 2 * RIM * side + HALO_TILES + 2 * i
-            own_side = (i >= half) if side == 0 else (i < half)
-            if own_side:
-                t = e - RIM if side == 0 else e - 3 * RIM + tile_dev
-                shift = HALO_TILES if side == 0 else HALO_TILES - tile_dev + 2 * RIM
-                partners = [(table_ref[n, t] + shift, table_ref[n, t + 1] + shift) for n in range(listed)]
-                store = rim_pair_ref.at[half * side + i % half]
-            else:
-                first = (2 * i if side == 0 else HALO_TILES + 2 * (i - half)) * listed
-                shift = HALO_TILES - tile_dev if side == 0 else HALO_TILES + 2 * RIM
-                partners = [
-                    (rim_lists_ref[first + n] + shift, rim_lists_ref[first + listed + n] + shift) for n in range(listed)
-                ]
-                store = None
-            at = 16 * (edge_pairs * side + i)
-            density_pair(turned_ref, pair_weights(mine_ref, e), partners, rim_part_ref, at, store)
-
-    inner_tiles = tile_dev - RIM
+    for r in range(rim_pairs):
+        weights_ref[r] = pair_weights(mine_ref, HALO_TILES + 2 * r + (RIM if 2 * r >= rim_pairs else 0))
+
+    outer = RIM + HALO_TILES
+    inner_raw = sum(part_ref[pl.ds(k, tile_dev - RIM, stride=8)] for k in range(8)) * norm[outer:ext - outer]
+    for r in range(rim_pairs):
+        first = 2 * r * listed
+        partners = [(rim_lists_ref[first + n], rim_lists_ref[first + listed + n]) for n in range(listed)]
+        density_pair(turned_ref, weights_ref[r], partners, rim_part_ref, 16 * r, rim_pair_ref.at[r])
+
+    rim_raw = sum(rim_part_ref[pl.ds(k, 2 * RIM, stride=8)] for k in range(8))
     raw = jnp.concatenate(
-        [
-            sum(rim_part_ref[pl.ds(k, RIM, stride=8)] for k in range(8)),
-            sum(part_ref[pl.ds(k, inner_tiles, stride=8)] for k in range(8)),
-            sum(rim_part_ref[pl.ds(8 * RIM + k, RIM, stride=8)] for k in range(8)),
-        ],
-        axis=0,
+        [rim_raw[:RIM] * norm[HALO_TILES:outer], inner_raw, rim_raw[RIM:] * norm[ext - outer:ext - HALO_TILES]], axis=0
     )
-    inner = slice(HALO_TILES, ext - HALO_TILES)
-    raw = raw * norm[inner]
-    q = jnp.where(live[inner], jnp.exp2(jnp.log2(jnp.where(live[inner], raw, 1.0)) * (-1.0 / 3.0)), 0.0)
+    q = pressure(raw, live[HALO_TILES:ext - HALO_TILES])
     pad = jnp.zeros((HALO_TILES, rows), f32)
     q = jnp.concatenate([pad, q, pad], axis=0)
-    put_rows(coef_ref, [jnp.ones_like(q)] + pos + [q] + [q * x for x in pos])
-
-    @pl.loop(0, ext, unroll=8)
-    def _(e):
-        coefb_ref[e] = jnp.concatenate(parts_of(tile_of(coef_ref, e), 2), axis=0).astype(bf16)
-
-    def force_pair(t, pair):
-        total = None
-        for n in range(listed):
-            e0, e1 = table_ref[n, t] + HALO_TILES, table_ref[n, t + 1] + HALO_TILES
-            left = jnp.concatenate([coefb_ref[e0], coefb_ref[e1]], axis=0)
-            w = pair[n * rows:(n + 1) * rows]
-            high = w.astype(bf16)
-            part = dot(left, high) + dot(left, (w - high.astype(f32)).astype(bf16))
-            total = part if total is None else total + part
-        at = 8 * t
-        out_ref[pl.ds(at, 8)] = total[:8, :rows] + total[8:16, :rows]
-        out_ref[pl.ds(at + 8, 8)] = total[16:24, rows:] + total[24:, rows:]
+    put_coefficients(coef_ref, pos, q)
+    for e in range(2 * RIM):
+        narrow(coefb_ref, coef_ref, HALO_TILES + e)
+        narrow(coefb_ref, coef_ref, ext - HALO_TILES - 2 * RIM + e)
+    half = HALO_TILES // 2
+    count = pair_ref.shape[0]
+
+    def edge_force(t, pair):
+        partners = [(table_ref[n, t] + HALO_TILES, table_ref[n, t + 1] + HALO_TILES) for n in range(listed)]
+        force_pair(coefb_ref, partners, pair, out_ref, 8 * t)
 
     for i in range(half):
-        force_pair(2 * i, rim_pair_ref.at[i])
-        force_pair(tile_dev - HALO_TILES + 2 * i, rim_pair_ref.at[half + i])
-
-    @pl.loop(0, pair_ref.shape[0], unroll=UNROLL)
-    def _(p):
-        force_pair(HALO_TILES + 2 * p, pair_ref.at[p])
+        edge_force(2 * i, rim_pair_ref.at[half + i])
+        edge_force(HALO_TILES + 2 * i, pair_ref.at[i])
+        edge_force(tile_dev - RIM + 2 * i, pair_ref.at[count - half + i])
+        edge_force(tile_dev - HALO_TILES + 2 * i, rim_pair_ref.at[2 * half + i])
 
     mine = slice(RIM, RIM + tile_dev)
     own_live = live_ref[...]
     density_ref[...] = raw[HALO_TILES:HALO_TILES + tile_dev] * own_live
     q_own = q[mine]
     scale = own_live * (2.0 * inverse_sq[mine] * norm[mine])
-    sums = [out_ref[pl.ds(k, tile_dev, stride=8)] for k in range(8)]
+    sums = [
+        jnp.concatenate(
+            [
+                out_ref[pl.ds(k, RIM, stride=8)],
+                inner_out_ref[pl.ds(8 * RIM + k, tile_dev - 2 * RIM, stride=8)],
+                out_ref[pl.ds(8 * (tile_dev - RIM) + k, RIM, stride=8)],
+            ],
+            axis=0,
+        )
+        for k in range(8)
+    ]
     for c in range(3):
         x = pos[c][mine]
         accel_ref[c] = scale * (q_own * (x * sums[0] - sums[1 + c]) + (x * sums[4] - sums[5 + c]))
@@ -364,34 +395,39 @@
         jax.ShapeDtypeStruct((tile_dev, rows, rows), bf16),
         jax.ShapeDtypeStruct((count, 2 * rows, 2 * rows), bf16),
     ]
-    edges = [jax.ShapeDtypeStruct((2 * RIM, rows, rows), bf16)] if late else []
+    features = [pltpu.VMEM((8 * tile_dev, rows), f32), pltpu.VMEM((8 * tile_dev, rows), f32)]
+    edges, forces = [], []
+    if late:
+        edges = [jax.ShapeDtypeStruct((2 * RIM, rows, rows), bf16), jax.ShapeDtypeStruct((8 * tile_dev, rows), f32)]
+        forces = [pltpu.VMEM((8 * tile_dev, rows), f32), pltpu.VMEM((tile_dev, 16, rows), bf16)]
     return pl.pallas_call(
         functools.partial(inner_kernel, late),
         out_shape=shapes + edges,
         in_specs=[SMEM] + [VMEM] * (2 + len(carried)),
         out_specs=[VMEM] * len(shapes + edges),
         input_output_aliases={3 + i: i for i in range(len(carried))},
-        scratch_shapes=[pltpu.VMEM((8 * tile_dev, rows), f32), pltpu.VMEM((8 * tile_dev, rows), f32)],
+        scratch_shapes=features + forces,
         compiler_params=pltpu.CompilerParams(vmem_limit_bytes=24 << 20),
         cost_estimate=pl.CostEstimate(flops=10 ** 9, bytes_accessed=10 ** 7, transcendentals=0),
         name="inner_late" if late else "inner_early",
     )(table, own, live, *carried)
 
 
-def outer_step(table, rim_lists, own, live, below, above, pair, part, edge):
+def outer_step(table, rim_lists, own, live, below, above, pair, part, edge, inner_out):
     tile_dev, rows = live.shape
     ext = tile_dev + 2 * RIM
     listed = table.shape[0] - 2
     return pl.pallas_call(
         outer_kernel,
         out_shape=(jax.ShapeDtypeStruct((tile_dev, rows), f32), jax.ShapeDtypeStruct((3, tile_dev, rows), f32)),
-        in_specs=[SMEM] * 2 + [VMEM] * 7,
+        in_specs=[SMEM] * 2 + [VMEM] * 8,
         out_specs=(VMEM, VMEM),
         scratch_shapes=[
             pltpu.VMEM((8 * 4 * RIM, rows), f32),
             pltpu.VMEM((8 * 4 * RIM, rows), f32),
             pltpu.VMEM((4 * RIM, rows, rows), bf16),
-            pltpu.VMEM((HALO_TILES, listed * rows, 2 * rows), f32),
+            pltpu.VMEM((RIM, 2 * rows, 2 * rows), bf16),
+            pltpu.VMEM((RIM, listed * rows, 2 * rows), f32),
             pltpu.VMEM((8 * 2 * RIM, rows), f32),
             pltpu.VMEM((8 * ext, rows), f32),
             pltpu.VMEM((ext, 16, rows), bf16),
@@ -399,7 +435,7 @@
         ],
         compiler_params=pltpu.CompilerParams(vmem_limit_bytes=24 << 20),
         name="outer_step",
-    )(table, rim_lists, own, live, below, above, pair, part, edge)
+    )(table, rim_lists, own, live, below, above, pair, part, edge, inner_out)
 
 
 def per_device(coords, smooth, masses, owners, counts, neighbours):
@@ -408,7 +444,7 @@
     subs = lax.axis_size("sub")
     per_dest = tile_dev // regions
     listed = neighbours.shape[1]
-    early = jnp.maximum(CHUNKS - 1 - lax.axis_index("sub"), 0).astype(jnp.int32)
+    early = jnp.maximum(CHUNKS - 1 - 2 * lax.axis_index("sub"), 0).astype(jnp.int32)
     pairwise = regions <= 4 and regions & (regions - 1) == 0
     grouped = group_tiles(coords, smooth, masses, owners, regions, pairwise)
     me = lax.axis_index("region") if pairwise else jnp.int32(0)
@@ -443,10 +479,16 @@
     below = lax.ppermute(rim(False), "sub", up)
     carried = inner_density(table, own, live)
     above = lax.ppermute(rim(True), "sub", down)
-    pair, part, _, _, edge = inner_density(table, own, live, carried)
+    pair, part, _, _, edge, inner_out = inner_density(table, own, live, carried)
     count = HALO_TILES * listed
-    rim_lists = jnp.concatenate([below[FIELDS * RIM, :count], above[FIELDS * RIM, :count]]).astype(jnp.int32)
-    return outer_step(table, rim_lists, own, live, below, above, pair, part, edge)
+    places = [
+        below[FIELDS * RIM, :count] + (HALO_TILES - tile_dev),
+        ids[0, 0, :count] + HALO_TILES,
+        ids[1, 0, :count] + (HALO_TILES - tile_dev + 2 * RIM),
+        above[FIELDS * RIM, :count] + (HALO_TILES + 2 * RIM),
+    ]
+    rim_lists = jnp.concatenate(places).astype(jnp.int32)
+    return outer_step(table, rim_lists, own, live, below, above, pair, part, edge, inner_out)
 
 
 def solution(mesh):

time: 26.5 us -> 24.3 us (0.917)
  waiting for transfers between devices: 3.58 us -> 1.53 us
    pallas_call x1, Pallas kernels: 5.67 us -> 3.04 us  [outer_step(): pl.pallas_call(outer_kernel, out_shape=(jax.ShapeDtypeStruct((tile_dev, r...]
    pallas_call x2, Pallas kernels: 4.42 us -> 6.95 us  [inner_density(): pl.pallas_call(functools.partial(inner_kernel, late), out_shape=shapes +...]
    ppermute x1, waiting for transfers between devices: 2.04 us -> 0.01 us  [per_device(): below = lax.ppermute(rim(False), 'sub', up)]
  transfers between devices with their start and end apart: 5 -> 5, of which waited for: 3 -> 2; matrix products, arithmetic and copies ran while one was open for 3% -> 3% of each run, Pallas kernels for 19% -> 31%
where the time goes in v6:
time: 24.3 us; the launch traced here: 24.1 us
  Pallas kernels  12.4 us (51%)
  starting transfers between devices  7.76 us (32%)
  waiting for transfers between devices  1.53 us (6%)
  other arithmetic  0.86 us (4%)
  local copies, waits for them, and re-layouts  0.81 us (3%)
  between operations  0.78 us (3%)
    pallas_call x2, Pallas kernels, inner_density(): pl.pallas_call(functools.partial(inner_kernel, late), out_shape=shapes +...  6.95 us
    ppermute x1, starting transfers between devices, per_device(): above = lax.ppermute(rim(True), 'sub', down)  4.58 us
    ppermute x3, starting transfers between devices, per_device(): lax.ppermute(grouped[k], 'region', [(i, i ^ k) for i in range(regions)])  3.18 us
    pallas_call x1, Pallas kernels, outer_step(): pl.pallas_call(outer_kernel, out_shape=(jax.ShapeDtypeStruct((tile_dev, r...  3.04 us
    pallas_call x1, Pallas kernels, group_tiles(): pl.pallas_call(functools.partial(group_kernel, pairwise, len(shapes)), ou...  1.75 us
    ppermute x3, waiting for transfers between devices, per_device(): lax.ppermute(grouped[k], 'region', [(i, i ^ k) for i in range(regions)])  1.53 us
    unnamed x2, local copies, waits for them, and re-layouts  0.78 us
    concatenate x1, other arithmetic, per_device(): table = jnp.concatenate([neighbours.T, counts[None], scalars[None]], axis=0)  0.71 us
  transfers between devices with their start and end apart: 5, of which 2 were waited for; matrix products, arithmetic and copies ran while one was open for 3% of the time, Pallas kernels for 31%

profile of v6, /device:TPU:0, one launch (start us, length us, event | category | flops | bytes accessed | tf_op | source)
XLA Modules:
  0.0 24.1 jit_solution(8945196435233558520)
XLA Ops:
  0.6 1.8 %group_tiles.1 = (f32[80,128]{1,0:T(8,128)}, f32[80,128]{1,0:T(8,128)}, f32[80,128]{1,0:T(8,128)}, f32[80,128]{1,0:T(8,128)}) custom-call(s32[64]{0:T(128)} %refs_0_.1, f32[3,64,128]{2,1,0:T(8,128)} %refs_1_.1, f32[64,128]{1,0:T(8,128)} %refs_2_.1, f32[64,128]{1,0:T(8,128)} %refs_3_.1), custom_call_target="tpu_custom_call" | custom-call | tf_op jit(solution)/shard_map/group_tiles/pallas_call | solution.py:74
  2.4 0.6 %collective-permute-start = (f32[80,128]{1,0:T(8,128)}, f32[80,128]{1,0:T(8,128)S(1)}, u32[]{:S(2)}, u32[]{:S(2)}) collective-permute-start(f32[80,128]{1,0:T(8,128)} %get-tuple-element.19), channel_id=1, source_target_pairs={{0,8},{8,0},{16,24},{24,16},{1,9},{9,1},{17,25},{25,17},{2,10},{10... | collective-permute-start | bytes 122888 | tf_op jit(solution)/shard_map/ppermute | solution.py:458
  2.9 2.6 %collective-permute-start.1 = (f32[80,128]{1,0:T(8,128)}, f32[80,128]{1,0:T(8,128)S(1)}, u32[]{:S(2)}, u32[]{:S(2)}) collective-permute-start(f32[80,128]{1,0:T(8,128)} %get-tuple-element.20), channel_id=1, source_target_pairs={{0,16},{8,24},{16,0},{24,8},{1,17},{9,25},{17,1},{25,9},{2,18},{10... | collective-permute-start | bytes 122888 | tf_op jit(solution)/shard_map/ppermute | solution.py:458
  5.5 0.0 collective-permute-start.2
  5.6 0.7 %pad_add_fusion.table_ref = s32[6,64]{1,0:T(8,128)S(1)} fusion(s32[1,64]{1,0:T(1,128)S(1)} %compare_select_fusion.1, s32[1,64]{1,0:T(1,128)} %bitcast.55, s32[4,64]{1,0:T(4,128)} %bitcast.54), kind=kLoop, calls=%fused_computation.14 | loop fusion | flops 768 | bytes 3072 | tf_op jit(solution)/shard_map/concatenate | solution.py:453
  6.3 0.0 copy-start
  6.3 0.8 %copy-done = f32[80,128]{1,0:T(8,128)S(1)} copy-done((f32[80,128]{1,0:T(8,128)S(1)}, f32[80,128]{1,0:T(8,128)}, u32[]{:S(2)}) %copy-start) | copy-done | bytes 40984
  7.1 0.6 %stage.1 = (f32[64,128]{1,0:T(8,128)S(1)}, f32[2,8,128]{2,1,0:T(8,128)S(1)}, f32[80,128]{1,0:T(8,128)S(1)}) custom-call(s32[6,64]{1,0:T(8,128)S(1)} %pad_add_fusion.table_ref, f32[80,128]{1,0:T(8,128)S(1)} %copy-done), custom_call_target="tpu_custom_call" | custom-call | tf_op jit(solution)/shard_map/stage/pallas_call | solution.py:107
  7.7 0.0 collective-permute-done
  7.7 0.2 collective-permute-done.1
  7.9 1.4 %collective-permute-done.2 = f32[80,128]{1,0:T(8,128)S(1)} collective-permute-done((f32[80,128]{1,0:T(8,128)}, f32[80,128]{1,0:T(8,128)S(1)}, u32[]{:S(2)}, u32[]{:S(2)}) %collective-permute-start.2) | collective-permute-done | bytes 40992 | tf_op jit(solution)/shard_map/ppermute | solution.py:458
  9.4 4.6 %collective-permute-start.4 = (f32[48,128]{1,0:T(8,128)S(1)}, f32[48,128]{1,0:T(8,128)S(1)}, u32[]{:S(2)}, u32[]{:S(2)}) collective-permute-start(f32[48,128]{1,0:T(8,128)S(1)} %pad_maximum_fusion.3), channel_id=1, source_target_pairs={{1,0},{2,1},{3,2},{4,3},{5,4},{6,5},{7,6},{0,7},{9,8},{10,9},{11,1... | collective-permute-start | bytes 73736 | tf_op jit(solution)/shard_map/ppermute | solution.py:481
  14.0 0.0 collective-permute-start.3
  14.0 3.1 %inner_early.1 = (f32[28,512,256]{2,1,0:T(8,128)S(1)}, f32[448,128]{1,0:T(8,128)S(1)}, bf16[64,128,128]{2,1,0:T(8,128)(2,1)S(1)}, bf16[28,256,256]{2,1,0:T(8,128)(2,1)S(1)}) custom-call(s32[6,64]{1,0:T(8,128)S(1)} %pad_add_fusion.table_ref, f32[4,80,128]{2,1,0:T(8,128)S(1)} %pad_maximum_fusion.1.own_ref, f32[64,128]{1,0:T(8,128)S(1)} %get-tuple-element.22.live_ref), custom_call_target="tpu_custom_call" | custom-call | flops 1000000000 | bytes 10000000 | tf_op jit(solution)/shard_map/inner_early/pallas_call | solution.py:403
  17.1 3.9 %inner_late.1 = (f32[28,512,256]{2,1,0:T(8,128)S(1)}, f32[448,128]{1,0:T(8,128)S(1)}, bf16[64,128,128]{2,1,0:T(8,128)(2,1)S(1)}, bf16[28,256,256]{2,1,0:T(8,128)...) custom-call(s32[6,64]{1,0:T(8,128)S(1)} %pad_add_fusion.table_ref, ...), custom_call_target="tpu_custom_call", output_to_operand_aliasing={{0}: (3, {}), {1}: (4, {}), {2}: (5, {}), {3}: (6, {})} | custom-call | flops 1000000000 | bytes 10000000 | tf_op jit(solution)/shard_map/inner_late/pallas_call | solution.py:403
  20.9 0.0 collective-permute-done.4.above_ref
  21.0 0.0 collective-permute-done.3.below_ref
  21.0 0.1 maximum_convert_fusion.rim_lists_ref
  21.1 3.0 %outer_step.1 = (f32[64,128]{1,0:T(8,128)}, f32[3,64,128]{2,1,0:T(8,128)}) custom-call(s32[6,64]{1,0:T(8,128)S(1)} %pad_add_fusion.table_ref, s32[64]{0:T(128)S(1)} %maximum_convert_fusion.rim_lists_ref, f32[4,80,128]{2,1,0:T(8,128)S(1)} %pad_maximum_fusion.1.own_ref, f32[64,128]{1,0:T(8,128)S(1)} %get-tuple-element.22.live_ref, ...), custom_call_target="tpu_custom_call" | custom-call | tf_op jit(solution)/shard_map/outer_step/pallas_call | solution.py:420
  (15 shorter events, 0.1 us)
Async XLA Ops:
  2.4 5.3 %collective-permute-start = (f32[80,128]{1,0:T(8,128)}, f32[80,128]{1,0:T(8,128)S(1)}, u32[]{:S(2)}, u32[]{:S(2)}) collective-permute-start(f32[80,128]{1,0:T(8,128)} %get-tuple-element.19), channel_id=1, source_target_pairs={{0,8},{8,0},{16,24},{24,16},{1,9},{9,1},{17,25},{25,17},{2,10},{10... | collective-permute-start | bytes 122888 | tf_op jit(solution)/shard_map/ppermute | solution.py:458
  2.9 5.0 %collective-permute-start.1 = (f32[80,128]{1,0:T(8,128)}, f32[80,128]{1,0:T(8,128)S(1)}, u32[]{:S(2)}, u32[]{:S(2)}) collective-permute-start(f32[80,128]{1,0:T(8,128)} %get-tuple-element.20), channel_id=1, source_target_pairs={{0,16},{8,24},{16,0},{24,8},{1,17},{9,25},{17,1},{25,9},{2,18},{10... | collective-permute-start | bytes 122888 | tf_op jit(solution)/shard_map/ppermute | solution.py:458
  5.5 3.7 %collective-permute-start.2 = (f32[80,128]{1,0:T(8,128)}, f32[80,128]{1,0:T(8,128)S(1)}, u32[]{:S(2)}, u32[]{:S(2)}) collective-permute-start(f32[80,128]{1,0:T(8,128)} %get-tuple-element.21), channel_id=1, source_target_pairs={{0,24},{8,16},{16,8},{24,0},{1,25},{9,17},{17,9},{25,1},{2,26},{10... | collective-permute-start | bytes 122888 | tf_op jit(solution)/shard_map/ppermute | solution.py:458
  6.3 0.8 %copy-start = (f32[80,128]{1,0:T(8,128)S(1)}, f32[80,128]{1,0:T(8,128)}, u32[]{:S(2)}) copy-start(f32[80,128]{1,0:T(8,128)} %get-tuple-element.17.local_ref) | copy-start | bytes 122884
  9.4 11.6 %collective-permute-start.4 = (f32[48,128]{1,0:T(8,128)S(1)}, f32[48,128]{1,0:T(8,128)S(1)}, u32[]{:S(2)}, u32[]{:S(2)}) collective-permute-start(f32[48,128]{1,0:T(8,128)S(1)} %pad_maximum_fusion.3), channel_id=1, source_target_pairs={{1,0},{2,1},{3,2},{4,3},{5,4},{6,5},{7,6},{0,7},{9,8},{10,9},{11,1... | collective-permute-start | bytes 73736 | tf_op jit(solution)/shard_map/ppermute | solution.py:481
  14.0 7.0 %collective-permute-start.3 = (f32[48,128]{1,0:T(8,128)S(1)}, f32[48,128]{1,0:T(8,128)S(1)}, u32[]{:S(2)}, u32[]{:S(2)}) collective-permute-start(f32[48,128]{1,0:T(8,128)S(1)} %pad_maximum_fusion.2), channel_id=1, source_target_pairs={{0,1},{1,2},{2,3},{3,4},{4,5},{5,6},{6,7},{7,0},{8,9},{9,10},{10,1... | collective-permute-start | bytes 73736 | tf_op jit(solution)/shard_map/ppermute | solution.py:479

commit v7 on v6

--- a/solution.py
+++ b/solution.py
@@ -20,6 +20,7 @@
 f32, bf16 = jnp.float32, jnp.bfloat16
 VMEM = pl.BlockSpec(memory_space=pltpu.VMEM)
 SMEM = pl.BlockSpec(memory_space=pltpu.SMEM)
+ANY = pl.BlockSpec(memory_space=pl.ANY)
 
 
 def group_kernel(pairwise, count, *refs):
@@ -85,7 +86,7 @@
 
 def stage_kernel(table_ref, local_ref, live_ref, ids_ref, here_ref):
     tile_dev, rows = live_ref.shape
-    listed = table_ref.shape[0] - 2
+    listed = table_ref.shape[0] - 1
     lane = lax.broadcasted_iota(jnp.int32, (8, rows), 1)
     row = lax.broadcasted_iota(jnp.int32, (8, rows), 0)
     for t in range(0, tile_dev, 8):
@@ -131,11 +132,12 @@
     return jnp.dot(a, b, preferred_element_type=f32)
 
 
-def own_field(table_ref, own_ref, live_ref, f):
+def own_field(pairwise, own_ref, live_ref, f):
     tile_dev = live_ref.shape[0]
     regions, per_dest = own_ref.shape[0], tile_dev // own_ref.shape[0]
     rows = pl.ds(f * per_dest, per_dest)
-    value = jnp.concatenate([own_ref[table_ref[table_ref.shape[0] - 1, 0] ^ r, rows] for r in range(regions)], axis=0)
+    me = lax.axis_index("region") if pairwise else 0
+    value = jnp.concatenate([own_ref[me ^ r, rows] for r in range(regions)], axis=0)
     return value * live_ref[...] if f == 4 else value
 
 
@@ -222,14 +224,16 @@
     out_ref[pl.ds(at + 8, 8)] = total[16:24, rows:] + total[24:, rows:]
 
 
-def inner_kernel(late, table_ref, own_ref, live_ref, *refs):
+def inner_kernel(late, pairwise, table_in_ref, own_ref, live_ref, *refs):
+    refs, (table_ref, table_sem) = refs[:-2], refs[-2:]
+    table_copy = pltpu.make_async_copy(table_in_ref, table_ref, table_sem.at[0])
     if late:
         refs, (edge_ref, out_ref, partner_ref, mine_ref, coef_ref, narrow_ref) = refs[:-6], refs[-6:]
     else:
         refs, (partner_ref, mine_ref) = refs[:-2], refs[-2:]
     pair_ref, part_ref, turned_ref, weights_ref = refs[-4:]
     tile_dev = live_ref.shape[0]
-    listed = table_ref.shape[0] - 2
+    listed = table_ref.shape[0] - 1
     chunk = pair_ref.shape[0] // CHUNKS
     ahead = 2 * chunk + 2 * HALO_TILES
 
@@ -240,9 +244,7 @@
         weights_ref[p] = pair_weights(mine_ref, HALO_TILES + 2 * p)
 
     def features():
-        pos, live, mass, inverse_sq, _ = field_terms(
-            [own_field(table_ref, own_ref, live_ref, f) for f in range(FIELDS)]
-        )
+        pos, live, mass, inverse_sq, _ = field_terms([own_field(pairwise, own_ref, live_ref, f) for f in range(FIELDS)])
         put_features(pos, live, mass, inverse_sq, partner_ref, mine_ref)
 
     def do_chunk(c, more=True):
@@ -257,23 +259,24 @@
             for i in range(chunk):
                 weigh((c + 1) * chunk + i)
 
-    early = table_ref[listed + 1, 1]
+    early = jnp.maximum(CHUNKS - 1 - 2 * lax.axis_index("sub"), 0)
 
     def begin():
-        features()
         for t in range(ahead):
             turn(t)
         for p in range(chunk):
             weigh(p)
 
     if late:
-        pl.when(early > 0)(features)
+        table_copy.start()
+        features()
         pl.when(early == 0)(begin)
+        table_copy.wait()
         pl.loop(early, CHUNKS - 1)(do_chunk)
         do_chunk(CHUNKS - 1, False)
         edge_ref[:RIM] = turned_ref[:RIM]
         edge_ref[RIM:] = turned_ref[tile_dev - RIM:]
-        pos, live, _, _, norm = field_terms([own_field(table_ref, own_ref, live_ref, f) for f in range(FIELDS)])
+        pos, live, _, _, norm = field_terms([own_field(pairwise, own_ref, live_ref, f) for f in range(FIELDS)])
         inside = slice(HALO_TILES, tile_dev - HALO_TILES)
         raw = sum(part_ref[pl.ds(k, tile_dev - RIM, stride=8)] for k in range(8)) * norm[inside]
         blank = jnp.zeros((HALO_TILES, live_ref.shape[1]), f32)
@@ -294,23 +297,32 @@
 
         @pl.when(early > 0)
         def _():
+            table_copy.start()
+            features()
             begin()
+            table_copy.wait()
             pl.loop(0, early)(do_chunk)
 
 
 def outer_kernel(
-    table_ref, rim_lists_ref, own_ref, live_ref, below_ref, above_ref, pair_ref, part_ref, edge_ref, inner_out_ref,
+    pairwise, table_in_ref, rim_lists_in_ref, own_ref, live_ref, below_ref, above_ref, pair_ref, part_ref, edge_ref, inner_out_ref,
     density_ref, accel_ref, partner_ref, mine_ref, turned_ref, weights_ref, rim_pair_ref, rim_part_ref, coef_ref,
-    coefb_ref, out_ref,
+    coefb_ref, out_ref, table_ref, rim_lists_ref, sems,
 ):
+    copies = [
+        pltpu.make_async_copy(table_in_ref, table_ref, sems.at[0]),
+        pltpu.make_async_copy(rim_lists_in_ref, rim_lists_ref, sems.at[1]),
+    ]
+    for copy in copies:
+        copy.start()
     tile_dev, rows = live_ref.shape
     ext = tile_dev + 2 * RIM
-    listed = table_ref.shape[0] - 2
+    listed = table_ref.shape[0] - 1
     fields = [
         jnp.concatenate(
             [
                 below_ref[f * RIM:(f + 1) * RIM],
-                own_field(table_ref, own_ref, live_ref, f),
+                own_field(pairwise, own_ref, live_ref, f),
                 above_ref[f * RIM:(f + 1) * RIM],
             ],
             axis=0,
@@ -334,6 +346,8 @@
 
     outer = RIM + HALO_TILES
     inner_raw = sum(part_ref[pl.ds(k, tile_dev - RIM, stride=8)] for k in range(8)) * norm[outer:ext - outer]
+    for copy in copies:
+        copy.wait()
     for r in range(rim_pairs):
         first = 2 * r * listed
         partners = [(rim_lists_ref[first + n], rim_lists_ref[first + listed + n]) for n in range(listed)]
@@ -384,9 +398,9 @@
         accel_ref[c] = scale * (q_own * (x * sums[0] - sums[1 + c]) + (x * sums[4] - sums[5 + c]))
 
 
-def inner_density(table, own, live, carried=()):
+def inner_density(pairwise, table, own, live, carried=()):
     tile_dev, rows = live.shape
-    listed = table.shape[0] - 2
+    listed = table.shape[0] - 1
     count = (tile_dev - RIM) // 2
     late = len(carried) > 0
     shapes = [
@@ -401,26 +415,26 @@
         edges = [jax.ShapeDtypeStruct((2 * RIM, rows, rows), bf16), jax.ShapeDtypeStruct((8 * tile_dev, rows), f32)]
         forces = [pltpu.VMEM((8 * tile_dev, rows), f32), pltpu.VMEM((tile_dev, 16, rows), bf16)]
     return pl.pallas_call(
-        functools.partial(inner_kernel, late),
+        functools.partial(inner_kernel, late, pairwise),
         out_shape=shapes + edges,
-        in_specs=[SMEM] + [VMEM] * (2 + len(carried)),
+        in_specs=[ANY] + [VMEM] * (2 + len(carried)),
         out_specs=[VMEM] * len(shapes + edges),
         input_output_aliases={3 + i: i for i in range(len(carried))},
-        scratch_shapes=features + forces,
+        scratch_shapes=features + forces + [pltpu.SMEM(table.shape, jnp.int32), pltpu.SemaphoreType.DMA((1,))],
         compiler_params=pltpu.CompilerParams(vmem_limit_bytes=24 << 20),
         cost_estimate=pl.CostEstimate(flops=10 ** 9, bytes_accessed=10 ** 7, transcendentals=0),
         name="inner_late" if late else "inner_early",
     )(table, own, live, *carried)
 
 
-def outer_step(table, rim_lists, own, live, below, above, pair, part, edge, inner_out):
+def outer_step(pairwise, table, rim_lists, own, live, below, above, pair, part, edge, inner_out):
     tile_dev, rows = live.shape
     ext = tile_dev + 2 * RIM
-    listed = table.shape[0] - 2
+    listed = table.shape[0] - 1
     return pl.pallas_call(
-        outer_kernel,
+        functools.partial(outer_kernel, pairwise),
         out_shape=(jax.ShapeDtypeStruct((tile_dev, rows), f32), jax.ShapeDtypeStruct((3, tile_dev, rows), f32)),
-        in_specs=[SMEM] * 2 + [VMEM] * 8,
+        in_specs=[ANY] * 2 + [VMEM] * 8,
         out_specs=(VMEM, VMEM),
         scratch_shapes=[
             pltpu.VMEM((8 * 4 * RIM, rows), f32),
@@ -432,6 +446,9 @@
             pltpu.VMEM((8 * ext, rows), f32),
             pltpu.VMEM((ext, 16, rows), bf16),
             pltpu.VMEM((8 * tile_dev, rows), f32),
+            pltpu.SMEM(table.shape, jnp.int32),
+            pltpu.SMEM(rim_lists.shape, jnp.int32),
+            pltpu.SemaphoreType.DMA((2,)),
         ],
         compiler_params=pltpu.CompilerParams(vmem_limit_bytes=24 << 20),
         name="outer_step",
@@ -444,13 +461,10 @@
     subs = lax.axis_size("sub")
     per_dest = tile_dev // regions
     listed = neighbours.shape[1]
-    early = jnp.maximum(CHUNKS - 1 - 2 * lax.axis_index("sub"), 0).astype(jnp.int32)
     pairwise = regions <= 4 and regions & (regions - 1) == 0
     grouped = group_tiles(coords, smooth, masses, owners, regions, pairwise)
     me = lax.axis_index("region") if pairwise else jnp.int32(0)
-    slot = jnp.arange(tile_dev, dtype=jnp.int32)
-    scalars = jnp.where(slot == 0, me, jnp.where(slot == 1, early, 0))
-    table = jnp.concatenate([neighbours.T, counts[None], scalars[None]], axis=0)
+    table = jnp.concatenate([neighbours.T, counts[None]], axis=0)
     if pairwise:
         live, ids, local = stage(table, grouped[0])
         blocks = [local]
@@ -477,9 +491,9 @@
     up = [(i, (i + 1) % subs) for i in range(subs)]
     down = [(j, i) for i, j in up]
     below = lax.ppermute(rim(False), "sub", up)
-    carried = inner_density(table, own, live)
+    carried = inner_density(pairwise, table, own, live)
     above = lax.ppermute(rim(True), "sub", down)
-    pair, part, _, _, edge, inner_out = inner_density(table, own, live, carried)
+    pair, part, _, _, edge, inner_out = inner_density(pairwise, table, own, live, carried)
     count = HALO_TILES * listed
     places = [
         below[FIELDS * RIM, :count] + (HALO_TILES - tile_dev),
@@ -488,7 +502,7 @@
         above[FIELDS * RIM, :count] + (HALO_TILES + 2 * RIM),
     ]
     rim_lists = jnp.concatenate(places).astype(jnp.int32)
-    return outer_step(table, rim_lists, own, live, below, above, pair, part, edge, inner_out)
+    return outer_step(pairwise, table, rim_lists, own, live, below, above, pair, part, edge, inner_out)
 
 
 def solution(mesh):

time: 24.3 us -> 23.8 us (0.979)
  Pallas kernels: 12.4 us -> 11.8 us
    pallas_call x3, Pallas kernels: 9.99 us -> 9.44 us  [the longest x2 6.61 us: inner_density(): pl.pallas_call(functools.partial(inner_kernel, late, pairwise), out_shape...]
where the time goes in v7:
time: 23.8 us; the launch traced here: 23.6 us
  Pallas kernels  11.8 us (50%)
  starting transfers between devices  7.76 us (33%)
  waiting for transfers between devices  1.54 us (6%)
  other arithmetic  0.85 us (4%)
  local copies, waits for them, and re-layouts  0.81 us (3%)
  between operations  0.79 us (3%)
    pallas_call x2, Pallas kernels, inner_density(): pl.pallas_call(functools.partial(inner_kernel, late, pairwise), out_shape...  6.61 us
    ppermute x1, starting transfers between devices, per_device(): above = lax.ppermute(rim(True), 'sub', down)  4.58 us
    ppermute x3, starting transfers between devices, per_device(): lax.ppermute(grouped[k], 'region', [(i, i ^ k) for i in range(regions)])  3.18 us
    pallas_call x1, Pallas kernels, outer_step(): pl.pallas_call(functools.partial(outer_kernel, pairwise), out_shape=(jax....  2.83 us
    pallas_call x1, Pallas kernels, group_tiles(): pl.pallas_call(functools.partial(group_kernel, pairwise, len(shapes)), ou...  1.75 us
    ppermute x3, waiting for transfers between devices, per_device(): lax.ppermute(grouped[k], 'region', [(i, i ^ k) for i in range(regions)])  1.53 us
    unnamed x2, local copies, waits for them, and re-layouts  0.78 us
    concatenate x1, other arithmetic, per_device(): table = jnp.concatenate([neighbours.T, counts[None]], axis=0)  0.71 us
  transfers between devices with their start and end apart: 5, of which 2 were waited for; matrix products, arithmetic and copies ran while one was open for 3% of the time, Pallas kernels for 31%

profile of v7, /device:TPU:0, one launch (start us, length us, event | category | flops | bytes accessed | tf_op | source)
XLA Modules:
  0.0 23.6 jit_solution(14376698546895191349)
XLA Ops:
  0.6 1.8 %group_tiles.1 = (f32[80,128]{1,0:T(8,128)}, f32[80,128]{1,0:T(8,128)}, f32[80,128]{1,0:T(8,128)}, f32[80,128]{1,0:T(8,128)}) custom-call(s32[64]{0:T(128)} %refs_0_.1, f32[3,64,128]{2,1,0:T(8,128)} %refs_1_.1, f32[64,128]{1,0:T(8,128)} %refs_2_.1, f32[64,128]{1,0:T(8,128)} %refs_3_.1), custom_call_target="tpu_custom_call" | custom-call | tf_op jit(solution)/shard_map/group_tiles/pallas_call | solution.py:75
  2.4 0.6 %collective-permute-start = (f32[80,128]{1,0:T(8,128)}, f32[80,128]{1,0:T(8,128)S(1)}, u32[]{:S(2)}, u32[]{:S(2)}) collective-permute-start(f32[80,128]{1,0:T(8,128)} %get-tuple-element.19), channel_id=1, source_target_pairs={{0,8},{8,0},{16,24},{24,16},{1,9},{9,1},{17,25},{25,17},{2,10},{10... | collective-permute-start | bytes 122888 | tf_op jit(solution)/shard_map/ppermute | solution.py:472
  2.9 2.6 %collective-permute-start.1 = (f32[80,128]{1,0:T(8,128)}, f32[80,128]{1,0:T(8,128)S(1)}, u32[]{:S(2)}, u32[]{:S(2)}) collective-permute-start(f32[80,128]{1,0:T(8,128)} %get-tuple-element.20), channel_id=1, source_target_pairs={{0,16},{8,24},{16,0},{24,8},{1,17},{9,25},{17,1},{25,9},{2,18},{10... | collective-permute-start | bytes 122888 | tf_op jit(solution)/shard_map/ppermute | solution.py:472
  5.5 0.0 collective-permute-start.2
  5.6 0.7 %pad_add_fusion.table_ref.table_in_ref = s32[5,64]{1,0:T(8,128)S(1)} fusion(s32[1,64]{1,0:T(1,128)} %bitcast.55, s32[4,64]{1,0:T(4,128)} %bitcast.54), kind=kLoop, calls=%fused_computation.14 | loop fusion | flops 320 | bytes 2560 | tf_op jit(solution)/shard_map/concatenate | solution.py:467
  6.3 0.0 copy-start
  6.3 0.8 %copy-done = f32[80,128]{1,0:T(8,128)S(1)} copy-done((f32[80,128]{1,0:T(8,128)S(1)}, f32[80,128]{1,0:T(8,128)}, u32[]{:S(2)}) %copy-start) | copy-done | bytes 40984
  7.1 0.6 %stage.1 = (f32[64,128]{1,0:T(8,128)S(1)}, f32[2,8,128]{2,1,0:T(8,128)S(1)}, f32[80,128]{1,0:T(8,128)S(1)}) custom-call(s32[5,64]{1,0:T(8,128)S(1)} %pad_add_fusion.table_ref.table_in_ref, f32[80,128]{1,0:T(8,128)S(1)} %copy-done), custom_call_target="tpu_custom_call" | custom-call | tf_op jit(solution)/shard_map/stage/pallas_call | solution.py:108
  7.7 0.0 collective-permute-done
  7.7 0.2 collective-permute-done.1
  7.9 1.4 %collective-permute-done.2 = f32[80,128]{1,0:T(8,128)S(1)} collective-permute-done((f32[80,128]{1,0:T(8,128)}, f32[80,128]{1,0:T(8,128)S(1)}, u32[]{:S(2)}, u32[]{:S(2)}) %collective-permute-start.2) | collective-permute-done | bytes 40992 | tf_op jit(solution)/shard_map/ppermute | solution.py:472
  9.4 4.6 %collective-permute-start.4 = (f32[48,128]{1,0:T(8,128)S(1)}, f32[48,128]{1,0:T(8,128)S(1)}, u32[]{:S(2)}, u32[]{:S(2)}) collective-permute-start(f32[48,128]{1,0:T(8,128)S(1)} %pad_maximum_fusion.3), channel_id=1, source_target_pairs={{1,0},{2,1},{3,2},{4,3},{5,4},{6,5},{7,6},{0,7},{9,8},{10,9},{11,1... | collective-permute-start | bytes 73736 | tf_op jit(solution)/shard_map/ppermute | solution.py:495
  14.0 0.0 collective-permute-start.3
  14.0 2.8 %inner_early.1 = (f32[28,512,256]{2,1,0:T(8,128)S(1)}, f32[448,128]{1,0:T(8,128)S(1)}, bf16[64,128,128]{2,1,0:T(8,128)(2,1)S(1)}, bf16[28,256,256]{2,1,0:T(8,128)(2,1)S(1)}) custom-call(s32[5,64]{1,0:T(8,128)S(1)} %pad_add_fusion.table_ref.table_in_ref, f32[4,80,128]{2,1,0:T(8,128)S(1)} %pad_maximum_fusion.1.own_ref, f32[64,128]{1,0:T(8,128)S(1)} %get-tuple-element.22.live_ref), custom_call_target="tpu_custom_call" | custom-call | flops 1000000000 | bytes 10000000 | tf_op jit(solution)/shard_map/inner_early/pallas_call | solution.py:417
  16.8 3.8 %inner_late.1 = (f32[28,512,256]{2,1,0:T(8,128)S(1)}, f32[448,128]{1,0:T(8,128)S(1)}, bf16[64,128,128]{2,1,0:T(8,128)(2,1)S(1)}, bf16[28,256,256]{2,1,0:T(8,128)...) custom-call(s32[5,64]{1,0:T(8,128)S(1)} %pad_add_fusion.table_ref.ta, ...), custom_call_target="tpu_custom_call", output_to_operand_aliasing={{0}: (3, {}), {1}: (4, {}), {2}: (5, {}), {3}: (6, {})} | custom-call | flops 1000000000 | bytes 10000000 | tf_op jit(solution)/shard_map/inner_late/pallas_call | solution.py:417
  20.6 0.0 collective-permute-done.4.above_ref
  20.6 0.0 collective-permute-done.3.below_ref
  20.7 0.1 maximum_convert_fusion.rim_lists_in_ref
  20.7 2.8 %outer_step.1 = (f32[64,128]{1,0:T(8,128)}, f32[3,64,128]{2,1,0:T(8,128)}) custom-call(s32[5,64]{1,0:T(8,128)S(1)} %pad_add_fusion.table_ref.table_in_ref, s32[64]{0:T(128)S(1)} %maximum_convert_fusion.rim_lists_in_ref, f32[4,80,128]{2,1,0:T(8,128)S(1)} %pad_maximum_fusion.1.own_ref, f32[64,128]{1,0:T(8,128)S(1)} %get-tuple-element.22.live_ref, ...), custom_call_target="tpu_custom_call" | custom-call | tf_op jit(solution)/shard_map/outer_step/pallas_call | solution.py:434
  (14 shorter events, 0.1 us)
Async XLA Ops:
  2.4 5.3 %collective-permute-start = (f32[80,128]{1,0:T(8,128)}, f32[80,128]{1,0:T(8,128)S(1)}, u32[]{:S(2)}, u32[]{:S(2)}) collective-permute-start(f32[80,128]{1,0:T(8,128)} %get-tuple-element.19), channel_id=1, source_target_pairs={{0,8},{8,0},{16,24},{24,16},{1,9},{9,1},{17,25},{25,17},{2,10},{10... | collective-permute-start | bytes 122888 | tf_op jit(solution)/shard_map/ppermute | solution.py:472
  2.9 5.0 %collective-permute-start.1 = (f32[80,128]{1,0:T(8,128)}, f32[80,128]{1,0:T(8,128)S(1)}, u32[]{:S(2)}, u32[]{:S(2)}) collective-permute-start(f32[80,128]{1,0:T(8,128)} %get-tuple-element.20), channel_id=1, source_target_pairs={{0,16},{8,24},{16,0},{24,8},{1,17},{9,25},{17,1},{25,9},{2,18},{10... | collective-permute-start | bytes 122888 | tf_op jit(solution)/shard_map/ppermute | solution.py:472
  5.5 3.7 %collective-permute-start.2 = (f32[80,128]{1,0:T(8,128)}, f32[80,128]{1,0:T(8,128)S(1)}, u32[]{:S(2)}, u32[]{:S(2)}) collective-permute-start(f32[80,128]{1,0:T(8,128)} %get-tuple-element.21), channel_id=1, source_target_pairs={{0,24},{8,16},{16,8},{24,0},{1,25},{9,17},{17,9},{25,1},{2,26},{10... | collective-permute-start | bytes 122888 | tf_op jit(solution)/shard_map/ppermute | solution.py:472
  6.3 0.8 %copy-start = (f32[80,128]{1,0:T(8,128)S(1)}, f32[80,128]{1,0:T(8,128)}, u32[]{:S(2)}) copy-start(f32[80,128]{1,0:T(8,128)} %get-tuple-element.17.local_ref) | copy-start | bytes 122884
  9.4 11.2 %collective-permute-start.4 = (f32[48,128]{1,0:T(8,128)S(1)}, f32[48,128]{1,0:T(8,128)S(1)}, u32[]{:S(2)}, u32[]{:S(2)}) collective-permute-start(f32[48,128]{1,0:T(8,128)S(1)} %pad_maximum_fusion.3), channel_id=1, source_target_pairs={{1,0},{2,1},{3,2},{4,3},{5,4},{6,5},{7,6},{0,7},{9,8},{10,9},{11,1... | collective-permute-start | bytes 73736 | tf_op jit(solution)/shard_map/ppermute | solution.py:495
  14.0 6.7 %collective-permute-start.3 = (f32[48,128]{1,0:T(8,128)S(1)}, f32[48,128]{1,0:T(8,128)S(1)}, u32[]{:S(2)}, u32[]{:S(2)}) collective-permute-start(f32[48,128]{1,0:T(8,128)S(1)} %pad_maximum_fusion.2), channel_id=1, source_target_pairs={{0,1},{1,2},{2,3},{3,4},{4,5},{5,6},{6,7},{7,0},{8,9},{9,10},{10,1... | collective-permute-start | bytes 73736 | tf_op jit(solution)/shard_map/ppermute | solution.py:493

commit v8 on v7

--- a/solution.py
+++ b/solution.py
@@ -25,7 +25,7 @@
 
 def group_kernel(pairwise, count, *refs):
     sources, outs = refs[:4], refs[4:4 + count]
-    owners_ref, coords_ref, smooth_ref, masses_ref, block_ref, sems, out_sems = refs[4 + count:]
+    owners_ref, coords_ref, smooth_ref, masses_ref, block_ref, sems = refs[4 + count:]
     targets = (owners_ref, coords_ref, smooth_ref, masses_ref)
     copies = [pltpu.make_async_copy(s, t, sems.at[i]) for i, (s, t) in enumerate(zip(sources, targets))]
     for copy in copies:
@@ -56,13 +56,8 @@
             block_ref[d, pl.ds(c * per_dest + k, 1)] = coords_ref[c, n:n + 1]
         block_ref[d, pl.ds(3 * per_dest + k, 1)] = smooth_ref[n:n + 1]
         block_ref[d, pl.ds(4 * per_dest + k, 1)] = masses_ref[n:n + 1]
-    copies = [
-        pltpu.make_async_copy(block_ref.at[k] if pairwise else block_ref, out, out_sems.at[k]) for k, out in enumerate(outs)
-    ]
-    for copy in copies:
-        copy.start()
-    for copy in copies:
-        copy.wait()
+    for k, out in enumerate(outs):
+        out[...] = block_ref[k] if pairwise else block_ref[...]
 
 
 def group_tiles(coords, smooth, masses, owners, regions, pairwise):
@@ -76,15 +71,16 @@
         functools.partial(group_kernel, pairwise, len(shapes)),
         out_shape=[jax.ShapeDtypeStruct(shape, f32) for shape in shapes],
         in_specs=[hbm] * 4,
-        out_specs=[hbm] * len(shapes),
+        out_specs=[VMEM] * len(shapes),
         scratch_shapes=[pltpu.SMEM(owners.shape, jnp.int32)]
         + [pltpu.VMEM(a.shape, f32) for a in (coords, smooth, masses)]
-        + [pltpu.VMEM(whole, f32), pltpu.SemaphoreType.DMA((4,)), pltpu.SemaphoreType.DMA((len(shapes),))],
+        + [pltpu.VMEM(whole, f32), pltpu.SemaphoreType.DMA((4,))],
+        compiler_params=pltpu.CompilerParams(vmem_limit_bytes=8 << 20),
         name="group_tiles",
-    )(owners, coords, smooth, masses)
-
-
-def stage_kernel(table_ref, local_ref, live_ref, ids_ref, here_ref):
+    )(*[pltpu.with_memory_space_constraint(a, pltpu.HBM) for a in (owners, coords, smooth, masses)])
+
+
+def stage_kernel(table_ref, live_ref, ids_ref):
     tile_dev, rows = live_ref.shape
     listed = table_ref.shape[0] - 1
     lane = lax.broadcasted_iota(jnp.int32, (8, rows), 1)
@@ -100,23 +96,21 @@
             for n in range(listed):
                 ids = jnp.where(lane == i * listed + n, table_ref[n, start + i].astype(f32), ids)
         ids_ref[side] = ids
-    here_ref[...] = local_ref[...]
-
-
-def stage(table, local):
-    tile_dev, rows = table.shape[1], local.shape[-1]
+
+
+def stage(table, rows):
+    tile_dev = table.shape[1]
     return pl.pallas_call(
         stage_kernel,
         out_shape=(
             jax.ShapeDtypeStruct((tile_dev, rows), f32),
             jax.ShapeDtypeStruct((2, 8, rows), f32),
-            jax.ShapeDtypeStruct(local.shape, f32),
         ),
-        in_specs=[SMEM, VMEM],
-        out_specs=(VMEM,) * 3,
+        in_specs=[SMEM],
+        out_specs=(VMEM,) * 2,
         compiler_params=pltpu.CompilerParams(vmem_limit_bytes=4 << 20),
         name="stage",
-    )(table, local)
+    )(table)
 
 
 def parts_of(x, count):
@@ -188,13 +182,11 @@
 
 def density_pair(turned_ref, own, partners, part_ref, at, store):
     rows = own.shape[1] // 2
-    total = None
-    for n, (e0, e1) in enumerate(partners):
-        t = jnp.exp2(dot(jnp.concatenate([turned_ref[e0], turned_ref[e1]], axis=1), own))
-        if store is not None:
-            store[n * rows:(n + 1) * rows] = t
-        part = jnp.sum(t.reshape(rows // 8, 8, 2 * rows), axis=0)
-        total = part if total is None else total + part
+    left = [jnp.concatenate([turned_ref[a], turned_ref[b]], axis=1) for a, b in partners]
+    t = jnp.exp2(dot(jnp.concatenate(left, axis=0), own))
+    if store is not None:
+        store[...] = t
+    total = jnp.sum(t.reshape(t.shape[0] // 8, 8, 2 * rows), axis=0)
     part_ref[pl.ds(at, 8)] = total[:, :rows]
     part_ref[pl.ds(at + 8, 8)] = total[:, rows:]
 
@@ -466,13 +458,13 @@
     me = lax.axis_index("region") if pairwise else jnp.int32(0)
     table = jnp.concatenate([neighbours.T, counts[None]], axis=0)
     if pairwise:
-        live, ids, local = stage(table, grouped[0])
-        blocks = [local]
+        live, ids = stage(table, rows)
+        blocks = [grouped[0]]
         for k in range(1, regions):
             blocks.append(lax.ppermute(grouped[k], "region", [(i, i ^ k) for i in range(regions)]))
         own = jnp.stack(blocks)
     else:
-        live, ids, _ = stage(table, grouped[0][0])
+        live, ids = stage(table, rows)
         own = lax.all_to_all(grouped[0], "region", 0, 0, tiled=True)
     by_field = own.reshape(regions, FIELDS, per_dest, rows)
 

time: 23.8 us -> 22.8 us (0.958)
  local copies, waits for them, and re-layouts: 0.81 us -> 0.03 us
  Pallas kernels: 11.8 us -> 11.1 us
  waiting for transfers between devices: 1.54 us -> 2.11 us
    unnamed x2 -> x0, local copies, waits for them, and re-layouts: 0.78 us -> none
    pallas_call x1, Pallas kernels: 1.75 us -> 1.08 us  [group_tiles(): pl.pallas_call(functools.partial(group_kernel, pairwise, len(shapes)), ou...]
    ppermute x3, waiting for transfers between devices: 1.53 us -> 2.1 us  [per_device(): lax.ppermute(grouped[k], 'region', [(i, i ^ k) for i in range(regions)])]
  transfers between devices with their start and end apart: 5 -> 5, of which waited for: 2 -> 2; matrix products, arithmetic and copies ran while one was open for 3% -> 3% of each run, Pallas kernels for 31% -> 32%
where the time goes in v8:
time: 22.8 us; the launch traced here: 22.6 us
  Pallas kernels  11.1 us (49%)
  starting transfers between devices  7.76 us (34%)
  waiting for transfers between devices  2.11 us (9%)
  other arithmetic  0.85 us (4%)
  between operations  0.78 us (3%)
    pallas_call x2, Pallas kernels, inner_density(): pl.pallas_call(functools.partial(inner_kernel, late, pairwise), out_shape...  6.55 us
    ppermute x1, starting transfers between devices, per_device(): above = lax.ppermute(rim(True), 'sub', down)  4.58 us
    ppermute x3, starting transfers between devices, per_device(): lax.ppermute(grouped[k], 'region', [(i, i ^ k) for i in range(regions)])  3.18 us
    pallas_call x1, Pallas kernels, outer_step(): pl.pallas_call(functools.partial(outer_kernel, pairwise), out_shape=(jax....  2.81 us
    ppermute x3, waiting for transfers between devices, per_device(): lax.ppermute(grouped[k], 'region', [(i, i ^ k) for i in range(regions)])  2.1 us
    pallas_call x1, Pallas kernels, group_tiles(): pl.pallas_call(functools.partial(group_kernel, pairwise, len(shapes)), ou...  1.08 us
    concatenate x1, other arithmetic, per_device(): table = jnp.concatenate([neighbours.T, counts[None]], axis=0)  0.71 us
    pallas_call x1, Pallas kernels, stage(): pl.pallas_call(stage_kernel, out_shape=(jax.ShapeDtypeStruct((tile_dev, r...  0.64 us
  transfers between devices with their start and end apart: 5, of which 2 were waited for; matrix products, arithmetic and copies ran while one was open for 3% of the time, Pallas kernels for 32%

profile of v8, /device:TPU:0, one launch (start us, length us, event | category | flops | bytes accessed | tf_op | source)
XLA Modules:
  0.0 22.6 jit_solution(15133432336022844292)
XLA Ops:
  0.6 1.1 %group_tiles.1 = (f32[80,128]{1,0:T(8,128)S(1)}, f32[80,128]{1,0:T(8,128)S(1)}, f32[80,128]{1,0:T(8,128)S(1)}, f32[80,128]{1,0:T(8,128)S(1)}) custom-call(s32[64]{0:T(128)} %refs_0_.1, f32[3,64,128]{2,1,0:T(8,128)} %refs_1_.1, f32[64,128]{1,0:T(8,128)} %refs_2_.1, f32[64,128]{1,0:T(8,128)} %refs_3_.1), custom_call_target="tpu_custom_call" | custom-call | tf_op jit(solution)/shard_map/group_tiles/pallas_call | solution.py:70
  1.7 0.6 %collective-permute-start = (f32[80,128]{1,0:T(8,128)S(1)}, f32[80,128]{1,0:T(8,128)S(1)}, u32[]{:S(2)}, u32[]{:S(2)}) collective-permute-start(f32[80,128]{1,0:T(8,128)S(1)} %get-tuple-element.17), channel_id=1, source_target_pairs={{0,8},{8,0},{16,24},{24,16},{1,9},{9,1},{17,25},{25,17},{2,10},{10... | collective-permute-start | bytes 122888 | tf_op jit(solution)/shard_map/ppermute | solution.py:464
  2.3 2.6 %collective-permute-start.1 = (f32[80,128]{1,0:T(8,128)S(1)}, f32[80,128]{1,0:T(8,128)S(1)}, u32[]{:S(2)}, u32[]{:S(2)}) collective-permute-start(f32[80,128]{1,0:T(8,128)S(1)} %get-tuple-element.18), channel_id=1, source_target_pairs={{0,16},{8,24},{16,0},{24,8},{1,17},{9,25},{17,1},{25,9},{2,18},{10... | collective-permute-start | bytes 122888 | tf_op jit(solution)/shard_map/ppermute | solution.py:464
  4.9 0.0 collective-permute-start.2
  4.9 0.7 %pad_add_fusion.table_ref.table_in_ref = s32[5,64]{1,0:T(8,128)S(1)} fusion(s32[1,64]{1,0:T(1,128)} %bitcast.55, s32[4,64]{1,0:T(4,128)} %bitcast.54), kind=kLoop, calls=%fused_computation.14 | loop fusion | flops 320 | bytes 2560 | tf_op jit(solution)/shard_map/concatenate | solution.py:459
  5.6 0.6 %stage.1 = (f32[64,128]{1,0:T(8,128)S(1)}, f32[2,8,128]{2,1,0:T(8,128)S(1)}) custom-call(s32[5,64]{1,0:T(8,128)S(1)} %pad_add_fusion.table_ref.table_in_ref), custom_call_target="tpu_custom_call" | custom-call | tf_op jit(solution)/shard_map/stage/pallas_call | solution.py:103
  6.3 0.0 collective-permute-done
  6.3 0.7 %collective-permute-done.1 = f32[80,128]{1,0:T(8,128)S(1)} collective-permute-done((f32[80,128]{1,0:T(8,128)S(1)}, f32[80,128]{1,0:T(8,128)S(1)}, u32[]{:S(2)}, u32[]{:S(2)}) %collective-permute-start.1) | collective-permute-done | bytes 40992 | tf_op jit(solution)/shard_map/ppermute | solution.py:464
  7.0 1.4 %collective-permute-done.2 = f32[80,128]{1,0:T(8,128)S(1)} collective-permute-done((f32[80,128]{1,0:T(8,128)S(1)}, f32[80,128]{1,0:T(8,128)S(1)}, u32[]{:S(2)}, u32[]{:S(2)}) %collective-permute-start.2) | collective-permute-done | bytes 40992 | tf_op jit(solution)/shard_map/ppermute | solution.py:464
  8.5 4.6 %collective-permute-start.4 = (f32[48,128]{1,0:T(8,128)S(1)}, f32[48,128]{1,0:T(8,128)S(1)}, u32[]{:S(2)}, u32[]{:S(2)}) collective-permute-start(f32[48,128]{1,0:T(8,128)S(1)} %pad_maximum_fusion.3), channel_id=1, source_target_pairs={{1,0},{2,1},{3,2},{4,3},{5,4},{6,5},{7,6},{0,7},{9,8},{10,9},{11,1... | collective-permute-start | bytes 73736 | tf_op jit(solution)/shard_map/ppermute | solution.py:487
  13.1 0.0 collective-permute-start.3
  13.1 2.7 %inner_early.1 = (f32[28,512,256]{2,1,0:T(8,128)S(1)}, f32[448,128]{1,0:T(8,128)S(1)}, bf16[64,128,128]{2,1,0:T(8,128)(2,1)S(1)}, bf16[28,256,256]{2,1,0:T(8,128)(2,1)S(1)}) custom-call(s32[5,64]{1,0:T(8,128)S(1)} %pad_add_fusion.table_ref.table_in_ref, f32[4,80,128]{2,1,0:T(8,128)S(1)} %pad_maximum_fusion.1.own_ref, f32[64,128]{1,0:T(8,128)S(1)} %get-tuple-element.20.live_ref), custom_call_target="tpu_custom_call" | custom-call | flops 1000000000 | bytes 10000000 | tf_op jit(solution)/shard_map/inner_early/pallas_call | solution.py:409
  15.9 3.8 %inner_late.1 = (f32[28,512,256]{2,1,0:T(8,128)S(1)}, f32[448,128]{1,0:T(8,128)S(1)}, bf16[64,128,128]{2,1,0:T(8,128)(2,1)S(1)}, bf16[28,256,256]{2,1,0:T(8,128)...) custom-call(s32[5,64]{1,0:T(8,128)S(1)} %pad_add_fusion.table_ref.ta, ...), custom_call_target="tpu_custom_call", output_to_operand_aliasing={{0}: (3, {}), {1}: (4, {}), {2}: (5, {}), {3}: (6, {})} | custom-call | flops 1000000000 | bytes 10000000 | tf_op jit(solution)/shard_map/inner_late/pallas_call | solution.py:409
  19.7 0.0 collective-permute-done.4.above_ref
  19.7 0.0 collective-permute-done.3.below_ref
  19.7 0.1 maximum_convert_fusion.rim_lists_in_ref
  19.8 2.8 %outer_step.1 = (f32[64,128]{1,0:T(8,128)}, f32[3,64,128]{2,1,0:T(8,128)}) custom-call(s32[5,64]{1,0:T(8,128)S(1)} %pad_add_fusion.table_ref.table_in_ref, s32[64]{0:T(128)S(1)} %maximum_convert_fusion.rim_lists_in_ref, f32[4,80,128]{2,1,0:T(8,128)S(1)} %pad_maximum_fusion.1.own_ref, f32[64,128]{1,0:T(8,128)S(1)} %get-tuple-element.20.live_ref, ...), custom_call_target="tpu_custom_call" | custom-call | tf_op jit(solution)/shard_map/outer_step/pallas_call | solution.py:426
  (14 shorter events, 0.1 us)
Async XLA Ops:
  1.7 4.6 %collective-permute-start = (f32[80,128]{1,0:T(8,128)S(1)}, f32[80,128]{1,0:T(8,128)S(1)}, u32[]{:S(2)}, u32[]{:S(2)}) collective-permute-start(f32[80,128]{1,0:T(8,128)S(1)} %get-tuple-element.17), channel_id=1, source_target_pairs={{0,8},{8,0},{16,24},{24,16},{1,9},{9,1},{17,25},{25,17},{2,10},{10... | collective-permute-start | bytes 122888 | tf_op jit(solution)/shard_map/ppermute | solution.py:464
  2.3 4.7 %collective-permute-start.1 = (f32[80,128]{1,0:T(8,128)S(1)}, f32[80,128]{1,0:T(8,128)S(1)}, u32[]{:S(2)}, u32[]{:S(2)}) collective-permute-start(f32[80,128]{1,0:T(8,128)S(1)} %get-tuple-element.18), channel_id=1, source_target_pairs={{0,16},{8,24},{16,0},{24,8},{1,17},{9,25},{17,1},{25,9},{2,18},{10... | collective-permute-start | bytes 122888 | tf_op jit(solution)/shard_map/ppermute | solution.py:464
  4.9 3.5 %collective-permute-start.2 = (f32[80,128]{1,0:T(8,128)S(1)}, f32[80,128]{1,0:T(8,128)S(1)}, u32[]{:S(2)}, u32[]{:S(2)}) collective-permute-start(f32[80,128]{1,0:T(8,128)S(1)} %get-tuple-element.19), channel_id=1, source_target_pairs={{0,24},{8,16},{16,8},{24,0},{1,25},{9,17},{17,9},{25,1},{2,26},{10... | collective-permute-start | bytes 122888 | tf_op jit(solution)/shard_map/ppermute | solution.py:464
  8.5 11.2 %collective-permute-start.4 = (f32[48,128]{1,0:T(8,128)S(1)}, f32[48,128]{1,0:T(8,128)S(1)}, u32[]{:S(2)}, u32[]{:S(2)}) collective-permute-start(f32[48,128]{1,0:T(8,128)S(1)} %pad_maximum_fusion.3), channel_id=1, source_target_pairs={{1,0},{2,1},{3,2},{4,3},{5,4},{6,5},{7,6},{0,7},{9,8},{10,9},{11,1... | collective-permute-start | bytes 73736 | tf_op jit(solution)/shard_map/ppermute | solution.py:487
  13.1 6.6 %collective-permute-start.3 = (f32[48,128]{1,0:T(8,128)S(1)}, f32[48,128]{1,0:T(8,128)S(1)}, u32[]{:S(2)}, u32[]{:S(2)}) collective-permute-start(f32[48,128]{1,0:T(8,128)S(1)} %pad_maximum_fusion.2), channel_id=1, source_target_pairs={{0,1},{1,2},{2,3},{3,4},{4,5},{5,6},{6,7},{7,0},{8,9},{9,10},{10,1... | collective-permute-start | bytes 73736 | tf_op jit(solution)/shard_map/ppermute | solution.py:485

commit v9 on v8

--- a/solution.py
+++ b/solution.py
@@ -251,7 +251,7 @@
             for i in range(chunk):
                 weigh((c + 1) * chunk + i)
 
-    early = jnp.maximum(CHUNKS - 1 - 2 * lax.axis_index("sub"), 0)
+    early = jnp.maximum(2 * CHUNKS - lax.axis_index("sub"), 0) // 2
 
     def begin():
         for t in range(ahead):
@@ -264,8 +264,8 @@
         features()
         pl.when(early == 0)(begin)
         table_copy.wait()
-        pl.loop(early, CHUNKS - 1)(do_chunk)
-        do_chunk(CHUNKS - 1, False)
+        pl.loop(jnp.minimum(early, CHUNKS - 1), CHUNKS - 1)(do_chunk)
+        pl.when(early < CHUNKS)(lambda: do_chunk(CHUNKS - 1, False))
         edge_ref[:RIM] = turned_ref[:RIM]
         edge_ref[RIM:] = turned_ref[tile_dev - RIM:]
         pos, live, _, _, norm = field_terms([own_field(pairwise, own_ref, live_ref, f) for f in range(FIELDS)])
@@ -293,7 +293,8 @@
             features()
             begin()
             table_copy.wait()
-            pl.loop(0, early)(do_chunk)
+            pl.loop(0, jnp.minimum(early, CHUNKS - 1))(do_chunk)
+            pl.when(early == CHUNKS)(lambda: do_chunk(CHUNKS - 1, False))
 
 
 def outer_kernel(

time: 22.8 us -> 22.8 us (level)
  no operation moved by 1% of the time
where the time goes in v9:
time: 22.8 us; the launch traced here: 22.6 us
  Pallas kernels  11.1 us (49%)
  starting transfers between devices  7.76 us (34%)
  waiting for transfers between devices  2.11 us (9%)
  other arithmetic  0.85 us (4%)
  between operations  0.78 us (3%)
    pallas_call x2, Pallas kernels, inner_density(): pl.pallas_call(functools.partial(inner_kernel, late, pairwise), out_shape...  6.58 us
    ppermute x1, starting transfers between devices, per_device(): above = lax.ppermute(rim(True), 'sub', down)  4.58 us
    ppermute x3, starting transfers between devices, per_device(): lax.ppermute(grouped[k], 'region', [(i, i ^ k) for i in range(regions)])  3.18 us
    pallas_call x1, Pallas kernels, outer_step(): pl.pallas_call(functools.partial(outer_kernel, pairwise), out_shape=(jax....  2.81 us
    ppermute x3, waiting for transfers between devices, per_device(): lax.ppermute(grouped[k], 'region', [(i, i ^ k) for i in range(regions)])  2.1 us
    pallas_call x1, Pallas kernels, group_tiles(): pl.pallas_call(functools.partial(group_kernel, pairwise, len(shapes)), ou...  1.08 us
    concatenate x1, other arithmetic, per_device(): table = jnp.concatenate([neighbours.T, counts[None]], axis=0)  0.71 us
    pallas_call x1, Pallas kernels, stage(): pl.pallas_call(stage_kernel, out_shape=(jax.ShapeDtypeStruct((tile_dev, r...  0.64 us
  transfers between devices with their start and end apart: 5, of which 2 were waited for; matrix products, arithmetic and copies ran while one was open for 3% of the time, Pallas kernels for 32%

profile of v9, /device:TPU:0, one launch (start us, length us, event | category | flops | bytes accessed | tf_op | source)
XLA Modules:
  0.0 22.6 jit_solution(15931957337668324276)
XLA Ops:
  0.6 1.1 %group_tiles.1 = (f32[80,128]{1,0:T(8,128)S(1)}, f32[80,128]{1,0:T(8,128)S(1)}, f32[80,128]{1,0:T(8,128)S(1)}, f32[80,128]{1,0:T(8,128)S(1)}) custom-call(s32[64]{0:T(128)} %refs_0_.1, f32[3,64,128]{2,1,0:T(8,128)} %refs_1_.1, f32[64,128]{1,0:T(8,128)} %refs_2_.1, f32[64,128]{1,0:T(8,128)} %refs_3_.1), custom_call_target="tpu_custom_call" | custom-call | tf_op jit(solution)/shard_map/group_tiles/pallas_call | solution.py:70
  1.7 0.6 %collective-permute-start = (f32[80,128]{1,0:T(8,128)S(1)}, f32[80,128]{1,0:T(8,128)S(1)}, u32[]{:S(2)}, u32[]{:S(2)}) collective-permute-start(f32[80,128]{1,0:T(8,128)S(1)} %get-tuple-element.17), channel_id=1, source_target_pairs={{0,8},{8,0},{16,24},{24,16},{1,9},{9,1},{17,25},{25,17},{2,10},{10... | collective-permute-start | bytes 122888 | tf_op jit(solution)/shard_map/ppermute | solution.py:465
  2.3 2.6 %collective-permute-start.1 = (f32[80,128]{1,0:T(8,128)S(1)}, f32[80,128]{1,0:T(8,128)S(1)}, u32[]{:S(2)}, u32[]{:S(2)}) collective-permute-start(f32[80,128]{1,0:T(8,128)S(1)} %get-tuple-element.18), channel_id=1, source_target_pairs={{0,16},{8,24},{16,0},{24,8},{1,17},{9,25},{17,1},{25,9},{2,18},{10... | collective-permute-start | bytes 122888 | tf_op jit(solution)/shard_map/ppermute | solution.py:465
  4.9 0.0 collective-permute-start.2
  4.9 0.7 %pad_add_fusion.table_ref.table_in_ref = s32[5,64]{1,0:T(8,128)S(1)} fusion(s32[1,64]{1,0:T(1,128)} %bitcast.55, s32[4,64]{1,0:T(4,128)} %bitcast.54), kind=kLoop, calls=%fused_computation.14 | loop fusion | flops 320 | bytes 2560 | tf_op jit(solution)/shard_map/concatenate | solution.py:460
  5.6 0.6 %stage.1 = (f32[64,128]{1,0:T(8,128)S(1)}, f32[2,8,128]{2,1,0:T(8,128)S(1)}) custom-call(s32[5,64]{1,0:T(8,128)S(1)} %pad_add_fusion.table_ref.table_in_ref), custom_call_target="tpu_custom_call" | custom-call | tf_op jit(solution)/shard_map/stage/pallas_call | solution.py:103
  6.3 0.0 collective-permute-done
  6.3 0.7 %collective-permute-done.1 = f32[80,128]{1,0:T(8,128)S(1)} collective-permute-done((f32[80,128]{1,0:T(8,128)S(1)}, f32[80,128]{1,0:T(8,128)S(1)}, u32[]{:S(2)}, u32[]{:S(2)}) %collective-permute-start.1) | collective-permute-done | bytes 40992 | tf_op jit(solution)/shard_map/ppermute | solution.py:465
  7.0 1.4 %collective-permute-done.2 = f32[80,128]{1,0:T(8,128)S(1)} collective-permute-done((f32[80,128]{1,0:T(8,128)S(1)}, f32[80,128]{1,0:T(8,128)S(1)}, u32[]{:S(2)}, u32[]{:S(2)}) %collective-permute-start.2) | collective-permute-done | bytes 40992 | tf_op jit(solution)/shard_map/ppermute | solution.py:465
  8.5 4.6 %collective-permute-start.4 = (f32[48,128]{1,0:T(8,128)S(1)}, f32[48,128]{1,0:T(8,128)S(1)}, u32[]{:S(2)}, u32[]{:S(2)}) collective-permute-start(f32[48,128]{1,0:T(8,128)S(1)} %pad_maximum_fusion.3), channel_id=1, source_target_pairs={{1,0},{2,1},{3,2},{4,3},{5,4},{6,5},{7,6},{0,7},{9,8},{10,9},{11,1... | collective-permute-start | bytes 73736 | tf_op jit(solution)/shard_map/ppermute | solution.py:488
  13.1 0.0 collective-permute-start.3
  13.1 3.4 %inner_early.1 = (f32[28,512,256]{2,1,0:T(8,128)S(1)}, f32[448,128]{1,0:T(8,128)S(1)}, bf16[64,128,128]{2,1,0:T(8,128)(2,1)S(1)}, bf16[28,256,256]{2,1,0:T(8,128)(2,1)S(1)}) custom-call(s32[5,64]{1,0:T(8,128)S(1)} %pad_add_fusion.table_ref.table_in_ref, f32[4,80,128]{2,1,0:T(8,128)S(1)} %pad_maximum_fusion.1.own_ref, f32[64,128]{1,0:T(8,128)S(1)} %get-tuple-element.20.live_ref), custom_call_target="tpu_custom_call" | custom-call | flops 1000000000 | bytes 10000000 | tf_op jit(solution)/shard_map/inner_early/pallas_call | solution.py:410
  16.5 3.2 %inner_late.1 = (f32[28,512,256]{2,1,0:T(8,128)S(1)}, f32[448,128]{1,0:T(8,128)S(1)}, bf16[64,128,128]{2,1,0:T(8,128)(2,1)S(1)}, bf16[28,256,256]{2,1,0:T(8,128)...) custom-call(s32[5,64]{1,0:T(8,128)S(1)} %pad_add_fusion.table_ref.ta, ...), custom_call_target="tpu_custom_call", output_to_operand_aliasing={{0}: (3, {}), {1}: (4, {}), {2}: (5, {}), {3}: (6, {})} | custom-call | flops 1000000000 | bytes 10000000 | tf_op jit(solution)/shard_map/inner_late/pallas_call | solution.py:410
  19.7 0.0 collective-permute-done.4.above_ref
  19.7 0.0 collective-permute-done.3.below_ref
  19.7 0.1 maximum_convert_fusion.rim_lists_in_ref
  19.8 2.8 %outer_step.1 = (f32[64,128]{1,0:T(8,128)}, f32[3,64,128]{2,1,0:T(8,128)}) custom-call(s32[5,64]{1,0:T(8,128)S(1)} %pad_add_fusion.table_ref.table_in_ref, s32[64]{0:T(128)S(1)} %maximum_convert_fusion.rim_lists_in_ref, f32[4,80,128]{2,1,0:T(8,128)S(1)} %pad_maximum_fusion.1.own_ref, f32[64,128]{1,0:T(8,128)S(1)} %get-tuple-element.20.live_ref, ...), custom_call_target="tpu_custom_call" | custom-call | tf_op jit(solution)/shard_map/outer_step/pallas_call | solution.py:427
  (14 shorter events, 0.1 us)
Async XLA Ops:
  1.7 4.6 %collective-permute-start = (f32[80,128]{1,0:T(8,128)S(1)}, f32[80,128]{1,0:T(8,128)S(1)}, u32[]{:S(2)}, u32[]{:S(2)}) collective-permute-start(f32[80,128]{1,0:T(8,128)S(1)} %get-tuple-element.17), channel_id=1, source_target_pairs={{0,8},{8,0},{16,24},{24,16},{1,9},{9,1},{17,25},{25,17},{2,10},{10... | collective-permute-start | bytes 122888 | tf_op jit(solution)/shard_map/ppermute | solution.py:465
  2.3 4.7 %collective-permute-start.1 = (f32[80,128]{1,0:T(8,128)S(1)}, f32[80,128]{1,0:T(8,128)S(1)}, u32[]{:S(2)}, u32[]{:S(2)}) collective-permute-start(f32[80,128]{1,0:T(8,128)S(1)} %get-tuple-element.18), channel_id=1, source_target_pairs={{0,16},{8,24},{16,0},{24,8},{1,17},{9,25},{17,1},{25,9},{2,18},{10... | collective-permute-start | bytes 122888 | tf_op jit(solution)/shard_map/ppermute | solution.py:465
  4.9 3.5 %collective-permute-start.2 = (f32[80,128]{1,0:T(8,128)S(1)}, f32[80,128]{1,0:T(8,128)S(1)}, u32[]{:S(2)}, u32[]{:S(2)}) collective-permute-start(f32[80,128]{1,0:T(8,128)S(1)} %get-tuple-element.19), channel_id=1, source_target_pairs={{0,24},{8,16},{16,8},{24,0},{1,25},{9,17},{17,9},{25,1},{2,26},{10... | collective-permute-start | bytes 122888 | tf_op jit(solution)/shard_map/ppermute | solution.py:465
  8.5 11.2 %collective-permute-start.4 = (f32[48,128]{1,0:T(8,128)S(1)}, f32[48,128]{1,0:T(8,128)S(1)}, u32[]{:S(2)}, u32[]{:S(2)}) collective-permute-start(f32[48,128]{1,0:T(8,128)S(1)} %pad_maximum_fusion.3), channel_id=1, source_target_pairs={{1,0},{2,1},{3,2},{4,3},{5,4},{6,5},{7,6},{0,7},{9,8},{10,9},{11,1... | collective-permute-start | bytes 73736 | tf_op jit(solution)/shard_map/ppermute | solution.py:488
  13.1 6.6 %collective-permute-start.3 = (f32[48,128]{1,0:T(8,128)S(1)}, f32[48,128]{1,0:T(8,128)S(1)}, u32[]{:S(2)}, u32[]{:S(2)}) collective-permute-start(f32[48,128]{1,0:T(8,128)S(1)} %pad_maximum_fusion.2), channel_id=1, source_target_pairs={{0,1},{1,2},{2,3},{3,4},{4,5},{5,6},{6,7},{7,0},{8,9},{9,10},{10,1... | collective-permute-start | bytes 73736 | tf_op jit(solution)/shard_map/ppermute | solution.py:486
